TPU v7x, 128 devices: a whole 4x4x4 slice. The times are simulated.
128 devices in a mesh: wide: 8 (over y, core), narrow: 16 (over z, x).
Axes of the slice: x: 4, y: 4, z: 4, core: 2. Of those that a mesh axis runs over, the one named last changes fastest.
Arguments:
- queries: bfloat16 [32768, 128], P(('wide', 'narrow')), may hold values from -6 to 6
- index_rows: bfloat16 [1048576, 128], P(('wide', 'narrow')), may hold values from -6 to 6
- lse_shift: float32 [32768], P('wide'), may hold values from 0 to 2.5
- loss_weight: float32 [32768], P('wide'), may hold values from 4 to 32
- positives: int32 [32768], P('wide'), may hold values from 0 to 131071
- tile_negs: int32 [256, 512], P('wide'), may hold values from 0 to 1023
- fetch_owner: int32 [8192, 1], P(('wide', 'narrow')), may hold values from 0 to 127; in each aligned block of 64 rows (0 to 63, 64 to 127, ...) at most 2 rows name the same one
- fetch_local: int32 [8192], P(('wide', 'narrow')), may hold values from 0 to 63
Outputs:
- query_grad: float32 [32768, 128], P(('wide', 'narrow'))
- index_grad: float32 [1048576, 128], P(('wide', 'narrow'))
Inputs may be any that keep to these rules, and one draw needn't show every extreme that they name: `fetch_owner`: among the 64 fetches of one device no owner is named more than 2 times, a bound that some block reaches.
All inputs are finite; a program needn't handle non-finite values.
Results may differ from a plain program's by a relative error of at most 0.0043.
Values may be sent and summed in bfloat16 or wider, within the bound.
No kernel may reach another device: no remote copies, remote signals or barrier semaphores. Data moves between devices by JAX's collectives and lax.ppermute only.
A program may use at most 128 MiB of HBM per device.

v0:
```python
import functools
import math

import jax
import jax.numpy as jnp
from jax import lax
from jax.experimental import pallas as pl
from jax.experimental.pallas import tpu as pltpu
from jax.sharding import Mesh
from jax.sharding import PartitionSpec as P


BLOCK = 128
QTILE = 128
CAP = 2
SAME_CORE = ("y", "z", "x")
NARROW = ("z", "x")
KEPT = 16
SLAB = 8
STEPS = (("x", 1), ("x", -1), ("y", 1), ("y", -1), ("z", 1), ("z", -1))
PLACES = 2 * CAP * (1 + len(STEPS))
FIELDS = 4
COUNT_AT = PLACES * FIELDS
DEAD = -1e30
UNROLL = 8
VMEM_LIMIT = 60 * 1024 * 1024


def tile_bits(flags):
    places = jnp.arange(flags.shape[0], dtype=jnp.int32)[:, None]
    return jnp.sum(jnp.left_shift(flags.astype(jnp.int32), places), axis=0)


def ask_kernel(sizes, where, owner, local, hits, lives, table):
    ring, narrow_count, blocks_here = sizes
    first_slot, core = where[0], where[1]

    def clear(d, carry):
        table[d, COUNT_AT] = 0
        return carry

    lax.fori_loop(0, table.shape[0], clear, 0)

    def ask(j, carry):
        own, block = owner[j], local[j]
        wide = own // narrow_count
        narrow = own % narrow_count
        turn = jnp.where(block < KEPT, -1, (block - KEPT) // SLAB)
        spot = {"y": wide // 2, "z": narrow // ring, "x": narrow % ring}
        for k, (axis, shift) in enumerate(STEPS):
            spot[axis] = spot[axis] + jnp.where(turn == k, shift + ring, 0)
        dest = ((spot["y"] % ring) * ring + spot["z"] % ring) * ring + spot["x"] % ring
        place = table[dest, COUNT_AT]
        table[dest, COUNT_AT] = place + 1
        at = place * FIELDS
        table[dest, at] = jnp.where(wide % 2 == core, 0, blocks_here) + block
        table[dest, at + 1] = first_slot + j
        table[dest, at + 2] = hits[j]
        table[dest, at + 3] = lives[j]
        return carry

    lax.fori_loop(0, owner.shape[0], ask, 0)


def turn_kernel(own, mate, blocks, turned):
    here = own.shape[0]

    def flip(i, carry):
        blocks[i] = own[i]
        blocks[i + here] = mate[i]
        turned[i] = own[i].T
        turned[i + here] = mate[i].T
        return carry

    lax.fori_loop(0, here, flip, 0)


def list_kernel(table, first_items, second_items, counts, live, base, hits):
    groups = 4
    sources = table.shape[0]
    in_group = sources // groups
    dead = jnp.int32(sources)
    lists = (first_items, second_items)

    def group_entries(group, cursor):
        def source_entries(n, count):
            src = group * in_group + n

            def place_entry(place, count):
                at = place * FIELDS
                base[count] = (table[src, at] << 7) | (table[src, at + 1] << 15)
                hits[count] = table[src, at + 2]
                live[count] = table[src, at + 3]
                return count + 1

            return lax.fori_loop(0, table[src, COUNT_AT], place_entry, count)

        entries = lax.fori_loop(0, in_group, source_entries, jnp.int32(0))

        def entry_items(e, cursor):
            start = base[e] + group * in_group
            alive = live[e]
            hit = hits[e]
            empty = base[e] + dead
            out = []
            for h, at in enumerate(cursor):
                for n in range(in_group):
                    bit = 2 * n + h
                    named = (hit << (25 - bit)) if bit <= 25 else (hit >> (bit - 25))
                    lists[h][at] = (start + n) | (named & (1 << 25))
                    at = at + ((alive >> bit) & 1)
                lists[h][at] = empty
                out.append(at + (at & 1))
            return tuple(out)

        return lax.fori_loop(0, entries, entry_items, cursor)

    ends = lax.fori_loop(0, groups, group_entries, (jnp.int32(0), jnp.int32(0)))
    for h in range(2):
        for i in range(4 * UNROLL):
            lists[h][ends[h] + i] = dead
        counts[h] = (ends[h] + 2 * UNROLL - 1) // (2 * UNROLL)


def chunk_kernel(h, first, last, items, counts, rows, q, blocks, turned, *rest):
    if first:
        (query_out, block_out, q_turned, query_acc, scores, grads) = rest
        block_acc = block_out
    else:
        (block_in, query_out, own_out, mate_out, q_turned, query_acc, scores, grads, block_acc, sem) = rest
        earlier = pltpu.make_async_copy(block_in, block_acc, sem)
        earlier.start()
    scale = 2.0 / math.sqrt(q.shape[2])
    factor = scale * math.log2(math.e)
    tiles = q.shape[0] - 1

    def turn(t, carry):
        q_turned[t] = q[t].T
        query_acc[t] = jnp.zeros((BLOCK, QTILE), jnp.float32)
        return carry

    lax.fori_loop(0, tiles + 1, turn, 0)
    scores[...] = jnp.zeros_like(scores)
    grads[...] = jnp.zeros_like(grads)
    if first:

        def clear(b, carry):
            block_acc[b] = jnp.zeros((BLOCK, QTILE), jnp.float32)
            return carry

        lax.fori_loop(0, block_acc.shape[0], clear, 0)
    else:
        earlier.wait()

    column = lax.broadcasted_iota(jnp.int32, (BLOCK, QTILE), 0)

    def tile_of(word):
        return word & 127

    def block_of(word):
        return (word >> 7) & 127

    def block_grads(words, grad):
        block = block_of(words[0])
        t1, t2 = tile_of(words[0]), tile_of(words[1])
        both = jnp.concatenate([q[t1], q[t2]], axis=0)
        to_block = jnp.dot(grad, both, preferred_element_type=jnp.float32)
        part = jnp.dot(turned[block], grad, preferred_element_type=jnp.float32)
        block_acc[block] += to_block
        sum1 = query_acc[t1] + part[:, :QTILE]
        sum2 = query_acc[t2] + part[:, QTILE:]
        query_acc[t1] = sum1
        query_acc[t2] = sum2

    def logit_grads(words, scores):
        slot = (words[0] >> 15) & 1023
        halves = []
        for side, word in enumerate(words):
            tile = tile_of(word)
            hit = (word >> 25) & 1
            shift = rows[tile, pl.ds(h, 1), :]
            loss = rows[tile, pl.ds(2 + h, 1), :]
            positive = rows[tile, pl.ds(4 + h, 1), :].astype(jnp.int32)
            mine = (positive >> 7) == slot
            shift = jnp.where(jnp.logical_or(mine, hit > 0), shift, DEAD)
            target = jnp.where(mine, positive & 127, -1)
            at = slice(side * QTILE, (side + 1) * QTILE)
            terms = jnp.exp2(scores[:, at] * factor + shift)
            terms = terms - jnp.where(column == target, loss, 0.0)
            halves.append(terms.astype(jnp.bfloat16))
        return jnp.concatenate(halves, axis=1)

    def next_scores(words):
        wide = jnp.concatenate([q_turned[tile_of(words[0])], q_turned[tile_of(words[1])]], axis=1)
        return jnp.dot(blocks[block_of(words[0])], wide, preferred_element_type=jnp.float32)

    def step(i, coming):
        starting = tuple((items[2 * (UNROLL * i + u)], items[2 * (UNROLL * i + u) + 1]) for u in range(UNROLL))
        for u in range(UNROLL):
            grad = logit_grads(coming[u], scores[u])
            block_grads(coming[u], grad)
            scores[u] = next_scores(starting[u])
        return starting

    dead = jnp.int32(tiles)
    lax.fori_loop(0, counts[h] + 1, step, ((dead, dead),) * UNROLL)

    def finish(t, carry):
        query_out[t] = (query_acc[t] * scale).T.astype(jnp.bfloat16)
        return carry

    lax.fori_loop(0, tiles, finish, 0)
    if last:
        half = own_out.shape[0]

        def deliver(b, carry):
            own_out[b] = block_acc[b] * scale
            mate_out[b] = (block_acc[b + half] * scale).astype(jnp.bfloat16)
            return carry

        lax.fori_loop(0, half, deliver, 0)


def shard_work(
    queries, index_rows, lse_shift, loss_weight, positives, tile_negs, fetch_owner, fetch_local
):
    narrow_count = lax.axis_size(NARROW)
    sources = lax.axis_size(SAME_CORE)
    core = lax.axis_index("c")
    narrow_pos = lax.axis_index(NARROW)
    feat_width = queries.shape[1]
    own_rows = queries.shape[0]
    blocks_here = index_rows.shape[0] // BLOCK
    stored = index_rows.reshape(blocks_here, BLOCK, feat_width)
    ring = lax.axis_size("x")
    ways = []
    for axis, shift in STEPS:
        size = lax.axis_size(axis)
        ways.append((axis, [(i, (i + shift) % size) for i in range(size)]))
    slabs = [slice(KEPT + SLAB * k, KEPT + SLAB * (k + 1)) for k in range(len(STEPS))]
    lent = [lax.ppermute(stored[at], axis, way) for at, (axis, way) in zip(slabs, ways)]
    held = jnp.concatenate([stored[:KEPT]] + lent)
    mate_held = lax.ppermute(held, "c", [(0, 1), (1, 0)])

    smem = pl.BlockSpec(memory_space=pltpu.SMEM)
    vmem = pl.BlockSpec(memory_space=pltpu.VMEM)
    limit = pltpu.CompilerParams(vmem_limit_bytes=VMEM_LIMIT)
    owners = fetch_owner[:, 0]
    fetch_count = owners.shape[0]
    first_slot = narrow_pos * fetch_count
    slot_ids = first_slot + jnp.arange(fetch_count, dtype=jnp.int32)
    tile_hit = jnp.any(tile_negs[:, :, None] == slot_ids[None, None, :], axis=1)
    tiles = tile_negs.shape[0]
    pos_slots = positives.reshape(tiles, QTILE) // BLOCK
    pos_hit = jnp.any(pos_slots[:, :, None] == slot_ids[None, None, :], axis=1)
    ask = pl.pallas_call(
        functools.partial(ask_kernel, (ring, narrow_count, blocks_here)),
        out_shape=jax.ShapeDtypeStruct((sources, QTILE), jnp.int32),
        in_specs=[smem] * 5,
        out_specs=smem,
        cost_estimate=pl.CostEstimate(flops=10**6, bytes_accessed=2**16, transcendentals=0),
        name="ask",
    )
    table = ask(
        jnp.stack([first_slot, core]),
        owners,
        fetch_local,
        tile_bits(tile_hit),
        tile_bits(jnp.logical_or(tile_hit, pos_hit)),
    )
    table = lax.all_to_all(table, SAME_CORE, 0, 0, tiled=True)

    first_row = narrow_pos * own_rows
    lse_own = lax.dynamic_slice_in_dim(lse_shift, first_row, own_rows, 0)
    loss_own = lax.dynamic_slice_in_dim(loss_weight, first_row, own_rows, 0)
    pos_own = lax.dynamic_slice_in_dim(positives, first_row, own_rows, 0)
    lse_full = lse_own + math.log(fetch_count * narrow_count * BLOCK)
    shift = jnp.log2(loss_own) - lse_full * math.log2(math.e)
    per_query = jnp.concatenate([shift, loss_own, pos_own.astype(jnp.float32), jnp.zeros_like(shift)])
    per_query = jnp.broadcast_to(per_query.reshape(8, QTILE)[None], (sources, 8, QTILE))
    rows = lax.all_to_all(per_query, SAME_CORE, 0, 0, tiled=True)
    rows = jnp.concatenate([rows, jnp.full((1, 8, QTILE), -1.0, jnp.float32)], axis=0)

    halves = []
    for h in range(2):
        part = queries[h * QTILE : (h + 1) * QTILE]
        spread = jnp.broadcast_to(part[None], (sources, QTILE, feat_width))
        part = lax.all_to_all(spread, SAME_CORE, 0, 0, tiled=True)
        halves.append(jnp.concatenate([part, jnp.zeros((1, QTILE, feat_width), part.dtype)]))

    held_shape = jax.ShapeDtypeStruct((2 * blocks_here, feat_width, BLOCK), jnp.bfloat16)
    turn = pl.pallas_call(
        turn_kernel,
        out_shape=(held_shape, held_shape),
        in_specs=[vmem, vmem],
        out_specs=(vmem, vmem),
        compiler_params=limit,
        cost_estimate=pl.CostEstimate(flops=10**9, bytes_accessed=2**24, transcendentals=0),
        name="turn",
    )
    blocks, turned = turn(held, mate_held)
    most = sources * PLACES * (tiles // 2) + 4 * UNROLL
    list_shape = jax.ShapeDtypeStruct((most,), jnp.int32)
    entries = sources // 4 * PLACES
    listing = pl.pallas_call(
        list_kernel,
        out_shape=(list_shape, list_shape, jax.ShapeDtypeStruct((2,), jnp.int32)),
        in_specs=[smem],
        out_specs=(smem, smem, smem),
        scratch_shapes=[pltpu.SMEM((entries,), jnp.int32)] * 3,
        cost_estimate=pl.CostEstimate(flops=10**9, bytes_accessed=2**20, transcendentals=0),
        name="listing",
    )
    *items, counts = listing(table)

    acc_shape = jax.ShapeDtypeStruct((2 * blocks_here, BLOCK, feat_width), jnp.float32)
    grad_shape = jax.ShapeDtypeStruct((sources, QTILE, feat_width), jnp.bfloat16)
    own_shape = jax.ShapeDtypeStruct((blocks_here, BLOCK, feat_width), jnp.float32)
    mate_shape = jax.ShapeDtypeStruct((blocks_here, BLOCK, feat_width), jnp.bfloat16)
    scratch = [
        pltpu.VMEM((sources + 1, feat_width, QTILE), jnp.bfloat16),
        pltpu.VMEM((sources + 1, feat_width, QTILE), jnp.float32),
        pltpu.VMEM((UNROLL, BLOCK, 2 * QTILE), jnp.float32),
        pltpu.VMEM((UNROLL, BLOCK, 2 * QTILE), jnp.bfloat16),
    ]
    cost = pl.CostEstimate(flops=2 * 10**10, bytes_accessed=2**25, transcendentals=10**7)
    chunk_0 = pl.pallas_call(
        functools.partial(chunk_kernel, 0, True, False),
        out_shape=(grad_shape, acc_shape),
        in_specs=[smem, smem, vmem, vmem, vmem, vmem],
        out_specs=(vmem, vmem),
        scratch_shapes=scratch,
        compiler_params=limit,
        cost_estimate=cost,
        name="chunk_0",
    )
    grad_0, acc = chunk_0(items[0], counts, rows, halves[0], blocks, turned)
    chunk_1 = pl.pallas_call(
        functools.partial(chunk_kernel, 1, False, True),
        out_shape=(grad_shape, own_shape, mate_shape),
        in_specs=[smem, smem, vmem, vmem, vmem, vmem, pl.BlockSpec(memory_space=pl.ANY)],
        out_specs=(vmem, vmem, vmem),
        scratch_shapes=scratch + [pltpu.VMEM(acc_shape.shape, jnp.float32), pltpu.SemaphoreType.DMA],
        compiler_params=limit,
        cost_estimate=cost,
        name="chunk_1",
    )
    grad_1, own_grad, mate_grad = chunk_1(items[1], counts, rows, halves[1], blocks, turned, acc)
    sums = []
    for part in (grad_0, grad_1):
        came = lax.all_to_all(part, SAME_CORE, 0, 0, tiled=True)
        sums.append(jnp.sum(came.astype(jnp.float32), axis=0))
    query_grad = jnp.concatenate(sums)
    from_mate = lax.ppermute(mate_grad, "c", [(0, 1), (1, 0)])
    held_grad = own_grad + from_mate.astype(jnp.float32)
    back = [
        lax.ppermute(held_grad[at].astype(jnp.bfloat16), axis, [(j, i) for i, j in way])
        for at, (axis, way) in zip(slabs, ways)
    ]
    index_grad = jnp.concatenate([held_grad[:KEPT]] + [part.astype(jnp.float32) for part in back])
    return (query_grad, index_grad.reshape(blocks_here * BLOCK, feat_width))


def solution(mesh):
    wide, narrow = mesh.devices.shape
    split = Mesh(mesh.devices.reshape(wide // 2, 2, 4, narrow // 4), ("y", "c", "z", "x"))
    every = ("y", "c", "z", "x")
    group = ("y", "c")
    in_specs = (
        P(every, None),
        P(every, None),
        P(group),
        P(group),
        P(group),
        P(group, None),
        P(every, None),
        P(every),
    )
    out_specs = (P(every, None), P(every, None))
    return jax.shard_map(shard_work, mesh=split, in_specs=in_specs, out_specs=out_specs, check_vma=False)
```

profile of v0, /device:TPU:0, one launch (start us, length us, event | category | flops | bytes accessed | tf_op | source)
XLA Modules:
  0.0 342.5 jit_solution(3627685389670557292)
XLA Ops:
  0.6 0.7 add_select_fusion
  1.4 1.5 compare_reduce_fusion
  4.8 5.6 %ask.1 = s32[64,128]{1,0:T(8,128)} custom-call(s32[2]{0:T(128)} %pad_add_fusion.where, s32[64]{0:T(128)} %bitcast.47, s32[64]{0:T(128)} %local.1, s32[64]{0:T(128)} %get-tuple-element.23.hits, s32[64]{0:T(128)} %get-tuple-element.22.lives), custom_call_target="tpu_custom_call" | custom-call | flops 1000000 | bytes 65536 | tf_op jit(solution)/shard_map/ask/pallas_call | solution.py:264
  10.4 11.5 %all-to-all-start = ((s32[64,1,128]{2,1,0:T(1,128)}), s32[64,1,128]{2,1,0:T(1,128)S(1)}, u32[]{:S(2)}, u32[]{:S(2)}) async-start(s32[64,1,128]{2,1,0:T(1,128)} %bitcast.45), calls=%async_computation | async-start | bytes 65536 | tf_op jit(solution)/shard_map/all_to_all | solution.py:271
  21.9 0.8 convert_bitcast_fusion
  22.7 0.8 subtract_bitcast_fusion
  23.6 7.8 %all-to-all-done = s32[64,1,128]{2,1,0:T(1,128)S(1)} async-done(((s32[64,1,128]{2,1,0:T(1,128)}), s32[64,1,128]{2,1,0:T(1,128)S(1)}, u32[]{:S(2)}, u32[]{:S(2)}) %all-to-all-start) | async-done | bytes 32800 | tf_op jit(solution)/shard_map/all_to_all | solution.py:271
  31.4 0.7 broadcast_in_dim.9
  32.1 5.0 %all-to-all-start.1 = ((f32[64,8,128]{2,1,0:T(8,128)}), f32[64,8,128]{2,1,0:T(8,128)S(1)}, u32[]{:S(2)}, u32[]{:S(2)}) async-start(f32[64,8,128]{2,1,0:T(8,128)} %broadcast_in_dim.9), calls=%async_computation.1 | async-start | bytes 524288 | tf_op jit(solution)/shard_map/all_to_all | solution.py:281
  37.1 0.8 fusion.6
  37.9 9.8 %all-to-all-done.1 = f32[64,8,128]{2,1,0:T(8,128)S(1)} async-done(((f32[64,8,128]{2,1,0:T(8,128)}), f32[64,8,128]{2,1,0:T(8,128)S(1)}, u32[]{:S(2)}, u32[]{:S(2)}) %all-to-all-start.1) | async-done | bytes 262176 | tf_op jit(solution)/shard_map/all_to_all | solution.py:281
  47.7 1.8 broadcast_in_dim.10
  49.5 4.9 %all-to-all-start.2 = ((bf16[64,128,128]{2,1,0:T(8,128)(2,1)}), bf16[64,128,128]{2,1,0:T(8,128)(2,1)S(1)}, u32[]{:S(2)}, u32[]{:S(2)}) async-start(bf16[64,128,128]{2,1,0:T(8,128)(2,1)} %broadcast_in_dim.10), calls=%async_computation.2 | async-start | bytes 4194304 | tf_op jit(solution)/shard_map/all_to_all | solution.py:288
  54.4 1.5 fusion.5
  55.9 1.6 collective-permute-start
  57.6 1.7 collective-permute-start.1
  59.2 3.0 collective-permute-start.3
  62.2 2.8 collective-permute-start.5
  65.0 0.8 constant_dynamic-update-slice_fusion.6
  65.8 16.8 %collective-permute-done = bf16[8,128,128]{2,1,0:T(8,128)(2,1)S(1)} collective-permute-done((bf16[8,128,128]{2,1,0:T(8,128)(2,1)S(1)}, bf16[8,128,128]{2,1,0:T(8,128)(2,1)S(1)}, u32[]{:S(2)}, u32[]{:S(2)}) %collective-permute-start) | collective-permute-done | bytes 262176 | tf_op jit(solution)/shard_map/ppermute | solution.py:241
  82.7 1.5 collective-permute-start.4
  84.1 0.7 constant_dynamic-update-slice_fusion.5
  85.6 0.7 constant_dynamic-update-slice_fusion.3
  86.3 0.7 constant_dynamic-update-slice_fusion.2
  87.1 3.3 collective-permute-done.4
  90.4 0.7 constant_dynamic-update-slice_fusion.1
  91.1 0.7 constant_dynamic-update-slice_fusion.own
  91.8 1.8 broadcast_in_dim.11
  93.7 7.1 %all-to-all-start.4 = ((bf16[64,128,128]{2,1,0:T(8,128)(2,1)}), bf16[64,128,128]{2,1,0:T(8,128)(2,1)}, u32[]{:S(2)}, u32[]{:S(2)}) async-start(bf16[64,128,128]{2,1,0:T(8,128)(2,1)} %broadcast_in_dim.11), calls=%async_computation.4 | async-start | bytes 4194304 | tf_op jit(solution)/shard_map/all_to_all | solution.py:288
  100.7 12.8 %listing.1 = (s32[28704]{0:T(1024)}, s32[28704]{0:T(1024)}, s32[2]{0:T(128)}) custom-call(s32[64,128]{1,0:T(8,128)} %bitcast.46), custom_call_target="tpu_custom_call" | custom-call | flops 1000000000 | bytes 1048576 | tf_op jit(solution)/shard_map/listing/pallas_call | solution.py:314
  113.6 0.7 concatenate.32.rows
  114.3 1.5 concatenate.33.q
  115.8 16.2 %all-to-all-done.4 = bf16[64,128,128]{2,1,0:T(8,128)(2,1)} async-done(((bf16[64,128,128]{2,1,0:T(8,128)(2,1)}), bf16[64,128,128]{2,1,0:T(8,128)(2,1)}, u32[]{:S(2)}, u32[]{:S(2)}) %all-to-all-start.4) | async-done | bytes 2097184 | tf_op jit(solution)/shard_map/all_to_all | solution.py:288
  132.1 3.2 concatenate.35.q
  135.3 10.5 %turn.1 = (bf16[128,128,128]{2,1,0:T(8,128)(2,1)}, bf16[128,128,128]{2,1,0:T(8,128)(2,1)}) custom-call(bf16[64,128,128]{2,1,0:T(8,128)(2,1)} %constant_dynamic-update-slice_fusion.own, bf16[64,128,128]{2,1,0:T(8,128)(2,1)} %collective-permute-done.6.mate), custom_call_target="tpu_custom_call" | custom-call | flops 1000000000 | bytes 16777216 | tf_op jit(solution)/shard_map/turn/pallas_call | solution.py:301
  145.7 40.0 %chunk_0.1 = (bf16[64,128,128]{2,1,0:T(8,128)(2,1)}, f32[128,128,128]{2,1,0:T(8,128)}) custom-call(s32[28704]{0:T(1024)} %get-tuple-element.12.items, s32[2]{0:T(128)} %get-tuple-element.13.counts, f32[65,8,128]{2,1,0:T(8,128)} %concatenate.32.rows, bf16[65,128,128]{2,1,0:T(8,128)(2,1)} %concatenate.33.q, bf16[128,128,128]{2,1,0:T(8,128)(2,1)} %get-tuple-element.14.blocks, ...), custom_call_target="tpu_custom_call" | custom-call | flops 20000000000 | bytes 33554432 | tf_op jit(solution)/shard_map/chunk_0/pallas_call | solution.py:337
  185.7 40.7 %chunk_1.1 = (bf16[64,128,128]{2,1,0:T(8,128)(2,1)}, f32[64,128,128]{2,1,0:T(8,128)}, bf16[64,128,128]{2,1,0:T(8,128)(2,1)}) custom-call(s32[28704]{0:T(1024)} %get-tuple-element.17.items, s32[2]{0:T(128)} %get-tuple-element.13.counts, f32[65,8,128]{2,1,0:T(8,128)} %concatenate.32.rows, bf16[65,128,128]{2,1,0:T(8,128)(2,1)} %concatenate.35.q, ...), custom_call_target="tpu_custom_call" | custom-call | flops 20000000000 | bytes 33554432 | tf_op jit(solution)/shard_map/chunk_1/pallas_call | solution.py:348
  226.4 57.3 %all_to_all.36 = bf16[64,128,128]{2,1,0:T(8,128)(2,1)} all-to-all(bf16[64,128,128]{2,1,0:T(8,128)(2,1)} %get-tuple-element.19), channel_id=1, replica_groups=mesh['y'=4,'c'=2,'z'=4,'x'=4] {'y','z','x'}, dimensions={0} | all-to-all | bytes 4194304 | tf_op jit(solution)/shard_map/all_to_all | solution.py:351
  283.7 4.9 %all-to-all-start.3 = ((bf16[64,128,128]{2,1,0:T(8,128)(2,1)}), bf16[64,128,128]{2,1,0:T(8,128)(2,1)S(1)}, u32[]{:S(2)}, u32[]{:S(2)}) async-start(bf16[64,128,128]{2,1,0:T(8,128)(2,1)} %get-tuple-element.16), calls=%async_computation.3 | async-start | bytes 4194304 | tf_op jit(solution)/shard_map/all_to_all | solution.py:351
  288.6 1.9 convert_reduce_fusion
  290.5 27.3 %all-to-all-done.3 = bf16[64,128,128]{2,1,0:T(8,128)(2,1)S(1)} async-done(((bf16[64,128,128]{2,1,0:T(8,128)(2,1)}), bf16[64,128,128]{2,1,0:T(8,128)(2,1)S(1)}, u32[]{:S(2)}, u32[]{:S(2)}) %all-to-all-start.3) | async-done | bytes 2097184 | tf_op jit(solution)/shard_map/all_to_all | solution.py:351
  318.8 3.7 %fusion.3 = (bf16[64,128,128]{2,1,0:T(8,128)(2,1)S(1)}, f32[64,128,128]{2,1,0:T(8,128)S(1)}) fusion(f32[64,128,128]{2,1,0:T(8,128)} %get-tuple-element.20, bf16[64,128,128]{2,1,0:T(8,128)(2,1)} %collective-permute-done.7), kind=kLoop, calls=%fused_computation.37 | loop fusion | flops 3145728 | bytes 12582912 | tf_op jit(solution)/shard_map/convert.5
  323.4 2.6 collective-permute-start.12
  326.4 3.1 collective-permute-start.8
  329.6 3.8 %collective-permute-done.8 = bf16[8,128,128]{2,1,0:T(8,128)(2,1)S(1)} collective-permute-done((bf16[8,128,128]{2,1,0:T(8,128)(2,1)S(1)}, bf16[8,128,128]{2,1,0:T(8,128)(2,1)S(1)}, u32[]{:S(2)}, u32[]{:S(2)}) %collective-permute-start.8) | collective-permute-done | bytes 262176 | tf_op jit(solution)/shard_map/ppermute | solution.py:357
  333.4 3.0 collective-permute-start.10
  336.5 3.8 %collective-permute-done.10 = bf16[8,128,128]{2,1,0:T(8,128)(2,1)S(1)} collective-permute-done((bf16[8,128,128]{2,1,0:T(8,128)(2,1)S(1)}, bf16[8,128,128]{2,1,0:T(8,128)(2,1)S(1)}, u32[]{:S(2)}, u32[]{:S(2)}) %collective-permute-start.10) | collective-permute-done | bytes 262176 | tf_op jit(solution)/shard_map/ppermute | solution.py:357
  340.5 2.0 copy-done
  (40 shorter events, 5.3 us)
Async XLA Ops:
  10.4 21.0 %all-to-all-start = ((s32[64,1,128]{2,1,0:T(1,128)}), s32[64,1,128]{2,1,0:T(1,128)S(1)}, u32[]{:S(2)}, u32[]{:S(2)}) async-start(s32[64,1,128]{2,1,0:T(1,128)} %bitcast.45), calls=%async_computation | async-start | bytes 65536 | tf_op jit(solution)/shard_map/all_to_all | solution.py:271
  31.4 18.1 %copy-start.1 = (s32[64,1,128]{2,1,0:T(1,128)}, s32[64,1,128]{2,1,0:T(1,128)S(1)}, u32[]{:S(2)}) copy-start(s32[64,1,128]{2,1,0:T(1,128)S(1)} %all-to-all-done) | copy-start | bytes 98308
  32.1 15.6 %all-to-all-start.1 = ((f32[64,8,128]{2,1,0:T(8,128)}), f32[64,8,128]{2,1,0:T(8,128)S(1)}, u32[]{:S(2)}, u32[]{:S(2)}) async-start(f32[64,8,128]{2,1,0:T(8,128)} %broadcast_in_dim.9), calls=%async_computation.1 | async-start | bytes 524288 | tf_op jit(solution)/shard_map/all_to_all | solution.py:281
  49.5 42.3 %all-to-all-start.2 = ((bf16[64,128,128]{2,1,0:T(8,128)(2,1)}), bf16[64,128,128]{2,1,0:T(8,128)(2,1)S(1)}, u32[]{:S(2)}, u32[]{:S(2)}) async-start(bf16[64,128,128]{2,1,0:T(8,128)(2,1)} %broadcast_in_dim.10), calls=%async_computation.2 | async-start | bytes 4194304 | tf_op jit(solution)/shard_map/all_to_all | solution.py:288
  54.4 10.6 %slice-start = ((bf16[8192,128]{1,0:T(8,128)(2,1)}), bf16[2048,128]{1,0:T(8,128)(2,1)S(1)}, s32[]{:S(2)}) async-start(bf16[8192,128]{1,0:T(8,128)(2,1)} %param.9), calls=%async_computation.6 | async-start | bytes 1048576 | tf_op jit(solution)/shard_map/slice | solution.py:242
  55.9 26.8 %collective-permute-start = (bf16[8,128,128]{2,1,0:T(8,128)(2,1)S(1)}, bf16[8,128,128]{2,1,0:T(8,128)(2,1)S(1)}, u32[]{:S(2)}, u32[]{:S(2)}) collective-permute-start(bf16[8,128,128]{2,1,0:T(8,128)(2,1)S(1)} %bitcast.43), channel_id=1, source_target_pairs={{0,1},{1,2},{2,3},{3,0},{4,5},{5,6},{6,7},{7,4},{8,9},{9,10},{10,1... | collective-permute-start | bytes 786440 | tf_op jit(solution)/shard_map/ppermute | solution.py:241
  57.6 27.3 %collective-permute-start.1 = (bf16[8,128,128]{2,1,0:T(8,128)(2,1)S(1)}, bf16[8,128,128]{2,1,0:T(8,128)(2,1)S(1)}, u32[]{:S(2)}, u32[]{:S(2)}) collective-permute-start(bf16[8,128,128]{2,1,0:T(8,128)(2,1)S(1)} %bitcast.42), channel_id=1, source_target_pairs={{0,3},{1,0},{2,1},{3,2},{4,7},{5,4},{6,5},{7,6},{8,11},{9,8},{10,9... | collective-permute-start | bytes 786440 | tf_op jit(solution)/shard_map/ppermute | solution.py:241
  59.2 27.1 %collective-permute-start.3 = (bf16[8,128,128]{2,1,0:T(8,128)(2,1)S(1)}, bf16[8,128,128]{2,1,0:T(8,128)(2,1)S(1)}, u32[]{:S(2)}, u32[]{:S(2)}) collective-permute-start(bf16[8,128,128]{2,1,0:T(8,128)(2,1)S(1)} %bitcast.40), channel_id=1, source_target_pairs={{0,96},{32,0},{64,32},{96,64},{1,97},{33,1},{65,33},{97,65},{2,98}... | collective-permute-start | bytes 786440 | tf_op jit(solution)/shard_map/ppermute | solution.py:241
  62.2 28.9 %collective-permute-start.5 = (bf16[8,128,128]{2,1,0:T(8,128)(2,1)S(1)}, bf16[8,128,128]{2,1,0:T(8,128)(2,1)S(1)}, u32[]{:S(2)}, u32[]{:S(2)}) collective-permute-start(bf16[8,128,128]{2,1,0:T(8,128)(2,1)S(1)} %bitcast.38), channel_id=1, source_target_pairs={{0,12},{4,0},{8,4},{12,8},{1,13},{5,1},{9,5},{13,9},{2,14},{6,2},{... | collective-permute-start | bytes 786440 | tf_op jit(solution)/shard_map/ppermute | solution.py:241
  65.0 20.6 %collective-permute-start.2 = (bf16[8,128,128]{2,1,0:T(8,128)(2,1)S(1)}, bf16[8,128,128]{2,1,0:T(8,128)(2,1)S(1)}, u32[]{:S(2)}, u32[]{:S(2)}) collective-permute-start(bf16[8,128,128]{2,1,0:T(8,128)(2,1)S(1)} %bitcast.41), channel_id=1, source_target_pairs={{0,32},{32,64},{64,96},{96,0},{1,33},{33,65},{65,97},{97,1},{2,34}... | collective-permute-start | bytes 786440 | tf_op jit(solution)/shard_map/ppermute | solution.py:241
  82.7 7.7 %collective-permute-start.4 = (bf16[8,128,128]{2,1,0:T(8,128)(2,1)S(1)}, bf16[8,128,128]{2,1,0:T(8,128)(2,1)S(1)}, u32[]{:S(2)}, u32[]{:S(2)}) collective-permute-start(bf16[8,128,128]{2,1,0:T(8,128)(2,1)S(1)} %bitcast.39), channel_id=1, source_target_pairs={{0,4},{4,8},{8,12},{12,0},{1,5},{5,9},{9,13},{13,1},{2,6},{6,10},{... | collective-permute-start | bytes 786440 | tf_op jit(solution)/shard_map/ppermute | solution.py:241
  91.8 43.4 %collective-permute-start.6 = (bf16[64,128,128]{2,1,0:T(8,128)(2,1)}, bf16[64,128,128]{2,1,0:T(8,128)(2,1)}, u32[]{:S(2)}, u32[]{:S(2)}) collective-permute-start(bf16[64,128,128]{2,1,0:T(8,128)(2,1)} %constant_dynamic-update-slice_fusion.own), channel_id=1, source_target_pairs={{0,16},{16,0},{1,17},{17,1},{2,18},{18,2},{3,19},{19,3},{4,20},{20... | collective-permute-start | bytes 6291464 | tf_op jit(solution)/shard_map/ppermute | solution.py:243
  93.7 38.4 %all-to-all-start.4 = ((bf16[64,128,128]{2,1,0:T(8,128)(2,1)}), bf16[64,128,128]{2,1,0:T(8,128)(2,1)}, u32[]{:S(2)}, u32[]{:S(2)}) async-start(bf16[64,128,128]{2,1,0:T(8,128)(2,1)} %broadcast_in_dim.11), calls=%async_computation.4 | async-start | bytes 4194304 | tf_op jit(solution)/shard_map/all_to_all | solution.py:288
  283.7 34.2 %all-to-all-start.3 = ((bf16[64,128,128]{2,1,0:T(8,128)(2,1)}), bf16[64,128,128]{2,1,0:T(8,128)(2,1)S(1)}, u32[]{:S(2)}, u32[]{:S(2)}) async-start(bf16[64,128,128]{2,1,0:T(8,128)(2,1)} %get-tuple-element.16), calls=%async_computation.3 | async-start | bytes 4194304 | tf_op jit(solution)/shard_map/all_to_all | solution.py:351
  288.5 30.3 %collective-permute-start.7 = (bf16[64,128,128]{2,1,0:T(8,128)(2,1)}, bf16[64,128,128]{2,1,0:T(8,128)(2,1)}, u32[]{:S(2)}, u32[]{:S(2)}) collective-permute-start(bf16[64,128,128]{2,1,0:T(8,128)(2,1)} %get-tuple-element.21), channel_id=1, source_target_pairs={{0,16},{16,0},{1,17},{17,1},{2,18},{18,2},{3,19},{19,3},{4,20},{20... | collective-permute-start | bytes 6291464 | tf_op jit(solution)/shard_map/ppermute | solution.py:354
  322.7 17.7 %collective-permute-start.13 = (bf16[8,128,128]{2,1,0:T(8,128)(2,1)S(1)}, bf16[8,128,128]{2,1,0:T(8,128)(2,1)S(1)}, u32[]{:S(2)}, u32[]{:S(2)}) collective-permute-start(bf16[8,128,128]{2,1,0:T(8,128)(2,1)S(1)} %get-tuple-element.26), channel_id=1, source_target_pairs={{12,0},{0,4},{4,8},{8,12},{13,1},{1,5},{5,9},{9,13},{14,2},{2,6},{... | collective-permute-start | bytes 786440 | tf_op jit(solution)/shard_map/ppermute | solution.py:357
  323.4 17.0 %collective-permute-start.12 = (bf16[8,128,128]{2,1,0:T(8,128)(2,1)S(1)}, bf16[8,128,128]{2,1,0:T(8,128)(2,1)S(1)}, u32[]{:S(2)}, u32[]{:S(2)}) collective-permute-start(bf16[8,128,128]{2,1,0:T(8,128)(2,1)S(1)} %get-tuple-element.27), channel_id=1, source_target_pairs={{4,0},{8,4},{12,8},{0,12},{5,1},{9,5},{13,9},{1,13},{6,2},{10,6},{... | collective-permute-start | bytes 786440 | tf_op jit(solution)/shard_map/ppermute | solution.py:357
  326.0 14.3 %collective-permute-start.11 = (bf16[8,128,128]{2,1,0:T(8,128)(2,1)S(1)}, bf16[8,128,128]{2,1,0:T(8,128)(2,1)S(1)}, u32[]{:S(2)}, u32[]{:S(2)}) collective-permute-start(bf16[8,128,128]{2,1,0:T(8,128)(2,1)S(1)} %get-tuple-element.28), channel_id=1, source_target_pairs={{96,0},{0,32},{32,64},{64,96},{97,1},{1,33},{33,65},{65,97},{98,2}... | collective-permute-start | bytes 786440 | tf_op jit(solution)/shard_map/ppermute | solution.py:357
  326.3 10.2 %collective-permute-start.9 = (bf16[8,128,128]{2,1,0:T(8,128)(2,1)S(1)}, bf16[8,128,128]{2,1,0:T(8,128)(2,1)S(1)}, u32[]{:S(2)}, u32[]{:S(2)}) collective-permute-start(bf16[8,128,128]{2,1,0:T(8,128)(2,1)S(1)} %get-tuple-element.30), channel_id=1, source_target_pairs={{3,0},{0,1},{1,2},{2,3},{7,4},{4,5},{5,6},{6,7},{11,8},{8,9},{9,10... | collective-permute-start | bytes 786440 | tf_op jit(solution)/shard_map/ppermute | solution.py:357
  326.4 7.0 %collective-permute-start.8 = (bf16[8,128,128]{2,1,0:T(8,128)(2,1)S(1)}, bf16[8,128,128]{2,1,0:T(8,128)(2,1)S(1)}, u32[]{:S(2)}, u32[]{:S(2)}) collective-permute-start(bf16[8,128,128]{2,1,0:T(8,128)(2,1)S(1)} %get-tuple-element.31), channel_id=1, source_target_pairs={{1,0},{2,1},{3,2},{0,3},{5,4},{6,5},{7,6},{4,7},{9,8},{10,9},{11,1... | collective-permute-start | bytes 786440 | tf_op jit(solution)/shard_map/ppermute | solution.py:357
  333.4 6.9 %collective-permute-start.10 = (bf16[8,128,128]{2,1,0:T(8,128)(2,1)S(1)}, bf16[8,128,128]{2,1,0:T(8,128)(2,1)S(1)}, u32[]{:S(2)}, u32[]{:S(2)}) collective-permute-start(bf16[8,128,128]{2,1,0:T(8,128)(2,1)S(1)} %get-tuple-element.29), channel_id=1, source_target_pairs={{32,0},{64,32},{96,64},{0,96},{33,1},{65,33},{97,65},{1,97},{34,2}... | collective-permute-start | bytes 786440 | tf_op jit(solution)/shard_map/ppermute | solution.py:357
  340.5 2.0 copy-start
where the time goes:
time: 345 us; the launch traced here: 343 us
  Pallas kernels  110 us (32%)
  waiting for transfers between devices  89 us (26%)
  blocking collectives  57.3 us (17%)
  starting transfers between devices  53.7 us (16%)
  local copies, waits for them, and re-layouts  19.7 us (6%)
  other arithmetic  12.5 us (4%)
    all_to_all x1, blocking collectives, shard_work(): came = lax.all_to_all(part, SAME_CORE, 0, 0, tiled=True)  57.3 us
    pallas_call x1, Pallas kernels, shard_work(): chunk_1(items[1], counts, rows, halves[1], blocks, turned, acc)  40.7 us
    pallas_call x1, Pallas kernels, shard_work(): grad_0, acc = chunk_0(items[0], counts, rows, halves[0], blocks, turned)  40 us
    all_to_all x1, waiting for transfers between devices, shard_work(): came = lax.all_to_all(part, SAME_CORE, 0, 0, tiled=True)  27.3 us
    ppermute x6, waiting for transfers between devices, shard_work(): lax.ppermute(stored[at], axis, way)  20.2 us
    all_to_all x2, waiting for transfers between devices, shard_work(): part = lax.all_to_all(spread, SAME_CORE, 0, 0, tiled=True)  16.2 us
    pallas_call x1, Pallas kernels, shard_work(): *items, counts = listing(table)  12.8 us
    all_to_all x2, starting transfers between devices, shard_work(): part = lax.all_to_all(spread, SAME_CORE, 0, 0, tiled=True)  11.9 us
  transfers between devices with their start and end apart: 19, of which 8 were waited for; matrix products, arithmetic and copies ran while one was open for 6% of the time, Pallas kernels for 4%

commit v1 on v0

--- a/solution.py
+++ b/solution.py
@@ -19,7 +19,7 @@
 SLAB = 8
 STEPS = (("x", 1), ("x", -1), ("y", 1), ("y", -1), ("z", 1), ("z", -1))
 PLACES = 2 * CAP * (1 + len(STEPS))
-FIELDS = 4
+FIELDS = 6
 COUNT_AT = PLACES * FIELDS
 DEAD = -1e30
 UNROLL = 8
@@ -55,24 +55,13 @@
         at = place * FIELDS
         table[dest, at] = jnp.where(wide % 2 == core, 0, blocks_here) + block
         table[dest, at + 1] = first_slot + j
-        table[dest, at + 2] = hits[j]
-        table[dest, at + 3] = lives[j]
+        table[dest, at + 2] = hits[j] & 0xFFFF
+        table[dest, at + 3] = (hits[j] >> 16) & 0xFFFF
+        table[dest, at + 4] = lives[j] & 0xFFFF
+        table[dest, at + 5] = (lives[j] >> 16) & 0xFFFF
         return carry
 
     lax.fori_loop(0, owner.shape[0], ask, 0)
-
-
-def turn_kernel(own, mate, blocks, turned):
-    here = own.shape[0]
-
-    def flip(i, carry):
-        blocks[i] = own[i]
-        blocks[i + here] = mate[i]
-        turned[i] = own[i].T
-        turned[i + here] = mate[i].T
-        return carry
-
-    lax.fori_loop(0, here, flip, 0)
 
 
 def list_kernel(table, first_items, second_items, counts, live, base, hits):
@@ -89,8 +78,8 @@
             def place_entry(place, count):
                 at = place * FIELDS
                 base[count] = (table[src, at] << 7) | (table[src, at + 1] << 15)
-                hits[count] = table[src, at + 2]
-                live[count] = table[src, at + 3]
+                hits[count] = table[src, at + 2] | (table[src, at + 3] << 16)
+                live[count] = table[src, at + 4] | (table[src, at + 5] << 16)
                 return count + 1
 
             return lax.fori_loop(0, table[src, COUNT_AT], place_entry, count)
@@ -122,35 +111,46 @@
         counts[h] = (ends[h] + 2 * UNROLL - 1) // (2 * UNROLL)
 
 
-def chunk_kernel(h, first, last, items, counts, rows, q, blocks, turned, *rest):
-    if first:
-        (query_out, block_out, q_turned, query_acc, scores, grads) = rest
-        block_acc = block_out
+def chunk_kernel(h, last, items, counts, rows_in, q_in, own_in, mate_in, *rest):
+    if last:
+        earlier_in, query_out, own_out, mate_out, block_acc, earlier = rest[:6]
     else:
-        (block_in, query_out, own_out, mate_out, q_turned, query_acc, scores, grads, block_acc, sem) = rest
-        earlier = pltpu.make_async_copy(block_in, block_acc, sem)
-        earlier.start()
+        query_out, block_acc = rest[:2]
+    rows, q, blocks, query_acc, scores, sems = rest[-6:]
     scale = 2.0 / math.sqrt(q.shape[2])
     factor = scale * math.log2(math.e)
-    tiles = q.shape[0] - 1
-
-    def turn(t, carry):
-        q_turned[t] = q[t].T
-        query_acc[t] = jnp.zeros((BLOCK, QTILE), jnp.float32)
-        return carry
-
-    lax.fori_loop(0, tiles + 1, turn, 0)
+    tiles = q_in.shape[0]
+    here = own_in.shape[0]
+    loads = [
+        pltpu.make_async_copy(q_in, q.at[pl.ds(0, tiles)], sems.at[0]),
+        pltpu.make_async_copy(own_in, blocks.at[pl.ds(0, here)], sems.at[1]),
+        pltpu.make_async_copy(mate_in, blocks.at[pl.ds(here, here)], sems.at[2]),
+        pltpu.make_async_copy(rows_in, rows.at[pl.ds(0, tiles)], sems.at[3]),
+    ]
+    if last:
+        summed = pltpu.make_async_copy(earlier_in, earlier, sems.at[4])
+    for load in loads:
+        load.start()
+    if last:
+        summed.start()
+    zero = jnp.zeros((BLOCK, QTILE), jnp.float32)
+    q[tiles] = zero.astype(q.dtype)
+    rows[tiles] = jnp.full(rows.shape[1:], -1.0, jnp.float32)
+    query_acc[tiles] = zero
+
+    def clear_query(t, carry):
+        query_acc[t] = zero
+        return carry
+
+    def clear_block(b, carry):
+        block_acc[b] = zero
+        return carry
+
+    lax.fori_loop(0, tiles, clear_query, 0, unroll=4)
+    lax.fori_loop(0, 2 * here, clear_block, 0, unroll=4)
     scores[...] = jnp.zeros_like(scores)
-    grads[...] = jnp.zeros_like(grads)
-    if first:
-
-        def clear(b, carry):
-            block_acc[b] = jnp.zeros((BLOCK, QTILE), jnp.float32)
-            return carry
-
-        lax.fori_loop(0, block_acc.shape[0], clear, 0)
-    else:
-        earlier.wait()
+    for load in loads:
+        load.wait()
 
     column = lax.broadcasted_iota(jnp.int32, (BLOCK, QTILE), 0)
 
@@ -165,7 +165,9 @@
         t1, t2 = tile_of(words[0]), tile_of(words[1])
         both = jnp.concatenate([q[t1], q[t2]], axis=0)
         to_block = jnp.dot(grad, both, preferred_element_type=jnp.float32)
-        part = jnp.dot(turned[block], grad, preferred_element_type=jnp.float32)
+        part = lax.dot_general(
+            blocks[block], grad, (((0,), (0,)), ((), ())), preferred_element_type=jnp.float32
+        )
         block_acc[block] += to_block
         sum1 = query_acc[t1] + part[:, :QTILE]
         sum2 = query_acc[t2] + part[:, QTILE:]
@@ -191,8 +193,10 @@
         return jnp.concatenate(halves, axis=1)
 
     def next_scores(words):
-        wide = jnp.concatenate([q_turned[tile_of(words[0])], q_turned[tile_of(words[1])]], axis=1)
-        return jnp.dot(blocks[block_of(words[0])], wide, preferred_element_type=jnp.float32)
+        both = jnp.concatenate([q[tile_of(words[0])], q[tile_of(words[1])]], axis=0)
+        return lax.dot_general(
+            blocks[block_of(words[0])], both, (((1,), (1,)), ((), ())), preferred_element_type=jnp.float32
+        )
 
     def step(i, coming):
         starting = tuple((items[2 * (UNROLL * i + u)], items[2 * (UNROLL * i + u) + 1]) for u in range(UNROLL))
@@ -209,16 +213,16 @@
         query_out[t] = (query_acc[t] * scale).T.astype(jnp.bfloat16)
         return carry
 
-    lax.fori_loop(0, tiles, finish, 0)
+    lax.fori_loop(0, tiles, finish, 0, unroll=4)
     if last:
-        half = own_out.shape[0]
+        summed.wait()
 
         def deliver(b, carry):
-            own_out[b] = block_acc[b] * scale
-            mate_out[b] = (block_acc[b + half] * scale).astype(jnp.bfloat16)
+            own_out[b] = (block_acc[b] + earlier[b]) * scale
+            mate_out[b] = ((block_acc[b + here] + earlier[b + here]) * scale).astype(jnp.bfloat16)
             return carry
 
-        lax.fori_loop(0, half, deliver, 0)
+        lax.fori_loop(0, here, deliver, 0, unroll=2)
 
 
 def shard_work(
@@ -232,6 +236,11 @@
     own_rows = queries.shape[0]
     blocks_here = index_rows.shape[0] // BLOCK
     stored = index_rows.reshape(blocks_here, BLOCK, feat_width)
+    halves = []
+    for h in range(2):
+        part = queries[h * QTILE : (h + 1) * QTILE]
+        spread = jnp.broadcast_to(part[None], (sources, QTILE, feat_width))
+        halves.append(lax.all_to_all(spread, SAME_CORE, 0, 0, tiled=True))
     ring = lax.axis_size("x")
     ways = []
     for axis, shift in STEPS:
@@ -255,7 +264,7 @@
     pos_hit = jnp.any(pos_slots[:, :, None] == slot_ids[None, None, :], axis=1)
     ask = pl.pallas_call(
         functools.partial(ask_kernel, (ring, narrow_count, blocks_here)),
-        out_shape=jax.ShapeDtypeStruct((sources, QTILE), jnp.int32),
+        out_shape=jax.ShapeDtypeStruct((sources, 2 * QTILE), jnp.int32),
         in_specs=[smem] * 5,
         out_specs=smem,
         cost_estimate=pl.CostEstimate(flops=10**6, bytes_accessed=2**16, transcendentals=0),
@@ -268,37 +277,18 @@
         tile_bits(tile_hit),
         tile_bits(jnp.logical_or(tile_hit, pos_hit)),
     )
-    table = lax.all_to_all(table, SAME_CORE, 0, 0, tiled=True)
-
     first_row = narrow_pos * own_rows
     lse_own = lax.dynamic_slice_in_dim(lse_shift, first_row, own_rows, 0)
     loss_own = lax.dynamic_slice_in_dim(loss_weight, first_row, own_rows, 0)
     pos_own = lax.dynamic_slice_in_dim(positives, first_row, own_rows, 0)
     lse_full = lse_own + math.log(fetch_count * narrow_count * BLOCK)
     shift = jnp.log2(loss_own) - lse_full * math.log2(math.e)
-    per_query = jnp.concatenate([shift, loss_own, pos_own.astype(jnp.float32), jnp.zeros_like(shift)])
-    per_query = jnp.broadcast_to(per_query.reshape(8, QTILE)[None], (sources, 8, QTILE))
-    rows = lax.all_to_all(per_query, SAME_CORE, 0, 0, tiled=True)
-    rows = jnp.concatenate([rows, jnp.full((1, 8, QTILE), -1.0, jnp.float32)], axis=0)
-
-    halves = []
-    for h in range(2):
-        part = queries[h * QTILE : (h + 1) * QTILE]
-        spread = jnp.broadcast_to(part[None], (sources, QTILE, feat_width))
-        part = lax.all_to_all(spread, SAME_CORE, 0, 0, tiled=True)
-        halves.append(jnp.concatenate([part, jnp.zeros((1, QTILE, feat_width), part.dtype)]))
-
-    held_shape = jax.ShapeDtypeStruct((2 * blocks_here, feat_width, BLOCK), jnp.bfloat16)
-    turn = pl.pallas_call(
-        turn_kernel,
-        out_shape=(held_shape, held_shape),
-        in_specs=[vmem, vmem],
-        out_specs=(vmem, vmem),
-        compiler_params=limit,
-        cost_estimate=pl.CostEstimate(flops=10**9, bytes_accessed=2**24, transcendentals=0),
-        name="turn",
-    )
-    blocks, turned = turn(held, mate_held)
+    per_query = jnp.concatenate([shift, loss_own, pos_own.astype(jnp.float32)]).reshape(6, QTILE)
+    per_query = jnp.broadcast_to(per_query[None], (sources, 6, QTILE))
+    packed = table.astype(jnp.float32).reshape(sources, 2, QTILE)
+    packed = jnp.concatenate([per_query, packed], axis=1)
+    rows = lax.all_to_all(packed, SAME_CORE, 0, 0, tiled=True)
+    table = rows[:, 6:].astype(jnp.int32).reshape(sources, 2 * QTILE)
     most = sources * PLACES * (tiles // 2) + 4 * UNROLL
     list_shape = jax.ShapeDtypeStruct((most,), jnp.int32)
     entries = sources // 4 * PLACES
@@ -317,35 +307,41 @@
     grad_shape = jax.ShapeDtypeStruct((sources, QTILE, feat_width), jnp.bfloat16)
     own_shape = jax.ShapeDtypeStruct((blocks_here, BLOCK, feat_width), jnp.float32)
     mate_shape = jax.ShapeDtypeStruct((blocks_here, BLOCK, feat_width), jnp.bfloat16)
-    scratch = [
-        pltpu.VMEM((sources + 1, feat_width, QTILE), jnp.bfloat16),
-        pltpu.VMEM((sources + 1, feat_width, QTILE), jnp.float32),
-        pltpu.VMEM((UNROLL, BLOCK, 2 * QTILE), jnp.float32),
-        pltpu.VMEM((UNROLL, BLOCK, 2 * QTILE), jnp.bfloat16),
-    ]
+
+    def scratch(extra):
+        return extra + [
+            pltpu.VMEM((sources + 1, 8, QTILE), jnp.float32),
+            pltpu.VMEM((sources + 1, QTILE, feat_width), jnp.bfloat16),
+            pltpu.VMEM((2 * blocks_here, BLOCK, feat_width), jnp.bfloat16),
+            pltpu.VMEM((sources + 1, feat_width, QTILE), jnp.float32),
+            pltpu.VMEM((UNROLL, BLOCK, 2 * QTILE), jnp.float32),
+            pltpu.SemaphoreType.DMA((5,)),
+        ]
+
+    hbm = pl.BlockSpec(memory_space=pl.ANY)
     cost = pl.CostEstimate(flops=2 * 10**10, bytes_accessed=2**25, transcendentals=10**7)
     chunk_0 = pl.pallas_call(
-        functools.partial(chunk_kernel, 0, True, False),
+        functools.partial(chunk_kernel, 0, False),
         out_shape=(grad_shape, acc_shape),
-        in_specs=[smem, smem, vmem, vmem, vmem, vmem],
+        in_specs=[smem, smem] + [hbm] * 4,
         out_specs=(vmem, vmem),
-        scratch_shapes=scratch,
+        scratch_shapes=scratch([]),
         compiler_params=limit,
         cost_estimate=cost,
         name="chunk_0",
     )
-    grad_0, acc = chunk_0(items[0], counts, rows, halves[0], blocks, turned)
+    grad_0, acc = chunk_0(items[0], counts, rows, halves[0], held, mate_held)
     chunk_1 = pl.pallas_call(
-        functools.partial(chunk_kernel, 1, False, True),
+        functools.partial(chunk_kernel, 1, True),
         out_shape=(grad_shape, own_shape, mate_shape),
-        in_specs=[smem, smem, vmem, vmem, vmem, vmem, pl.BlockSpec(memory_space=pl.ANY)],
+        in_specs=[smem, smem] + [hbm] * 5,
         out_specs=(vmem, vmem, vmem),
-        scratch_shapes=scratch + [pltpu.VMEM(acc_shape.shape, jnp.float32), pltpu.SemaphoreType.DMA],
+        scratch_shapes=scratch([pltpu.VMEM(acc_shape.shape, jnp.float32)] * 2),
         compiler_params=limit,
         cost_estimate=cost,
         name="chunk_1",
     )
-    grad_1, own_grad, mate_grad = chunk_1(items[1], counts, rows, halves[1], blocks, turned, acc)
+    grad_1, own_grad, mate_grad = chunk_1(items[1], counts, rows, halves[1], held, mate_held, acc)
     sums = []
     for part in (grad_0, grad_1):
         came = lax.all_to_all(part, SAME_CORE, 0, 0, tiled=True)

time: 345 us -> 269 us (0.78)
  blocking collectives: 57.3 us -> 0 us
  starting transfers between devices: 53.7 us -> 89.8 us
  waiting for transfers between devices: 89 us -> 59.4 us
  Pallas kernels: 110 us -> 86.8 us
  local copies, waits for them, and re-layouts: 19.7 us -> 15.3 us
    all_to_all x1 -> x0, blocking collectives: 57.3 us -> none  [shard_work(): came = lax.all_to_all(part, SAME_CORE, 0, 0, tiled=True)]
    all_to_all x1 -> x2, starting transfers between devices: 4.88 us -> 46.2 us  [shard_work(): came = lax.all_to_all(part, SAME_CORE, 0, 0, tiled=True)]
    pallas_call x3 -> x2, Pallas kernels: 91.1 us -> 65.9 us  [the longest x1 33.9 us: shard_work(): chunk_1(items[1], counts, rows, halves[1], held, mate_held, acc)]
    ppermute x6, waiting for transfers between devices: 20.2 us -> 7 us  [shard_work(): lax.ppermute(stored[at], axis, way)]
    all_to_all x4 -> x3, waiting for transfers between devices: 33.9 us -> 23.1 us  [the longest x2 23.1 us: shard_work(): halves.append(lax.all_to_all(spread, SAME_CORE, 0, 0, tiled=True))]
    all_to_all x1 -> x2, waiting for transfers between devices: 27.3 us -> 21.7 us  [shard_work(): came = lax.all_to_all(part, SAME_CORE, 0, 0, tiled=True)]
    concatenate x4 -> x0, local copies, waits for them, and re-layouts: 5.53 us -> none  [the longest x2 4.73 us: shard_work(): jnp.concatenate([part, jnp.zeros((1, QTILE, feat_width), part.dtype)])]
    all_to_all x4 -> x3, starting transfers between devices: 28.4 us -> 25 us  [the longest x2 13.5 us: shard_work(): halves.append(lax.all_to_all(spread, SAME_CORE, 0, 0, tiled=True))]
  transfers between devices with their start and end apart: 19 -> 19, of which waited for: 8 -> 5; matrix products, arithmetic and copies ran while one was open for 6% -> 6% of each run, Pallas kernels for 4% -> 30%
where the time goes in v1:
time: 269 us; the launch traced here: 266 us
  starting transfers between devices  89.8 us (33%)
  Pallas kernels  86.8 us (32%)
  waiting for transfers between devices  59.4 us (22%)
  local copies, waits for them, and re-layouts  15.3 us (6%)
  other arithmetic  14.2 us (5%)
    all_to_all x2, starting transfers between devices, shard_work(): came = lax.all_to_all(part, SAME_CORE, 0, 0, tiled=True)  46.2 us
    pallas_call x1, Pallas kernels, shard_work(): chunk_1(items[1], counts, rows, halves[1], held, mate_held, acc)  33.9 us
    pallas_call x1, Pallas kernels, shard_work(): grad_0, acc = chunk_0(items[0], counts, rows, halves[0], held, mate_held)  32 us
    all_to_all x2, waiting for transfers between devices, shard_work(): halves.append(lax.all_to_all(spread, SAME_CORE, 0, 0, tiled=True))  23.1 us
    all_to_all x2, waiting for transfers between devices, shard_work(): came = lax.all_to_all(part, SAME_CORE, 0, 0, tiled=True)  21.7 us
    pallas_call x1, Pallas kernels, shard_work(): *items, counts = listing(table)  14.1 us
    all_to_all x2, starting transfers between devices, shard_work(): halves.append(lax.all_to_all(spread, SAME_CORE, 0, 0, tiled=True))  13.5 us
    all_to_all x1, starting transfers between devices, shard_work(): rows = lax.all_to_all(packed, SAME_CORE, 0, 0, tiled=True)  11.5 us
  transfers between devices with their start and end apart: 19, of which 5 were waited for; matrix products, arithmetic and copies ran while one was open for 6% of the time, Pallas kernels for 30%

profile of v1, /device:TPU:0, one launch (start us, length us, event | category | flops | bytes accessed | tf_op | source)
XLA Modules:
  0.0 266.4 jit_solution(7579667052316222528)
XLA Ops:
  0.6 0.7 add_select_fusion
  1.4 0.8 convert_bitcast_fusion
  2.1 1.5 compare_reduce_fusion
  3.7 0.7 compare_reduce_fusion.1
  4.4 0.6 pad_add_fusion.where
  5.0 0.6 shift-left_reduce_fusion
  5.6 6.8 %ask.1 = s32[64,256]{1,0:T(8,128)} custom-call(s32[2]{0:T(128)} %pad_add_fusion.where, s32[64]{0:T(128)} %bitcast.47, s32[64]{0:T(128)} %local.1, s32[64]{0:T(128)} %get-tuple-element.19.hits, s32[64]{0:T(128)} %get-tuple-element.18.lives), custom_call_target="tpu_custom_call" | custom-call | flops 1000000 | bytes 65536 | tf_op jit(solution)/shard_map/ask/pallas_call | solution.py:273
  12.4 0.8 convert_element_type.51
  13.3 0.8 subtract_bitcast_fusion
  14.1 0.8 pad_maximum_fusion
  14.9 11.5 %all-to-all-start = ((f32[64,8,128]{2,1,0:T(8,128)}), f32[64,8,128]{2,1,0:T(8,128)S(1)}, u32[]{:S(2)}, u32[]{:S(2)}) async-start(f32[64,8,128]{2,1,0:T(8,128)} %pad_maximum_fusion), calls=%async_computation | async-start | bytes 524288 | tf_op jit(solution)/shard_map/all_to_all | solution.py:290
  26.4 1.5 fusion.5
  27.9 3.1 %collective-permute-start.3 = (bf16[8,128,128]{2,1,0:T(8,128)(2,1)S(1)}, bf16[8,128,128]{2,1,0:T(8,128)(2,1)}, u32[]{:S(2)}, u32[]{:S(2)}) collective-permute-start(bf16[8,128,128]{2,1,0:T(8,128)(2,1)S(1)} %bitcast.40), channel_id=1, source_target_pairs={{0,96},{32,0},{64,32},{96,64},{1,97},{33,1},{65,33},{97,65},{2,98}... | collective-permute-start | bytes 786440 | tf_op jit(solution)/shard_map/ppermute | solution.py:250
  31.0 2.8 %collective-permute-start.5 = (bf16[8,128,128]{2,1,0:T(8,128)(2,1)S(1)}, bf16[8,128,128]{2,1,0:T(8,128)(2,1)S(1)}, u32[]{:S(2)}, u32[]{:S(2)}) collective-permute-start(bf16[8,128,128]{2,1,0:T(8,128)(2,1)S(1)} %bitcast.38), channel_id=1, source_target_pairs={{0,12},{4,0},{8,4},{12,8},{1,13},{5,1},{9,5},{13,9},{2,14},{6,2},{... | collective-permute-start | bytes 786440 | tf_op jit(solution)/shard_map/ppermute | solution.py:250
  33.8 2.7 %collective-permute-start.1 = (bf16[8,128,128]{2,1,0:T(8,128)(2,1)S(1)}, bf16[8,128,128]{2,1,0:T(8,128)(2,1)S(1)}, u32[]{:S(2)}, u32[]{:S(2)}) collective-permute-start(bf16[8,128,128]{2,1,0:T(8,128)(2,1)S(1)} %bitcast.42), channel_id=1, source_target_pairs={{0,3},{1,0},{2,1},{3,2},{4,7},{5,4},{6,5},{7,6},{8,11},{9,8},{10,9... | collective-permute-start | bytes 786440 | tf_op jit(solution)/shard_map/ppermute | solution.py:250
  36.5 0.8 constant_dynamic-update-slice_fusion.6
  37.3 7.0 %collective-permute-done = bf16[8,128,128]{2,1,0:T(8,128)(2,1)S(1)} collective-permute-done((bf16[8,128,128]{2,1,0:T(8,128)(2,1)S(1)}, bf16[8,128,128]{2,1,0:T(8,128)(2,1)S(1)}, u32[]{:S(2)}, u32[]{:S(2)}) %collective-permute-start) | collective-permute-done | bytes 262176 | tf_op jit(solution)/shard_map/ppermute | solution.py:250
  44.3 0.7 constant_dynamic-update-slice_fusion.5
  45.0 0.7 constant_dynamic-update-slice_fusion.4
  45.8 0.7 constant_dynamic-update-slice_fusion.3
  46.5 1.8 broadcast_in_dim.7
  48.3 7.9 %all-to-all-start.1 = ((bf16[64,128,128]{2,1,0:T(8,128)(2,1)}), bf16[64,128,128]{2,1,0:T(8,128)(2,1)S(1)}, u32[]{:S(2)}, u32[]{:S(2)}) async-start(bf16[64,128,128]{2,1,0:T(8,128)(2,1)} %broadcast_in_dim.7), calls=%async_computation.1 | async-start | bytes 4194304 | tf_op jit(solution)/shard_map/all_to_all | solution.py:243
  56.2 1.7 constant_dynamic-update-slice_fusion.2
  57.9 1.7 constant_dynamic-update-slice_fusion.1
  59.6 0.7 constant_dynamic-update-slice_fusion.own_in
  60.3 23.1 %all-to-all-done.1.q_in = bf16[64,128,128]{2,1,0:T(8,128)(2,1)S(1)} async-done(((bf16[64,128,128]{2,1,0:T(8,128)(2,1)}), bf16[64,128,128]{2,1,0:T(8,128)(2,1)S(1)}, u32[]{:S(2)}, u32[]{:S(2)}) %all-to-all-start.1) | async-done | bytes 2097184 | tf_op jit(solution)/shard_map/all_to_all | solution.py:243
  83.4 2.0 broadcast_in_dim.8
  85.4 5.6 %all-to-all-start.3 = ((bf16[64,128,128]{2,1,0:T(8,128)(2,1)}), bf16[64,128,128]{2,1,0:T(8,128)(2,1)}, u32[]{:S(2)}, u32[]{:S(2)}) async-start(bf16[64,128,128]{2,1,0:T(8,128)(2,1)} %broadcast_in_dim.8), calls=%async_computation.3 | async-start | bytes 4194304 | tf_op jit(solution)/shard_map/all_to_all | solution.py:243
  91.0 0.6 copy.12
  91.6 14.1 %listing.1 = (s32[28704]{0:T(1024)}, s32[28704]{0:T(1024)}, s32[2]{0:T(128)}) custom-call(s32[64,256]{1,0:T(8,128)} %bitcast.46), custom_call_target="tpu_custom_call" | custom-call | flops 1000000000 | bytes 1048576 | tf_op jit(solution)/shard_map/listing/pallas_call | solution.py:304
  105.7 32.0 %chunk_0.1 = (bf16[64,128,128]{2,1,0:T(8,128)(2,1)}, f32[128,128,128]{2,1,0:T(8,128)}) custom-call(s32[28704]{0:T(1024)} %get-tuple-element.10.items, s32[2]{0:T(128)} %get-tuple-element.11.counts, f32[64,8,128]{2,1,0:T(8,128)} %copy-done.1, bf16[64,128,128]{2,1,0:T(8,128)(2,1)} %copy-done, bf16[64,128,128]{2,1,0:T(8,128)(2,1)} %constant_dynamic-update-slice_fusion.own_in, ...), custom_call_target="tpu_custom_call" | custom-call | flops 20000000000 | bytes 33554432 | tf_op jit(solution)/shard_map/chunk_0/pallas_call | solution.py:333
  137.7 24.4 %all-to-all-start.2 = ((bf16[64,128,128]{2,1,0:T(8,128)(2,1)}), bf16[64,128,128]{2,1,0:T(8,128)(2,1)S(1)}, u32[]{:S(2)}, u32[]{:S(2)}) async-start(bf16[64,128,128]{2,1,0:T(8,128)(2,1)} %get-tuple-element.12), calls=%async_computation.2 | async-start | bytes 4194304 | tf_op jit(solution)/shard_map/all_to_all | solution.py:347
  162.2 33.9 %chunk_1.1 = (bf16[64,128,128]{2,1,0:T(8,128)(2,1)}, f32[64,128,128]{2,1,0:T(8,128)}, bf16[64,128,128]{2,1,0:T(8,128)(2,1)}) custom-call(s32[28704]{0:T(1024)} %get-tuple-element.13.items, s32[2]{0:T(128)} %get-tuple-element.11.counts, f32[64,8,128]{2,1,0:T(8,128)} %copy-done.1, bf16[64,128,128]{2,1,0:T(8,128)(2,1)} %all-to-all-done.3.q_in, ...), custom_call_target="tpu_custom_call" | custom-call | flops 20000000000 | bytes 33554432 | tf_op jit(solution)/shard_map/chunk_1/pallas_call | solution.py:344
  196.1 21.8 %all-to-all-start.4 = ((bf16[64,128,128]{2,1,0:T(8,128)(2,1)}), bf16[64,128,128]{2,1,0:T(8,128)(2,1)}, u32[]{:S(2)}, u32[]{:S(2)}) async-start(bf16[64,128,128]{2,1,0:T(8,128)(2,1)} %get-tuple-element.15), calls=%async_computation.4 | async-start | bytes 4194304 | tf_op jit(solution)/shard_map/all_to_all | solution.py:347
  217.9 0.3 collective-permute-start.7
  218.1 0.3 convert_reduce_fusion.1
  218.5 21.7 %all-to-all-done.4 = bf16[64,128,128]{2,1,0:T(8,128)(2,1)} async-done(((bf16[64,128,128]{2,1,0:T(8,128)(2,1)}), bf16[64,128,128]{2,1,0:T(8,128)(2,1)}, u32[]{:S(2)}, u32[]{:S(2)}) %all-to-all-start.4) | async-done | bytes 2097184 | tf_op jit(solution)/shard_map/all_to_all | solution.py:347
  240.2 1.9 convert_reduce_fusion
  242.1 0.7 pad_maximum_fusion.1
  242.8 3.7 %fusion.3 = (bf16[64,128,128]{2,1,0:T(8,128)(2,1)S(1)}, f32[64,128,128]{2,1,0:T(8,128)S(1)}) fusion(f32[64,128,128]{2,1,0:T(8,128)} %get-tuple-element.16, bf16[64,128,128]{2,1,0:T(8,128)(2,1)} %collective-permute-done.7), kind=kLoop, calls=%fused_computation.40 | loop fusion | flops 3145728 | bytes 12582912 | tf_op jit(solution)/shard_map/convert.5
  246.6 0.7 collective-permute-start.13
  247.3 2.6 collective-permute-start.12
  249.9 0.4 collective-permute-start.9
  250.3 2.9 %collective-permute-start.8 = (bf16[8,128,128]{2,1,0:T(8,128)(2,1)S(1)}, bf16[8,128,128]{2,1,0:T(8,128)(2,1)S(1)}, u32[]{:S(2)}, u32[]{:S(2)}) collective-permute-start(bf16[8,128,128]{2,1,0:T(8,128)(2,1)S(1)} %get-tuple-element.27), channel_id=1, source_target_pairs={{1,0},{2,1},{3,2},{0,3},{5,4},{6,5},{7,6},{4,7},{9,8},{10,9},{11,1... | collective-permute-start | bytes 786440 | tf_op jit(solution)/shard_map/ppermute | solution.py:353
  253.3 3.8 %collective-permute-done.8 = bf16[8,128,128]{2,1,0:T(8,128)(2,1)S(1)} collective-permute-done((bf16[8,128,128]{2,1,0:T(8,128)(2,1)S(1)}, bf16[8,128,128]{2,1,0:T(8,128)(2,1)S(1)}, u32[]{:S(2)}, u32[]{:S(2)}) %collective-permute-start.8) | collective-permute-done | bytes 262176 | tf_op jit(solution)/shard_map/ppermute | solution.py:353
  257.1 3.2 %collective-permute-start.10 = (bf16[8,128,128]{2,1,0:T(8,128)(2,1)S(1)}, bf16[8,128,128]{2,1,0:T(8,128)(2,1)S(1)}, u32[]{:S(2)}, u32[]{:S(2)}) collective-permute-start(bf16[8,128,128]{2,1,0:T(8,128)(2,1)S(1)} %get-tuple-element.25), channel_id=1, source_target_pairs={{32,0},{64,32},{96,64},{0,96},{33,1},{65,33},{97,65},{1,97},{34,2}... | collective-permute-start | bytes 786440 | tf_op jit(solution)/shard_map/ppermute | solution.py:353
  260.4 3.8 %collective-permute-done.10 = bf16[8,128,128]{2,1,0:T(8,128)(2,1)S(1)} collective-permute-done((bf16[8,128,128]{2,1,0:T(8,128)(2,1)S(1)}, bf16[8,128,128]{2,1,0:T(8,128)(2,1)S(1)}, u32[]{:S(2)}, u32[]{:S(2)}) %collective-permute-start.10) | collective-permute-done | bytes 262176 | tf_op jit(solution)/shard_map/ppermute | solution.py:353
  264.4 2.0 copy-done.2
  (42 shorter events, 0.7 us)
Async XLA Ops:
  14.1 22.3 %copy-start.3 = (bf16[256,128]{1,0:T(8,128)(2,1)S(1)}, bf16[256,128]{1,0:T(8,128)(2,1)}, u32[]{:S(2)}) copy-start(bf16[256,128]{1,0:T(8,128)(2,1)} %param.8) | copy-start | bytes 196612
  14.9 31.6 %all-to-all-start = ((f32[64,8,128]{2,1,0:T(8,128)}), f32[64,8,128]{2,1,0:T(8,128)S(1)}, u32[]{:S(2)}, u32[]{:S(2)}) async-start(f32[64,8,128]{2,1,0:T(8,128)} %pad_maximum_fusion), calls=%async_computation | async-start | bytes 524288 | tf_op jit(solution)/shard_map/all_to_all | solution.py:290
  26.4 10.1 %slice-start = ((bf16[8192,128]{1,0:T(8,128)(2,1)}), bf16[2048,128]{1,0:T(8,128)(2,1)S(1)}, s32[]{:S(2)}) async-start(bf16[8192,128]{1,0:T(8,128)(2,1)} %param.9), calls=%async_computation.5 | async-start | bytes 1048576 | tf_op jit(solution)/shard_map/slice | solution.py:251
  27.9 28.3 %collective-permute-start.3 = (bf16[8,128,128]{2,1,0:T(8,128)(2,1)S(1)}, bf16[8,128,128]{2,1,0:T(8,128)(2,1)}, u32[]{:S(2)}, u32[]{:S(2)}) collective-permute-start(bf16[8,128,128]{2,1,0:T(8,128)(2,1)S(1)} %bitcast.40), channel_id=1, source_target_pairs={{0,96},{32,0},{64,32},{96,64},{1,97},{33,1},{65,33},{97,65},{2,98}... | collective-permute-start | bytes 786440 | tf_op jit(solution)/shard_map/ppermute | solution.py:250
  31.0 28.6 %collective-permute-start.5 = (bf16[8,128,128]{2,1,0:T(8,128)(2,1)S(1)}, bf16[8,128,128]{2,1,0:T(8,128)(2,1)S(1)}, u32[]{:S(2)}, u32[]{:S(2)}) collective-permute-start(bf16[8,128,128]{2,1,0:T(8,128)(2,1)S(1)} %bitcast.38), channel_id=1, source_target_pairs={{0,12},{4,0},{8,4},{12,8},{1,13},{5,1},{9,5},{13,9},{2,14},{6,2},{... | collective-permute-start | bytes 786440 | tf_op jit(solution)/shard_map/ppermute | solution.py:250
  33.8 12.0 %collective-permute-start.2 = (bf16[8,128,128]{2,1,0:T(8,128)(2,1)S(1)}, bf16[8,128,128]{2,1,0:T(8,128)(2,1)S(1)}, u32[]{:S(2)}, u32[]{:S(2)}) collective-permute-start(bf16[8,128,128]{2,1,0:T(8,128)(2,1)S(1)} %bitcast.41), channel_id=1, source_target_pairs={{0,32},{32,64},{64,96},{96,0},{1,33},{33,65},{65,97},{97,1},{2,34}... | collective-permute-start | bytes 786440 | tf_op jit(solution)/shard_map/ppermute | solution.py:250
  33.8 11.3 %collective-permute-start.1 = (bf16[8,128,128]{2,1,0:T(8,128)(2,1)S(1)}, bf16[8,128,128]{2,1,0:T(8,128)(2,1)S(1)}, u32[]{:S(2)}, u32[]{:S(2)}) collective-permute-start(bf16[8,128,128]{2,1,0:T(8,128)(2,1)S(1)} %bitcast.42), channel_id=1, source_target_pairs={{0,3},{1,0},{2,1},{3,2},{4,7},{5,4},{6,5},{7,6},{8,11},{9,8},{10,9... | collective-permute-start | bytes 786440 | tf_op jit(solution)/shard_map/ppermute | solution.py:250
  36.5 7.9 %collective-permute-start = (bf16[8,128,128]{2,1,0:T(8,128)(2,1)S(1)}, bf16[8,128,128]{2,1,0:T(8,128)(2,1)S(1)}, u32[]{:S(2)}, u32[]{:S(2)}) collective-permute-start(bf16[8,128,128]{2,1,0:T(8,128)(2,1)S(1)} %bitcast.43), channel_id=1, source_target_pairs={{0,1},{1,2},{2,3},{3,0},{4,5},{5,6},{6,7},{7,4},{8,9},{9,10},{10,1... | collective-permute-start | bytes 786440 | tf_op jit(solution)/shard_map/ppermute | solution.py:250
  44.3 13.6 %collective-permute-start.4 = (bf16[8,128,128]{2,1,0:T(8,128)(2,1)S(1)}, bf16[8,128,128]{2,1,0:T(8,128)(2,1)}, u32[]{:S(2)}, u32[]{:S(2)}) collective-permute-start(bf16[8,128,128]{2,1,0:T(8,128)(2,1)S(1)} %bitcast.39), channel_id=1, source_target_pairs={{0,4},{4,8},{8,12},{12,0},{1,5},{5,9},{9,13},{13,1},{2,6},{6,10},{... | collective-permute-start | bytes 786440 | tf_op jit(solution)/shard_map/ppermute | solution.py:250
  46.5 44.5 %copy-start.1 = (f32[64,8,128]{2,1,0:T(8,128)}, f32[64,8,128]{2,1,0:T(8,128)S(1)}, u32[]{:S(2)}) copy-start(f32[64,8,128]{2,1,0:T(8,128)S(1)} %all-to-all-done.rows_in) | copy-start | bytes 786436
  48.3 35.1 %all-to-all-start.1 = ((bf16[64,128,128]{2,1,0:T(8,128)(2,1)}), bf16[64,128,128]{2,1,0:T(8,128)(2,1)S(1)}, u32[]{:S(2)}, u32[]{:S(2)}) async-start(bf16[64,128,128]{2,1,0:T(8,128)(2,1)} %broadcast_in_dim.7), calls=%async_computation.1 | async-start | bytes 4194304 | tf_op jit(solution)/shard_map/all_to_all | solution.py:243
  60.3 45.4 %collective-permute-start.6 = (bf16[64,128,128]{2,1,0:T(8,128)(2,1)}, bf16[64,128,128]{2,1,0:T(8,128)(2,1)}, u32[]{:S(2)}, u32[]{:S(2)}) collective-permute-start(bf16[64,128,128]{2,1,0:T(8,128)(2,1)} %constant_dynamic-update-slice_fusion.own_in), channel_id=1, source_target_pairs={{0,16},{16,0},{1,17},{17,1},{2,18},{18,2},{3,19},{19,3},{4,20},{20... | collective-permute-start | bytes 6291464 | tf_op jit(solution)/shard_map/ppermute | solution.py:252
  83.4 2.0 copy-start
  85.4 52.4 %all-to-all-start.3 = ((bf16[64,128,128]{2,1,0:T(8,128)(2,1)}), bf16[64,128,128]{2,1,0:T(8,128)(2,1)}, u32[]{:S(2)}, u32[]{:S(2)}) async-start(bf16[64,128,128]{2,1,0:T(8,128)(2,1)} %broadcast_in_dim.8), calls=%async_computation.3 | async-start | bytes 4194304 | tf_op jit(solution)/shard_map/all_to_all | solution.py:243
  137.7 58.3 %all-to-all-start.2 = ((bf16[64,128,128]{2,1,0:T(8,128)(2,1)}), bf16[64,128,128]{2,1,0:T(8,128)(2,1)S(1)}, u32[]{:S(2)}, u32[]{:S(2)}) async-start(bf16[64,128,128]{2,1,0:T(8,128)(2,1)} %get-tuple-element.12), calls=%async_computation.2 | async-start | bytes 4194304 | tf_op jit(solution)/shard_map/all_to_all | solution.py:347
  196.1 44.1 %all-to-all-start.4 = ((bf16[64,128,128]{2,1,0:T(8,128)(2,1)}), bf16[64,128,128]{2,1,0:T(8,128)(2,1)}, u32[]{:S(2)}, u32[]{:S(2)}) async-start(bf16[64,128,128]{2,1,0:T(8,128)(2,1)} %get-tuple-element.15), calls=%async_computation.4 | async-start | bytes 4194304 | tf_op jit(solution)/shard_map/all_to_all | solution.py:347
  217.9 24.9 %collective-permute-start.7 = (bf16[64,128,128]{2,1,0:T(8,128)(2,1)}, bf16[64,128,128]{2,1,0:T(8,128)(2,1)}, u32[]{:S(2)}, u32[]{:S(2)}) collective-permute-start(bf16[64,128,128]{2,1,0:T(8,128)(2,1)} %get-tuple-element.17), channel_id=1, source_target_pairs={{0,16},{16,0},{1,17},{17,1},{2,18},{18,2},{3,19},{19,3},{4,20},{20... | collective-permute-start | bytes 6291464 | tf_op jit(solution)/shard_map/ppermute | solution.py:350
  246.6 17.7 %collective-permute-start.13 = (bf16[8,128,128]{2,1,0:T(8,128)(2,1)S(1)}, bf16[8,128,128]{2,1,0:T(8,128)(2,1)S(1)}, u32[]{:S(2)}, u32[]{:S(2)}) collective-permute-start(bf16[8,128,128]{2,1,0:T(8,128)(2,1)S(1)} %get-tuple-element.22), channel_id=1, source_target_pairs={{12,0},{0,4},{4,8},{8,12},{13,1},{1,5},{5,9},{9,13},{14,2},{2,6},{... | collective-permute-start | bytes 786440 | tf_op jit(solution)/shard_map/ppermute | solution.py:353
  247.3 17.0 %collective-permute-start.12 = (bf16[8,128,128]{2,1,0:T(8,128)(2,1)S(1)}, bf16[8,128,128]{2,1,0:T(8,128)(2,1)S(1)}, u32[]{:S(2)}, u32[]{:S(2)}) collective-permute-start(bf16[8,128,128]{2,1,0:T(8,128)(2,1)S(1)} %get-tuple-element.23), channel_id=1, source_target_pairs={{4,0},{8,4},{12,8},{0,12},{5,1},{9,5},{13,9},{1,13},{6,2},{10,6},{... | collective-permute-start | bytes 786440 | tf_op jit(solution)/shard_map/ppermute | solution.py:353
  249.9 14.3 %collective-permute-start.11 = (bf16[8,128,128]{2,1,0:T(8,128)(2,1)S(1)}, bf16[8,128,128]{2,1,0:T(8,128)(2,1)S(1)}, u32[]{:S(2)}, u32[]{:S(2)}) collective-permute-start(bf16[8,128,128]{2,1,0:T(8,128)(2,1)S(1)} %get-tuple-element.24), channel_id=1, source_target_pairs={{96,0},{0,32},{32,64},{64,96},{97,1},{1,33},{33,65},{65,97},{98,2}... | collective-permute-start | bytes 786440 | tf_op jit(solution)/shard_map/ppermute | solution.py:353
  249.9 10.4 %collective-permute-start.9 = (bf16[8,128,128]{2,1,0:T(8,128)(2,1)S(1)}, bf16[8,128,128]{2,1,0:T(8,128)(2,1)S(1)}, u32[]{:S(2)}, u32[]{:S(2)}) collective-permute-start(bf16[8,128,128]{2,1,0:T(8,128)(2,1)S(1)} %get-tuple-element.26), channel_id=1, source_target_pairs={{3,0},{0,1},{1,2},{2,3},{7,4},{4,5},{5,6},{6,7},{11,8},{8,9},{9,10... | collective-permute-start | bytes 786440 | tf_op jit(solution)/shard_map/ppermute | solution.py:353
  250.3 6.8 %collective-permute-start.8 = (bf16[8,128,128]{2,1,0:T(8,128)(2,1)S(1)}, bf16[8,128,128]{2,1,0:T(8,128)(2,1)S(1)}, u32[]{:S(2)}, u32[]{:S(2)}) collective-permute-start(bf16[8,128,128]{2,1,0:T(8,128)(2,1)S(1)} %get-tuple-element.27), channel_id=1, source_target_pairs={{1,0},{2,1},{3,2},{0,3},{5,4},{6,5},{7,6},{4,7},{9,8},{10,9},{11,1... | collective-permute-start | bytes 786440 | tf_op jit(solution)/shard_map/ppermute | solution.py:353
  257.1 7.1 %collective-permute-start.10 = (bf16[8,128,128]{2,1,0:T(8,128)(2,1)S(1)}, bf16[8,128,128]{2,1,0:T(8,128)(2,1)S(1)}, u32[]{:S(2)}, u32[]{:S(2)}) collective-permute-start(bf16[8,128,128]{2,1,0:T(8,128)(2,1)S(1)} %get-tuple-element.25), channel_id=1, source_target_pairs={{32,0},{64,32},{96,64},{0,96},{33,1},{65,33},{97,65},{1,97},{34,2}... | collective-permute-start | bytes 786440 | tf_op jit(solution)/shard_map/ppermute | solution.py:353
  264.4 2.0 copy-start.2

commit v2 on v1

--- a/solution.py
+++ b/solution.py
@@ -22,7 +22,7 @@
 FIELDS = 6
 COUNT_AT = PLACES * FIELDS
 DEAD = -1e30
-UNROLL = 8
+UNROLL = 12
 VMEM_LIMIT = 60 * 1024 * 1024
 
 
@@ -33,27 +33,30 @@
 
 def ask_kernel(sizes, where, owner, local, hits, lives, table):
     ring, narrow_count, blocks_here = sizes
+    ring_bits, narrow_bits = ring.bit_length() - 1, narrow_count.bit_length() - 1
+    slab_bits = SLAB.bit_length() - 1
     first_slot, core = where[0], where[1]
 
     def clear(d, carry):
         table[d, COUNT_AT] = 0
         return carry
 
-    lax.fori_loop(0, table.shape[0], clear, 0)
+    lax.fori_loop(0, table.shape[0], clear, 0, unroll=8)
 
     def ask(j, carry):
         own, block = owner[j], local[j]
-        wide = own // narrow_count
-        narrow = own % narrow_count
-        turn = jnp.where(block < KEPT, -1, (block - KEPT) // SLAB)
-        spot = {"y": wide // 2, "z": narrow // ring, "x": narrow % ring}
+        wide = own >> narrow_bits
+        narrow = own & (narrow_count - 1)
+        turn = (block - KEPT) >> slab_bits
+        spot = {"y": wide >> 1, "z": narrow >> ring_bits, "x": narrow & (ring - 1)}
         for k, (axis, shift) in enumerate(STEPS):
             spot[axis] = spot[axis] + jnp.where(turn == k, shift + ring, 0)
-        dest = ((spot["y"] % ring) * ring + spot["z"] % ring) * ring + spot["x"] % ring
+        edge = ring - 1
+        dest = ((spot["y"] & edge) << (2 * ring_bits)) | ((spot["z"] & edge) << ring_bits) | (spot["x"] & edge)
         place = table[dest, COUNT_AT]
         table[dest, COUNT_AT] = place + 1
         at = place * FIELDS
-        table[dest, at] = jnp.where(wide % 2 == core, 0, blocks_here) + block
+        table[dest, at] = jnp.where((wide & 1) == core, 0, blocks_here) + block
         table[dest, at + 1] = first_slot + j
         table[dest, at + 2] = hits[j] & 0xFFFF
         table[dest, at + 3] = (hits[j] >> 16) & 0xFFFF
@@ -61,10 +64,10 @@
         table[dest, at + 5] = (lives[j] >> 16) & 0xFFFF
         return carry
 
-    lax.fori_loop(0, owner.shape[0], ask, 0)
-
-
-def list_kernel(table, first_items, second_items, counts, live, base, hits):
+    lax.fori_loop(0, owner.shape[0], ask, 0, unroll=4)
+
+
+def list_kernel(table, first_items, second_items, counts, base, hits, live):
     groups = 4
     sources = table.shape[0]
     in_group = sources // groups
@@ -72,46 +75,49 @@
     lists = (first_items, second_items)
 
     def group_entries(group, cursor):
+        begin = cursor[2]
+
         def source_entries(n, count):
             src = group * in_group + n
 
             def place_entry(place, count):
                 at = place * FIELDS
-                base[count] = (table[src, at] << 7) | (table[src, at + 1] << 15)
+                base[count] = table[src, at] | (table[src, at + 1] << 7)
                 hits[count] = table[src, at + 2] | (table[src, at + 3] << 16)
                 live[count] = table[src, at + 4] | (table[src, at + 5] << 16)
                 return count + 1
 
             return lax.fori_loop(0, table[src, COUNT_AT], place_entry, count)
 
-        entries = lax.fori_loop(0, in_group, source_entries, jnp.int32(0))
-
-        def entry_items(e, cursor):
-            start = base[e] + group * in_group
+        finish = lax.fori_loop(0, in_group, source_entries, begin)
+
+        def entry_items(e, ends):
+            start = (e << 7) + group * in_group
             alive = live[e]
-            hit = hits[e]
-            empty = base[e] + dead
+            empty = (e << 7) + dead
             out = []
-            for h, at in enumerate(cursor):
+            for h, at in enumerate(ends):
                 for n in range(in_group):
-                    bit = 2 * n + h
-                    named = (hit << (25 - bit)) if bit <= 25 else (hit >> (bit - 25))
-                    lists[h][at] = (start + n) | (named & (1 << 25))
-                    at = at + ((alive >> bit) & 1)
+                    lists[h][at] = start + n
+                    at = at + ((alive >> (2 * n + h)) & 1)
                 lists[h][at] = empty
                 out.append(at + (at & 1))
             return tuple(out)
 
-        return lax.fori_loop(0, entries, entry_items, cursor)
-
-    ends = lax.fori_loop(0, groups, group_entries, (jnp.int32(0), jnp.int32(0)))
+        ends = lax.fori_loop(begin, finish, entry_items, cursor[:2])
+        return ends + (finish,)
+
+    zero = jnp.int32(0)
+    base[0] = zero
+    hits[0] = zero
+    ends = lax.fori_loop(0, groups, group_entries, (zero, zero, zero))
     for h in range(2):
         for i in range(4 * UNROLL):
             lists[h][ends[h] + i] = dead
         counts[h] = (ends[h] + 2 * UNROLL - 1) // (2 * UNROLL)
 
 
-def chunk_kernel(h, last, items, counts, rows_in, q_in, own_in, mate_in, *rest):
+def chunk_kernel(h, last, items, counts, base, hits, rows_in, q_in, own_in, mate_in, *rest):
     if last:
         earlier_in, query_out, own_out, mate_out, block_acc, earlier = rest[:6]
     else:
@@ -158,7 +164,7 @@
         return word & 127
 
     def block_of(word):
-        return (word >> 7) & 127
+        return base[word >> 7] & 127
 
     def block_grads(words, grad):
         block = block_of(words[0])
@@ -175,11 +181,11 @@
         query_acc[t2] = sum2
 
     def logit_grads(words, scores):
-        slot = (words[0] >> 15) & 1023
+        slot = base[words[0] >> 7] >> 7
         halves = []
         for side, word in enumerate(words):
             tile = tile_of(word)
-            hit = (word >> 25) & 1
+            hit = (hits[word >> 7] >> (2 * (tile & (tiles // 4 - 1)) + h)) & 1
             shift = rows[tile, pl.ds(h, 1), :]
             loss = rows[tile, pl.ds(2 + h, 1), :]
             positive = rows[tile, pl.ds(4 + h, 1), :].astype(jnp.int32)
@@ -223,6 +229,13 @@
             return carry
 
         lax.fori_loop(0, here, deliver, 0, unroll=2)
+
+
+def assemble_kernel(kept, *rest):
+    *back, out = rest
+    out[pl.ds(0, KEPT)] = kept[...]
+    for k, part in enumerate(back):
+        out[pl.ds(KEPT + SLAB * k, SLAB)] = part[...].astype(jnp.float32)
 
 
 def shard_work(
@@ -291,17 +304,17 @@
     table = rows[:, 6:].astype(jnp.int32).reshape(sources, 2 * QTILE)
     most = sources * PLACES * (tiles // 2) + 4 * UNROLL
     list_shape = jax.ShapeDtypeStruct((most,), jnp.int32)
-    entries = sources // 4 * PLACES
+    entry_shape = jax.ShapeDtypeStruct((sources * PLACES,), jnp.int32)
     listing = pl.pallas_call(
         list_kernel,
-        out_shape=(list_shape, list_shape, jax.ShapeDtypeStruct((2,), jnp.int32)),
+        out_shape=(list_shape, list_shape, jax.ShapeDtypeStruct((2,), jnp.int32), entry_shape, entry_shape),
         in_specs=[smem],
-        out_specs=(smem, smem, smem),
-        scratch_shapes=[pltpu.SMEM((entries,), jnp.int32)] * 3,
+        out_specs=(smem,) * 5,
+        scratch_shapes=[pltpu.SMEM(entry_shape.shape, jnp.int32)],
         cost_estimate=pl.CostEstimate(flops=10**9, bytes_accessed=2**20, transcendentals=0),
         name="listing",
     )
-    *items, counts = listing(table)
+    *items, counts, base, hits = listing(table)
 
     acc_shape = jax.ShapeDtypeStruct((2 * blocks_here, BLOCK, feat_width), jnp.float32)
     grad_shape = jax.ShapeDtypeStruct((sources, QTILE, feat_width), jnp.bfloat16)
@@ -323,25 +336,25 @@
     chunk_0 = pl.pallas_call(
         functools.partial(chunk_kernel, 0, False),
         out_shape=(grad_shape, acc_shape),
-        in_specs=[smem, smem] + [hbm] * 4,
+        in_specs=[smem] * 4 + [hbm] * 4,
         out_specs=(vmem, vmem),
         scratch_shapes=scratch([]),
         compiler_params=limit,
         cost_estimate=cost,
         name="chunk_0",
     )
-    grad_0, acc = chunk_0(items[0], counts, rows, halves[0], held, mate_held)
+    grad_0, acc = chunk_0(items[0], counts, base, hits, rows, halves[0], held, mate_held)
     chunk_1 = pl.pallas_call(
         functools.partial(chunk_kernel, 1, True),
         out_shape=(grad_shape, own_shape, mate_shape),
-        in_specs=[smem, smem] + [hbm] * 5,
+        in_specs=[smem] * 4 + [hbm] * 5,
         out_specs=(vmem, vmem, vmem),
         scratch_shapes=scratch([pltpu.VMEM(acc_shape.shape, jnp.float32)] * 2),
         compiler_params=limit,
         cost_estimate=cost,
         name="chunk_1",
     )
-    grad_1, own_grad, mate_grad = chunk_1(items[1], counts, rows, halves[1], held, mate_held, acc)
+    grad_1, own_grad, mate_grad = chunk_1(items[1], counts, base, hits, rows, halves[1], held, mate_held, acc)
     sums = []
     for part in (grad_0, grad_1):
         came = lax.all_to_all(part, SAME_CORE, 0, 0, tiled=True)
@@ -353,7 +366,16 @@
         lax.ppermute(held_grad[at].astype(jnp.bfloat16), axis, [(j, i) for i, j in way])
         for at, (axis, way) in zip(slabs, ways)
     ]
-    index_grad = jnp.concatenate([held_grad[:KEPT]] + [part.astype(jnp.float32) for part in back])
+    assemble = pl.pallas_call(
+        assemble_kernel,
+        out_shape=own_shape,
+        in_specs=[vmem] * (1 + len(back)),
+        out_specs=vmem,
+        compiler_params=limit,
+        cost_estimate=pl.CostEstimate(flops=10**6, bytes_accessed=2**23, transcendentals=0),
+        name="assemble",
+    )
+    index_grad = assemble(held_grad[:KEPT], *back)
     return (query_grad, index_grad.reshape(blocks_here * BLOCK, feat_width))
 
 

time: 269 us -> 257 us (0.955)
  waiting for transfers between devices: 59.4 us -> 50 us
  Pallas kernels: 86.8 us -> 84 us
    all_to_all x2, waiting for transfers between devices: 21.7 us -> 0.01 us  [shard_work(): came = lax.all_to_all(part, SAME_CORE, 0, 0, tiled=True)]
    ppermute x6, waiting for transfers between devices: 7.6 us -> 19.9 us  [shard_work(): lax.ppermute(held_grad[at].astype(jnp.bfloat16), axis, [(j, i) for i, j i...]
    all_to_all x2, starting transfers between devices: 46.2 us -> 42.4 us  [shard_work(): came = lax.all_to_all(part, SAME_CORE, 0, 0, tiled=True)]
    pallas_call x3 -> x4, Pallas kernels: 80 us -> 79.2 us  [the longest x1 32.5 us: shard_work(): chunk_1(items[1], counts, base, hits, rows, halves[1], held, mate_held, acc)]
    unnamed x16 -> x19, local copies, waits for them, and re-layouts: 9.05 us -> 8.98 us
  transfers between devices with their start and end apart: 19 -> 19, of which waited for: 5 -> 4; matrix products, arithmetic and copies ran while one was open for 6% -> 9% of each run, Pallas kernels for 30% -> 30%
where the time goes in v2:
time: 257 us; the launch traced here: 255 us
  starting transfers between devices  87.6 us (34%)
  Pallas kernels  84 us (33%)
  waiting for transfers between devices  50 us (19%)
  local copies, waits for them, and re-layouts  17.5 us (7%)
  other arithmetic  14.6 us (6%)
    all_to_all x2, starting transfers between devices, shard_work(): came = lax.all_to_all(part, SAME_CORE, 0, 0, tiled=True)  42.4 us
    pallas_call x1, Pallas kernels, shard_work(): chunk_1(items[1], counts, base, hits, rows, halves[1], held, mate_held, acc)  32.5 us
    pallas_call x1, Pallas kernels, shard_work(): chunk_0(items[0], counts, base, hits, rows, halves[0], held, mate_held)  30.1 us
    all_to_all x2, waiting for transfers between devices, shard_work(): halves.append(lax.all_to_all(spread, SAME_CORE, 0, 0, tiled=True))  23.1 us
    ppermute x6, waiting for transfers between devices, shard_work(): lax.ppermute(held_grad[at].astype(jnp.bfloat16), axis, [(j, i) for i, j i...  19.9 us
    all_to_all x2, starting transfers between devices, shard_work(): halves.append(lax.all_to_all(spread, SAME_CORE, 0, 0, tiled=True))  13.5 us
    pallas_call x1, Pallas kernels, shard_work(): *items, counts, base, hits = listing(table)  12.6 us
    ppermute x6, starting transfers between devices, shard_work(): lax.ppermute(held_grad[at].astype(jnp.bfloat16), axis, [(j, i) for i, j i...  11.7 us
  transfers between devices with their start and end apart: 19, of which 4 were waited for; matrix products, arithmetic and copies ran while one was open for 9% of the time, Pallas kernels for 30%

profile of v2, /device:TPU:0, one launch (start us, length us, event | category | flops | bytes accessed | tf_op | source)
XLA Modules:
  0.0 254.7 jit_solution(10466385898584521782)
XLA Ops:
  0.6 0.7 add_select_fusion
  1.4 0.8 convert_bitcast_fusion
  2.1 1.5 compare_reduce_fusion
  3.7 0.7 compare_reduce_fusion.1
  4.4 0.7 pad_add_fusion.where
  5.0 0.5 shift-left_reduce_fusion
  5.6 4.8 %ask.1 = s32[64,256]{1,0:T(8,128)} custom-call(s32[2]{0:T(128)} %pad_add_fusion.where, s32[64]{0:T(128)} %bitcast.47, s32[64]{0:T(128)} %local.1, s32[64]{0:T(128)} %get-tuple-element.23.hits, s32[64]{0:T(128)} %get-tuple-element.22.lives), custom_call_target="tpu_custom_call" | custom-call | flops 1000000 | bytes 65536 | tf_op jit(solution)/shard_map/ask/pallas_call | solution.py:286
  10.4 0.8 convert_element_type.33
  11.3 0.8 subtract_bitcast_fusion
  12.1 0.8 pad_maximum_fusion
  12.9 11.5 %all-to-all-start = ((f32[64,8,128]{2,1,0:T(8,128)}), f32[64,8,128]{2,1,0:T(8,128)S(1)}, u32[]{:S(2)}, u32[]{:S(2)}) async-start(f32[64,8,128]{2,1,0:T(8,128)} %pad_maximum_fusion), calls=%async_computation | async-start | bytes 524288 | tf_op jit(solution)/shard_map/all_to_all | solution.py:303
  24.4 1.5 fusion.5
  25.9 3.1 %collective-permute-start.3 = (bf16[8,128,128]{2,1,0:T(8,128)(2,1)S(1)}, bf16[8,128,128]{2,1,0:T(8,128)(2,1)}, u32[]{:S(2)}, u32[]{:S(2)}) collective-permute-start(bf16[8,128,128]{2,1,0:T(8,128)(2,1)S(1)} %bitcast.41), channel_id=1, source_target_pairs={{0,96},{32,0},{64,32},{96,64},{1,97},{33,1},{65,33},{97,65},{2,98}... | collective-permute-start | bytes 786440 | tf_op jit(solution)/shard_map/ppermute | solution.py:263
  29.0 2.8 %collective-permute-start.5 = (bf16[8,128,128]{2,1,0:T(8,128)(2,1)S(1)}, bf16[8,128,128]{2,1,0:T(8,128)(2,1)S(1)}, u32[]{:S(2)}, u32[]{:S(2)}) collective-permute-start(bf16[8,128,128]{2,1,0:T(8,128)(2,1)S(1)} %bitcast.39), channel_id=1, source_target_pairs={{0,12},{4,0},{8,4},{12,8},{1,13},{5,1},{9,5},{13,9},{2,14},{6,2},{... | collective-permute-start | bytes 786440 | tf_op jit(solution)/shard_map/ppermute | solution.py:263
  31.7 2.7 %collective-permute-start.1 = (bf16[8,128,128]{2,1,0:T(8,128)(2,1)S(1)}, bf16[8,128,128]{2,1,0:T(8,128)(2,1)S(1)}, u32[]{:S(2)}, u32[]{:S(2)}) collective-permute-start(bf16[8,128,128]{2,1,0:T(8,128)(2,1)S(1)} %bitcast.43), channel_id=1, source_target_pairs={{0,3},{1,0},{2,1},{3,2},{4,7},{5,4},{6,5},{7,6},{8,11},{9,8},{10,9... | collective-permute-start | bytes 786440 | tf_op jit(solution)/shard_map/ppermute | solution.py:263
  34.5 0.8 constant_dynamic-update-slice_fusion.6
  35.3 7.0 %collective-permute-done = bf16[8,128,128]{2,1,0:T(8,128)(2,1)S(1)} collective-permute-done((bf16[8,128,128]{2,1,0:T(8,128)(2,1)S(1)}, bf16[8,128,128]{2,1,0:T(8,128)(2,1)S(1)}, u32[]{:S(2)}, u32[]{:S(2)}) %collective-permute-start) | collective-permute-done | bytes 262176 | tf_op jit(solution)/shard_map/ppermute | solution.py:263
  42.3 0.7 constant_dynamic-update-slice_fusion.5
  43.0 0.7 constant_dynamic-update-slice_fusion.4
  43.8 0.7 constant_dynamic-update-slice_fusion.3
  44.5 1.8 broadcast_in_dim.7
  46.3 7.9 %all-to-all-start.1 = ((bf16[64,128,128]{2,1,0:T(8,128)(2,1)}), bf16[64,128,128]{2,1,0:T(8,128)(2,1)S(1)}, u32[]{:S(2)}, u32[]{:S(2)}) async-start(bf16[64,128,128]{2,1,0:T(8,128)(2,1)} %broadcast_in_dim.7), calls=%async_computation.1 | async-start | bytes 4194304 | tf_op jit(solution)/shard_map/all_to_all | solution.py:256
  54.2 1.7 constant_dynamic-update-slice_fusion.2
  55.9 1.7 constant_dynamic-update-slice_fusion.1
  57.6 0.7 constant_dynamic-update-slice_fusion.own_in
  58.3 23.1 %all-to-all-done.1.q_in = bf16[64,128,128]{2,1,0:T(8,128)(2,1)S(1)} async-done(((bf16[64,128,128]{2,1,0:T(8,128)(2,1)}), bf16[64,128,128]{2,1,0:T(8,128)(2,1)S(1)}, u32[]{:S(2)}, u32[]{:S(2)}) %all-to-all-start.1) | async-done | bytes 2097184 | tf_op jit(solution)/shard_map/all_to_all | solution.py:256
  81.4 2.0 broadcast_in_dim.8
  83.4 5.6 %all-to-all-start.3 = ((bf16[64,128,128]{2,1,0:T(8,128)(2,1)}), bf16[64,128,128]{2,1,0:T(8,128)(2,1)}, u32[]{:S(2)}, u32[]{:S(2)}) async-start(bf16[64,128,128]{2,1,0:T(8,128)(2,1)} %broadcast_in_dim.8), calls=%async_computation.3 | async-start | bytes 4194304 | tf_op jit(solution)/shard_map/all_to_all | solution.py:256
  89.0 0.6 copy.12
  89.6 12.6 %listing.1 = (s32[28720]{0:T(1024)}, s32[28720]{0:T(1024)}, s32[2]{0:T(128)}, s32[1792]{0:T(1024)}, s32[1792]{0:T(1024)}) custom-call(s32[64,256]{1,0:T(8,128)} %bitcast.46), custom_call_target="tpu_custom_call" | custom-call | flops 1000000000 | bytes 1048576 | tf_op jit(solution)/shard_map/listing/pallas_call | solution.py:317
  102.2 30.1 %chunk_0.1 = (bf16[64,128,128]{2,1,0:T(8,128)(2,1)}, f32[128,128,128]{2,1,0:T(8,128)}) custom-call(s32[28720]{0:T(1024)} %get-tuple-element.12.items, s32[2]{0:T(128)} %get-tuple-element.13.counts, s32[1792]{0:T(1024)} %get-tuple-element.14.base, s32[1792]{0:T(1024)} %get-tuple-element.15.hits, f32[64,8,128]{2,1,0:T(8,128)} %copy-done.3, ...), custom_call_target="tpu_custom_call" | custom-call | flops 20000000000 | bytes 33554432 | tf_op jit(solution)/shard_map/chunk_0/pallas_call | solution.py:346
  132.4 22.6 %all-to-all-start.2 = ((bf16[64,128,128]{2,1,0:T(8,128)(2,1)}), bf16[64,128,128]{2,1,0:T(8,128)(2,1)S(1)}, u32[]{:S(2)}, u32[]{:S(2)}) async-start(bf16[64,128,128]{2,1,0:T(8,128)(2,1)} %get-tuple-element.16), calls=%async_computation.2 | async-start | bytes 4194304 | tf_op jit(solution)/shard_map/all_to_all | solution.py:360
  155.0 32.5 %chunk_1.1 = (bf16[64,128,128]{2,1,0:T(8,128)(2,1)}, f32[64,128,128]{2,1,0:T(8,128)}, bf16[64,128,128]{2,1,0:T(8,128)(2,1)}) custom-call(s32[28720]{0:T(1024)} %get-tuple-element.17.items, s32[2]{0:T(128)} %get-tuple-element.13.counts, s32[1792]{0:T(1024)} %get-tuple-element.14.base, s32[1792]{0:T(1024)} %get-tuple-element.15.hits, f32[64,8,128]{2,1,0:T(8,128)} %copy-done.3, ...), custom_call_target="tpu_custom_call" | custom-call | flops 20000000000 | bytes 33554432 | tf_op jit(solution)/shard_map/chunk_1/pallas_call | solution.py:357
  187.6 1.3 copy-done
  189.0 19.7 %all-to-all-start.4 = ((bf16[64,128,128]{2,1,0:T(8,128)(2,1)}), bf16[64,128,128]{2,1,0:T(8,128)(2,1)S(1)}, u32[]{:S(2)}, u32[]{:S(2)}) async-start(bf16[64,128,128]{2,1,0:T(8,128)(2,1)} %get-tuple-element.19), calls=%async_computation.4 | async-start | bytes 4194304 | tf_op jit(solution)/shard_map/all_to_all | solution.py:360
  208.7 6.0 %fusion.3 = (bf16[64,128,128]{2,1,0:T(8,128)(2,1)S(1)}, f32[64,128,128]{2,1,0:T(8,128)}) fusion(f32[64,128,128]{2,1,0:T(8,128)} %get-tuple-element.20, bf16[64,128,128]{2,1,0:T(8,128)(2,1)} %collective-permute-done.7), kind=kLoop, calls=%fused_computation.33 | loop fusion | flops 3145728 | bytes 12582912 | tf_op jit(solution)/shard_map/convert.5
  214.8 1.6 collective-permute-start.13
  216.8 2.7 %collective-permute-start.12 = (bf16[8,128,128]{2,1,0:T(8,128)(2,1)S(1)}, bf16[8,128,128]{2,1,0:T(8,128)(2,1)}, u32[]{:S(2)}, u32[]{:S(2)}) collective-permute-start(bf16[8,128,128]{2,1,0:T(8,128)(2,1)S(1)} %get-tuple-element.27), channel_id=1, source_target_pairs={{4,0},{8,4},{12,8},{0,12},{5,1},{9,5},{13,9},{1,13},{6,2},{10,6},{... | collective-permute-start | bytes 786440 | tf_op jit(solution)/shard_map/ppermute | solution.py:366
  219.4 1.5 collective-permute-start.11
  221.0 1.7 collective-permute-start.10
  222.7 1.5 collective-permute-start.9
  224.1 17.3 %collective-permute-done.13.rest_5_ = bf16[8,128,128]{2,1,0:T(8,128)(2,1)S(1)} collective-permute-done((bf16[8,128,128]{2,1,0:T(8,128)(2,1)S(1)}, bf16[8,128,128]{2,1,0:T(8,128)(2,1)S(1)}, u32[]{:S(2)}, u32[]{:S(2)}) %collective-permute-start.13) | collective-permute-done | bytes 262176 | tf_op jit(solution)/shard_map/ppermute | solution.py:366
  241.5 0.7 copy-done.4
  242.2 2.6 %collective-permute-start.8 = (bf16[8,128,128]{2,1,0:T(8,128)(2,1)S(1)}, bf16[8,128,128]{2,1,0:T(8,128)(2,1)}, u32[]{:S(2)}, u32[]{:S(2)}) collective-permute-start(bf16[8,128,128]{2,1,0:T(8,128)(2,1)S(1)} %get-tuple-element.31), channel_id=1, source_target_pairs={{1,0},{2,1},{3,2},{0,3},{5,4},{6,5},{7,6},{4,7},{9,8},{10,9},{11,1... | collective-permute-start | bytes 786440 | tf_op jit(solution)/shard_map/ppermute | solution.py:366
  245.1 0.7 pad_maximum_fusion.1
  245.8 2.3 slice.103.kept
  248.1 2.6 %collective-permute-done.8.rest_0_ = bf16[8,128,128]{2,1,0:T(8,128)(2,1)} collective-permute-done((bf16[8,128,128]{2,1,0:T(8,128)(2,1)S(1)}, bf16[8,128,128]{2,1,0:T(8,128)(2,1)}, u32[]{:S(2)}, u32[]{:S(2)}) %collective-permute-start.8) | collective-permute-done | bytes 262176 | tf_op jit(solution)/shard_map/ppermute | solution.py:366
  250.7 3.9 %assemble.1 = f32[64,128,128]{2,1,0:T(8,128)} custom-call(f32[16,128,128]{2,1,0:T(8,128)} %slice.103.kept, bf16[8,128,128]{2,1,0:T(8,128)(2,1)} %collective-permute-done.8.rest_0_, bf16[8,128,128]{2,1,0:T(8,128)(2,1)} %collective-permute-done.9.rest_1_, bf16[8,128,128]{2,1,0:T(8,128)(2,1)} %collective-permute-done.10.rest_2_, ...), custom_call_target="tpu_custom_call" | custom-call | flops 1000000 | bytes 8388608 | tf_op jit(solution)/shard_map/assemble/pallas_call | solution.py:378
  (41 shorter events, 1.0 us)
Async XLA Ops:
  12.1 22.3 %copy-start.5 = (bf16[256,128]{1,0:T(8,128)(2,1)S(1)}, bf16[256,128]{1,0:T(8,128)(2,1)}, u32[]{:S(2)}) copy-start(bf16[256,128]{1,0:T(8,128)(2,1)} %param.8) | copy-start | bytes 196612
  12.9 31.6 %all-to-all-start = ((f32[64,8,128]{2,1,0:T(8,128)}), f32[64,8,128]{2,1,0:T(8,128)S(1)}, u32[]{:S(2)}, u32[]{:S(2)}) async-start(f32[64,8,128]{2,1,0:T(8,128)} %pad_maximum_fusion), calls=%async_computation | async-start | bytes 524288 | tf_op jit(solution)/shard_map/all_to_all | solution.py:303
  24.4 10.1 %slice-start = ((bf16[8192,128]{1,0:T(8,128)(2,1)}), bf16[2048,128]{1,0:T(8,128)(2,1)S(1)}, s32[]{:S(2)}) async-start(bf16[8192,128]{1,0:T(8,128)(2,1)} %param.9), calls=%async_computation.5 | async-start | bytes 1048576 | tf_op jit(solution)/shard_map/slice | solution.py:264
  25.9 28.3 %collective-permute-start.3 = (bf16[8,128,128]{2,1,0:T(8,128)(2,1)S(1)}, bf16[8,128,128]{2,1,0:T(8,128)(2,1)}, u32[]{:S(2)}, u32[]{:S(2)}) collective-permute-start(bf16[8,128,128]{2,1,0:T(8,128)(2,1)S(1)} %bitcast.41), channel_id=1, source_target_pairs={{0,96},{32,0},{64,32},{96,64},{1,97},{33,1},{65,33},{97,65},{2,98}... | collective-permute-start | bytes 786440 | tf_op jit(solution)/shard_map/ppermute | solution.py:263
  29.0 28.6 %collective-permute-start.5 = (bf16[8,128,128]{2,1,0:T(8,128)(2,1)S(1)}, bf16[8,128,128]{2,1,0:T(8,128)(2,1)S(1)}, u32[]{:S(2)}, u32[]{:S(2)}) collective-permute-start(bf16[8,128,128]{2,1,0:T(8,128)(2,1)S(1)} %bitcast.39), channel_id=1, source_target_pairs={{0,12},{4,0},{8,4},{12,8},{1,13},{5,1},{9,5},{13,9},{2,14},{6,2},{... | collective-permute-start | bytes 786440 | tf_op jit(solution)/shard_map/ppermute | solution.py:263
  31.7 12.0 %collective-permute-start.2 = (bf16[8,128,128]{2,1,0:T(8,128)(2,1)S(1)}, bf16[8,128,128]{2,1,0:T(8,128)(2,1)S(1)}, u32[]{:S(2)}, u32[]{:S(2)}) collective-permute-start(bf16[8,128,128]{2,1,0:T(8,128)(2,1)S(1)} %bitcast.42), channel_id=1, source_target_pairs={{0,32},{32,64},{64,96},{96,0},{1,33},{33,65},{65,97},{97,1},{2,34}... | collective-permute-start | bytes 786440 | tf_op jit(solution)/shard_map/ppermute | solution.py:263
  31.7 11.3 %collective-permute-start.1 = (bf16[8,128,128]{2,1,0:T(8,128)(2,1)S(1)}, bf16[8,128,128]{2,1,0:T(8,128)(2,1)S(1)}, u32[]{:S(2)}, u32[]{:S(2)}) collective-permute-start(bf16[8,128,128]{2,1,0:T(8,128)(2,1)S(1)} %bitcast.43), channel_id=1, source_target_pairs={{0,3},{1,0},{2,1},{3,2},{4,7},{5,4},{6,5},{7,6},{8,11},{9,8},{10,9... | collective-permute-start | bytes 786440 | tf_op jit(solution)/shard_map/ppermute | solution.py:263
  34.4 7.9 %collective-permute-start = (bf16[8,128,128]{2,1,0:T(8,128)(2,1)S(1)}, bf16[8,128,128]{2,1,0:T(8,128)(2,1)S(1)}, u32[]{:S(2)}, u32[]{:S(2)}) collective-permute-start(bf16[8,128,128]{2,1,0:T(8,128)(2,1)S(1)} %bitcast.44), channel_id=1, source_target_pairs={{0,1},{1,2},{2,3},{3,0},{4,5},{5,6},{6,7},{7,4},{8,9},{9,10},{10,1... | collective-permute-start | bytes 786440 | tf_op jit(solution)/shard_map/ppermute | solution.py:263
  42.3 13.6 %collective-permute-start.4 = (bf16[8,128,128]{2,1,0:T(8,128)(2,1)S(1)}, bf16[8,128,128]{2,1,0:T(8,128)(2,1)}, u32[]{:S(2)}, u32[]{:S(2)}) collective-permute-start(bf16[8,128,128]{2,1,0:T(8,128)(2,1)S(1)} %bitcast.40), channel_id=1, source_target_pairs={{0,4},{4,8},{8,12},{12,0},{1,5},{5,9},{9,13},{13,1},{2,6},{6,10},{... | collective-permute-start | bytes 786440 | tf_op jit(solution)/shard_map/ppermute | solution.py:263
  44.5 44.5 %copy-start.3 = (f32[64,8,128]{2,1,0:T(8,128)}, f32[64,8,128]{2,1,0:T(8,128)S(1)}, u32[]{:S(2)}) copy-start(f32[64,8,128]{2,1,0:T(8,128)S(1)} %all-to-all-done.rows_in) | copy-start | bytes 786436
  46.3 35.1 %all-to-all-start.1 = ((bf16[64,128,128]{2,1,0:T(8,128)(2,1)}), bf16[64,128,128]{2,1,0:T(8,128)(2,1)S(1)}, u32[]{:S(2)}, u32[]{:S(2)}) async-start(bf16[64,128,128]{2,1,0:T(8,128)(2,1)} %broadcast_in_dim.7), calls=%async_computation.1 | async-start | bytes 4194304 | tf_op jit(solution)/shard_map/all_to_all | solution.py:256
  58.3 43.9 %collective-permute-start.6 = (bf16[64,128,128]{2,1,0:T(8,128)(2,1)}, bf16[64,128,128]{2,1,0:T(8,128)(2,1)}, u32[]{:S(2)}, u32[]{:S(2)}) collective-permute-start(bf16[64,128,128]{2,1,0:T(8,128)(2,1)} %constant_dynamic-update-slice_fusion.own_in), channel_id=1, source_target_pairs={{0,16},{16,0},{1,17},{17,1},{2,18},{18,2},{3,19},{19,3},{4,20},{20... | collective-permute-start | bytes 6291464 | tf_op jit(solution)/shard_map/ppermute | solution.py:265
  81.4 2.0 copy-start.2
  83.4 49.0 %all-to-all-start.3 = ((bf16[64,128,128]{2,1,0:T(8,128)(2,1)}), bf16[64,128,128]{2,1,0:T(8,128)(2,1)}, u32[]{:S(2)}, u32[]{:S(2)}) async-start(bf16[64,128,128]{2,1,0:T(8,128)(2,1)} %broadcast_in_dim.8), calls=%async_computation.3 | async-start | bytes 4194304 | tf_op jit(solution)/shard_map/all_to_all | solution.py:256
  132.4 55.3 %all-to-all-start.2 = ((bf16[64,128,128]{2,1,0:T(8,128)(2,1)}), bf16[64,128,128]{2,1,0:T(8,128)(2,1)S(1)}, u32[]{:S(2)}, u32[]{:S(2)}) async-start(bf16[64,128,128]{2,1,0:T(8,128)(2,1)} %get-tuple-element.16), calls=%async_computation.2 | async-start | bytes 4194304 | tf_op jit(solution)/shard_map/all_to_all | solution.py:360
  187.5 21.2 %collective-permute-start.7 = (bf16[64,128,128]{2,1,0:T(8,128)(2,1)}, bf16[64,128,128]{2,1,0:T(8,128)(2,1)}, u32[]{:S(2)}, u32[]{:S(2)}) collective-permute-start(bf16[64,128,128]{2,1,0:T(8,128)(2,1)} %get-tuple-element.21), channel_id=1, source_target_pairs={{0,16},{16,0},{1,17},{17,1},{2,18},{18,2},{3,19},{19,3},{4,20},{20... | collective-permute-start | bytes 6291464 | tf_op jit(solution)/shard_map/ppermute | solution.py:363
  187.6 1.3 copy-start
  189.0 55.9 %all-to-all-start.4 = ((bf16[64,128,128]{2,1,0:T(8,128)(2,1)}), bf16[64,128,128]{2,1,0:T(8,128)(2,1)S(1)}, u32[]{:S(2)}, u32[]{:S(2)}) async-start(bf16[64,128,128]{2,1,0:T(8,128)(2,1)} %get-tuple-element.19), calls=%async_computation.4 | async-start | bytes 4194304 | tf_op jit(solution)/shard_map/all_to_all | solution.py:360
  214.7 1.8 copy-start.1
  214.8 26.7 %collective-permute-start.13 = (bf16[8,128,128]{2,1,0:T(8,128)(2,1)S(1)}, bf16[8,128,128]{2,1,0:T(8,128)(2,1)S(1)}, u32[]{:S(2)}, u32[]{:S(2)}) collective-permute-start(bf16[8,128,128]{2,1,0:T(8,128)(2,1)S(1)} %get-tuple-element.26), channel_id=1, source_target_pairs={{12,0},{0,4},{4,8},{8,12},{13,1},{1,5},{5,9},{9,13},{14,2},{2,6},{... | collective-permute-start | bytes 786440 | tf_op jit(solution)/shard_map/ppermute | solution.py:366
  216.8 31.4 %collective-permute-start.12 = (bf16[8,128,128]{2,1,0:T(8,128)(2,1)S(1)}, bf16[8,128,128]{2,1,0:T(8,128)(2,1)}, u32[]{:S(2)}, u32[]{:S(2)}) collective-permute-start(bf16[8,128,128]{2,1,0:T(8,128)(2,1)S(1)} %get-tuple-element.27), channel_id=1, source_target_pairs={{4,0},{8,4},{12,8},{0,12},{5,1},{9,5},{13,9},{1,13},{6,2},{10,6},{... | collective-permute-start | bytes 786440 | tf_op jit(solution)/shard_map/ppermute | solution.py:366
  219.4 28.7 %collective-permute-start.11 = (bf16[8,128,128]{2,1,0:T(8,128)(2,1)S(1)}, bf16[8,128,128]{2,1,0:T(8,128)(2,1)}, u32[]{:S(2)}, u32[]{:S(2)}) collective-permute-start(bf16[8,128,128]{2,1,0:T(8,128)(2,1)S(1)} %get-tuple-element.28), channel_id=1, source_target_pairs={{96,0},{0,32},{32,64},{64,96},{97,1},{1,33},{33,65},{65,97},{98,2}... | collective-permute-start | bytes 786440 | tf_op jit(solution)/shard_map/ppermute | solution.py:366
  221.0 27.1 %collective-permute-start.10 = (bf16[8,128,128]{2,1,0:T(8,128)(2,1)S(1)}, bf16[8,128,128]{2,1,0:T(8,128)(2,1)}, u32[]{:S(2)}, u32[]{:S(2)}) collective-permute-start(bf16[8,128,128]{2,1,0:T(8,128)(2,1)S(1)} %get-tuple-element.29), channel_id=1, source_target_pairs={{32,0},{64,32},{96,64},{0,96},{33,1},{65,33},{97,65},{1,97},{34,2}... | collective-permute-start | bytes 786440 | tf_op jit(solution)/shard_map/ppermute | solution.py:366
  222.7 25.4 %collective-permute-start.9 = (bf16[8,128,128]{2,1,0:T(8,128)(2,1)S(1)}, bf16[8,128,128]{2,1,0:T(8,128)(2,1)}, u32[]{:S(2)}, u32[]{:S(2)}) collective-permute-start(bf16[8,128,128]{2,1,0:T(8,128)(2,1)S(1)} %get-tuple-element.30), channel_id=1, source_target_pairs={{3,0},{0,1},{1,2},{2,3},{7,4},{4,5},{5,6},{6,7},{11,8},{8,9},{9,10... | collective-permute-start | bytes 786440 | tf_op jit(solution)/shard_map/ppermute | solution.py:366
  241.5 0.7 copy-start.4
  242.2 8.6 %collective-permute-start.8 = (bf16[8,128,128]{2,1,0:T(8,128)(2,1)S(1)}, bf16[8,128,128]{2,1,0:T(8,128)(2,1)}, u32[]{:S(2)}, u32[]{:S(2)}) collective-permute-start(bf16[8,128,128]{2,1,0:T(8,128)(2,1)S(1)} %get-tuple-element.31), channel_id=1, source_target_pairs={{1,0},{2,1},{3,2},{0,3},{5,4},{6,5},{7,6},{4,7},{9,8},{10,9},{11,1... | collective-permute-start | bytes 786440 | tf_op jit(solution)/shard_map/ppermute | solution.py:366

commit v3 on v2

--- a/solution.py
+++ b/solution.py
@@ -231,6 +231,16 @@
         lax.fori_loop(0, here, deliver, 0, unroll=2)
 
 
+def hold_kernel(counts, kept, *rest):
+    *lent, out = rest
+
+    @pl.when(counts[0] >= 0)
+    def _():
+        out[pl.ds(0, KEPT)] = kept[...]
+        for k, part in enumerate(lent):
+            out[pl.ds(KEPT + SLAB * k, SLAB)] = part[...]
+
+
 def assemble_kernel(kept, *rest):
     *back, out = rest
     out[pl.ds(0, KEPT)] = kept[...]
@@ -261,9 +271,7 @@
         ways.append((axis, [(i, (i + shift) % size) for i in range(size)]))
     slabs = [slice(KEPT + SLAB * k, KEPT + SLAB * (k + 1)) for k in range(len(STEPS))]
     lent = [lax.ppermute(stored[at], axis, way) for at, (axis, way) in zip(slabs, ways)]
-    held = jnp.concatenate([stored[:KEPT]] + lent)
-    mate_held = lax.ppermute(held, "c", [(0, 1), (1, 0)])
-
+    kept = stored[:KEPT]
     smem = pl.BlockSpec(memory_space=pltpu.SMEM)
     vmem = pl.BlockSpec(memory_space=pltpu.VMEM)
     limit = pltpu.CompilerParams(vmem_limit_bytes=VMEM_LIMIT)
@@ -315,6 +323,17 @@
         name="listing",
     )
     *items, counts, base, hits = listing(table)
+    hold = pl.pallas_call(
+        hold_kernel,
+        out_shape=jax.ShapeDtypeStruct(stored.shape, stored.dtype),
+        in_specs=[smem] + [vmem] * (1 + len(lent)),
+        out_specs=vmem,
+        compiler_params=limit,
+        cost_estimate=pl.CostEstimate(flops=10**6, bytes_accessed=2**22, transcendentals=0),
+        name="hold",
+    )
+    held = hold(counts, kept, *lent)
+    mate_held = lax.ppermute(held, "c", [(0, 1), (1, 0)])
 
     acc_shape = jax.ShapeDtypeStruct((2 * blocks_here, BLOCK, feat_width), jnp.float32)
     grad_shape = jax.ShapeDtypeStruct((sources, QTILE, feat_width), jnp.bfloat16)

time: 257 us -> 234 us (0.911)
  waiting for transfers between devices: 50 us -> 34.4 us
  local copies, waits for them, and re-layouts: 17.5 us -> 13.1 us
  starting transfers between devices: 87.6 us -> 83.6 us
  Pallas kernels: 84 us -> 87 us
    all_to_all x2, waiting for transfers between devices: 23.1 us -> 11.8 us  [shard_work(): halves.append(lax.all_to_all(spread, SAME_CORE, 0, 0, tiled=True))]
    ppermute x6, waiting for transfers between devices: 7.01 us -> 0.02 us  [shard_work(): lax.ppermute(stored[at], axis, way)]
    unnamed x19, local copies, waits for them, and re-layouts: 8.98 us -> 2.67 us
    all_to_all x2, starting transfers between devices: 42.4 us -> 39 us  [shard_work(): came = lax.all_to_all(part, SAME_CORE, 0, 0, tiled=True)]
    pallas_call x0 -> x1, Pallas kernels: none -> 3.01 us  [shard_work(): held = hold(counts, kept, *lent)]
    all_to_all x1, waiting for transfers between devices: 0.01 us -> 2.6 us  [shard_work(): rows = lax.all_to_all(packed, SAME_CORE, 0, 0, tiled=True)]
  transfers between devices with their start and end apart: 19 -> 19, of which waited for: 4 -> 4; matrix products, arithmetic and copies ran while one was open for 9% -> 9% of each run, Pallas kernels for 30% -> 36%
where the time goes in v3:
time: 234 us; the launch traced here: 232 us
  Pallas kernels  87 us (37%)
  starting transfers between devices  83.6 us (36%)
  waiting for transfers between devices  34.4 us (15%)
  local copies, waits for them, and re-layouts  13.1 us (6%)
  other arithmetic  12.5 us (5%)
    all_to_all x2, starting transfers between devices, shard_work(): came = lax.all_to_all(part, SAME_CORE, 0, 0, tiled=True)  39 us
    pallas_call x1, Pallas kernels, shard_work(): chunk_1(items[1], counts, base, hits, rows, halves[1], held, mate_held, acc)  32.5 us
    pallas_call x1, Pallas kernels, shard_work(): chunk_0(items[0], counts, base, hits, rows, halves[0], held, mate_held)  30.1 us
    ppermute x6, waiting for transfers between devices, shard_work(): lax.ppermute(held_grad[at].astype(jnp.bfloat16), axis, [(j, i) for i, j i...  19.9 us
    all_to_all x2, starting transfers between devices, shard_work(): halves.append(lax.all_to_all(spread, SAME_CORE, 0, 0, tiled=True))  13.5 us
    pallas_call x1, Pallas kernels, shard_work(): *items, counts, base, hits = listing(table)  12.6 us
    all_to_all x2, waiting for transfers between devices, shard_work(): halves.append(lax.all_to_all(spread, SAME_CORE, 0, 0, tiled=True))  11.8 us
    ppermute x6, starting transfers between devices, shard_work(): lax.ppermute(held_grad[at].astype(jnp.bfloat16), axis, [(j, i) for i, j i...  11.7 us
  transfers between devices with their start and end apart: 19, of which 4 were waited for; matrix products, arithmetic and copies ran while one was open for 9% of the time, Pallas kernels for 36%

profile of v3, /device:TPU:0, one launch (start us, length us, event | category | flops | bytes accessed | tf_op | source)
XLA Modules:
  0.0 231.6 jit_solution(14935214730950470286)
XLA Ops:
  0.6 2.3 fusion.5
  2.9 3.1 %collective-permute-start.3 = (bf16[8,128,128]{2,1,0:T(8,128)(2,1)S(1)}, bf16[8,128,128]{2,1,0:T(8,128)(2,1)S(1)}, u32[]{:S(2)}, u32[]{:S(2)}) collective-permute-start(bf16[8,128,128]{2,1,0:T(8,128)(2,1)S(1)} %bitcast.42), channel_id=1, source_target_pairs={{0,96},{32,0},{64,32},{96,64},{1,97},{33,1},{65,33},{97,65},{2,98}... | collective-permute-start | bytes 786440 | tf_op jit(solution)/shard_map/ppermute | solution.py:273
  6.1 0.1 convert_bitcast_fusion
  6.2 0.8 compare_reduce_fusion
  7.0 0.7 compare_reduce_fusion.1
  7.7 0.6 pad_add_fusion.where
  8.3 0.6 shift-left_reduce_fusion
  8.9 4.8 %ask.1 = s32[64,256]{1,0:T(8,128)} custom-call(s32[2]{0:T(128)} %pad_add_fusion.where, s32[64]{0:T(128)} %bitcast.45, s32[64]{0:T(128)} %local.1, s32[64]{0:T(128)} %get-tuple-element.23.hits, s32[64]{0:T(128)} %get-tuple-element.22.lives), custom_call_target="tpu_custom_call" | custom-call | flops 1000000 | bytes 65536 | tf_op jit(solution)/shard_map/ask/pallas_call | solution.py:294
  13.7 0.8 convert_element_type.33
  14.6 0.8 subtract_bitcast_fusion
  15.4 0.8 pad_maximum_fusion
  16.2 9.0 %all-to-all-start = ((f32[64,8,128]{2,1,0:T(8,128)}), f32[64,8,128]{2,1,0:T(8,128)S(1)}, u32[]{:S(2)}, u32[]{:S(2)}) async-start(f32[64,8,128]{2,1,0:T(8,128)} %pad_maximum_fusion), calls=%async_computation | async-start | bytes 524288 | tf_op jit(solution)/shard_map/all_to_all | solution.py:311
  25.1 2.9 %collective-permute-start.5 = (bf16[8,128,128]{2,1,0:T(8,128)(2,1)}, bf16[8,128,128]{2,1,0:T(8,128)(2,1)}, u32[]{:S(2)}, u32[]{:S(2)}) collective-permute-start(bf16[8,128,128]{2,1,0:T(8,128)(2,1)} %bitcast.13), channel_id=1, source_target_pairs={{0,12},{4,0},{8,4},{12,8},{1,13},{5,1},{9,5},{13,9},{2,14},{6,2},{... | collective-permute-start | bytes 786440 | tf_op jit(solution)/shard_map/ppermute | solution.py:273
  28.0 1.5 collective-permute-start.2
  29.5 2.7 %collective-permute-start.1 = (bf16[8,128,128]{2,1,0:T(8,128)(2,1)S(1)}, bf16[8,128,128]{2,1,0:T(8,128)(2,1)}, u32[]{:S(2)}, u32[]{:S(2)}) collective-permute-start(bf16[8,128,128]{2,1,0:T(8,128)(2,1)S(1)} %bitcast.41), channel_id=1, source_target_pairs={{0,3},{1,0},{2,1},{3,2},{4,7},{5,4},{6,5},{7,6},{8,11},{9,8},{10,9... | collective-permute-start | bytes 786440 | tf_op jit(solution)/shard_map/ppermute | solution.py:273
  32.2 1.9 slice.80
  34.1 0.1 collective-permute-start.4
  34.2 2.6 %all-to-all-done.rows_in = f32[64,8,128]{2,1,0:T(8,128)S(1)} async-done(((f32[64,8,128]{2,1,0:T(8,128)}), f32[64,8,128]{2,1,0:T(8,128)S(1)}, u32[]{:S(2)}, u32[]{:S(2)}) %all-to-all-start) | async-done | bytes 262176 | tf_op jit(solution)/shard_map/all_to_all | solution.py:311
  36.8 1.8 broadcast_in_dim.7
  38.7 7.9 %all-to-all-start.1 = ((bf16[64,128,128]{2,1,0:T(8,128)(2,1)}), bf16[64,128,128]{2,1,0:T(8,128)(2,1)S(1)}, u32[]{:S(2)}, u32[]{:S(2)}) async-start(bf16[64,128,128]{2,1,0:T(8,128)(2,1)} %broadcast_in_dim.7), calls=%async_computation.1 | async-start | bytes 4194304 | tf_op jit(solution)/shard_map/all_to_all | solution.py:266
  46.6 0.6 copy.12
  47.3 12.6 %listing.1 = (s32[28720]{0:T(1024)}, s32[28720]{0:T(1024)}, s32[2]{0:T(128)}, s32[1792]{0:T(1024)}, s32[1792]{0:T(1024)}) custom-call(s32[64,256]{1,0:T(8,128)} %bitcast.44), custom_call_target="tpu_custom_call" | custom-call | flops 1000000000 | bytes 1048576 | tf_op jit(solution)/shard_map/listing/pallas_call | solution.py:325
  59.9 3.0 %hold.1.own_in = bf16[64,128,128]{2,1,0:T(8,128)(2,1)} custom-call(s32[2]{0:T(128)} %get-tuple-element.13.counts, bf16[16,128,128]{2,1,0:T(8,128)(2,1)} %bitcast.38, bf16[8,128,128]{2,1,0:T(8,128)(2,1)} %collective-permute-done.rest_0_, bf16[8,128,128]{2,1,0:T(8,128)(2,1)} %collective-permute-done.1.rest_1_, ...), custom_call_target="tpu_custom_call" | custom-call | flops 1000000 | bytes 4194304 | tf_op jit(solution)/shard_map/hold/pallas_call | solution.py:335
  62.9 11.8 %all-to-all-done.1.q_in = bf16[64,128,128]{2,1,0:T(8,128)(2,1)S(1)} async-done(((bf16[64,128,128]{2,1,0:T(8,128)(2,1)}), bf16[64,128,128]{2,1,0:T(8,128)(2,1)S(1)}, u32[]{:S(2)}, u32[]{:S(2)}) %all-to-all-start.1) | async-done | bytes 2097184 | tf_op jit(solution)/shard_map/all_to_all | solution.py:266
  74.8 2.0 broadcast_in_dim.8
  76.8 5.6 %all-to-all-start.3 = ((bf16[64,128,128]{2,1,0:T(8,128)(2,1)}), bf16[64,128,128]{2,1,0:T(8,128)(2,1)}, u32[]{:S(2)}, u32[]{:S(2)}) async-start(bf16[64,128,128]{2,1,0:T(8,128)(2,1)} %broadcast_in_dim.8), calls=%async_computation.3 | async-start | bytes 4194304 | tf_op jit(solution)/shard_map/all_to_all | solution.py:266
  82.4 30.1 %chunk_0.1 = (bf16[64,128,128]{2,1,0:T(8,128)(2,1)}, f32[128,128,128]{2,1,0:T(8,128)}) custom-call(s32[28720]{0:T(1024)} %get-tuple-element.12.items, s32[2]{0:T(128)} %get-tuple-element.13.counts, s32[1792]{0:T(1024)} %get-tuple-element.14.base, s32[1792]{0:T(1024)} %get-tuple-element.15.hits, f32[64,8,128]{2,1,0:T(8,128)} %copy-done.3, ...), custom_call_target="tpu_custom_call" | custom-call | flops 20000000000 | bytes 33554432 | tf_op jit(solution)/shard_map/chunk_0/pallas_call | solution.py:365
  112.5 19.4 %all-to-all-start.2 = ((bf16[64,128,128]{2,1,0:T(8,128)(2,1)}), bf16[64,128,128]{2,1,0:T(8,128)(2,1)S(1)}, u32[]{:S(2)}, u32[]{:S(2)}) async-start(bf16[64,128,128]{2,1,0:T(8,128)(2,1)} %get-tuple-element.16), calls=%async_computation.2 | async-start | bytes 4194304 | tf_op jit(solution)/shard_map/all_to_all | solution.py:379
  131.9 32.5 %chunk_1.1 = (bf16[64,128,128]{2,1,0:T(8,128)(2,1)}, f32[64,128,128]{2,1,0:T(8,128)}, bf16[64,128,128]{2,1,0:T(8,128)(2,1)}) custom-call(s32[28720]{0:T(1024)} %get-tuple-element.17.items, s32[2]{0:T(128)} %get-tuple-element.13.counts, s32[1792]{0:T(1024)} %get-tuple-element.14.base, s32[1792]{0:T(1024)} %get-tuple-element.15.hits, f32[64,8,128]{2,1,0:T(8,128)} %copy-done.3, ...), custom_call_target="tpu_custom_call" | custom-call | flops 20000000000 | bytes 33554432 | tf_op jit(solution)/shard_map/chunk_1/pallas_call | solution.py:376
  164.5 0.3 collective-permute-start.7
  164.8 1.3 copy-done
  166.1 19.6 %all-to-all-start.4 = ((bf16[64,128,128]{2,1,0:T(8,128)(2,1)}), bf16[64,128,128]{2,1,0:T(8,128)(2,1)S(1)}, u32[]{:S(2)}, u32[]{:S(2)}) async-start(bf16[64,128,128]{2,1,0:T(8,128)(2,1)} %get-tuple-element.19), calls=%async_computation.4 | async-start | bytes 4194304 | tf_op jit(solution)/shard_map/all_to_all | solution.py:379
  185.7 6.0 %fusion.3 = (bf16[64,128,128]{2,1,0:T(8,128)(2,1)S(1)}, f32[64,128,128]{2,1,0:T(8,128)}) fusion(f32[64,128,128]{2,1,0:T(8,128)} %get-tuple-element.20, bf16[64,128,128]{2,1,0:T(8,128)(2,1)} %collective-permute-done.7), kind=kLoop, calls=%fused_computation.26 | loop fusion | flops 3145728 | bytes 12582912 | tf_op jit(solution)/shard_map/convert.5
  191.6 0.1 fusion.4
  191.7 1.6 collective-permute-start.13
  193.4 0.3 convert_reduce_fusion.1
  193.7 2.7 %collective-permute-start.12 = (bf16[8,128,128]{2,1,0:T(8,128)(2,1)S(1)}, bf16[8,128,128]{2,1,0:T(8,128)(2,1)}, u32[]{:S(2)}, u32[]{:S(2)}) collective-permute-start(bf16[8,128,128]{2,1,0:T(8,128)(2,1)S(1)} %get-tuple-element.27), channel_id=1, source_target_pairs={{4,0},{8,4},{12,8},{0,12},{5,1},{9,5},{13,9},{1,13},{6,2},{10,6},{... | collective-permute-start | bytes 786440 | tf_op jit(solution)/shard_map/ppermute | solution.py:385
  196.4 1.5 collective-permute-start.11
  197.9 1.7 collective-permute-start.10
  199.6 1.5 collective-permute-start.9
  201.1 17.3 %collective-permute-done.13.rest_5_ = bf16[8,128,128]{2,1,0:T(8,128)(2,1)S(1)} collective-permute-done((bf16[8,128,128]{2,1,0:T(8,128)(2,1)S(1)}, bf16[8,128,128]{2,1,0:T(8,128)(2,1)S(1)}, u32[]{:S(2)}, u32[]{:S(2)}) %collective-permute-start.13) | collective-permute-done | bytes 262176 | tf_op jit(solution)/shard_map/ppermute | solution.py:385
  218.4 0.7 copy-done.5
  219.1 2.6 %collective-permute-start.8 = (bf16[8,128,128]{2,1,0:T(8,128)(2,1)S(1)}, bf16[8,128,128]{2,1,0:T(8,128)(2,1)}, u32[]{:S(2)}, u32[]{:S(2)}) collective-permute-start(bf16[8,128,128]{2,1,0:T(8,128)(2,1)S(1)} %get-tuple-element.31), channel_id=1, source_target_pairs={{1,0},{2,1},{3,2},{0,3},{5,4},{6,5},{7,6},{4,7},{9,8},{10,9},{11,1... | collective-permute-start | bytes 786440 | tf_op jit(solution)/shard_map/ppermute | solution.py:385
  221.8 0.3 convert_reduce_fusion
  222.1 0.7 pad_maximum_fusion.1
  222.7 2.3 slice.103.kept
  225.1 2.6 %collective-permute-done.8.rest_0_ = bf16[8,128,128]{2,1,0:T(8,128)(2,1)} collective-permute-done((bf16[8,128,128]{2,1,0:T(8,128)(2,1)S(1)}, bf16[8,128,128]{2,1,0:T(8,128)(2,1)}, u32[]{:S(2)}, u32[]{:S(2)}) %collective-permute-start.8) | collective-permute-done | bytes 262176 | tf_op jit(solution)/shard_map/ppermute | solution.py:385
  227.7 3.9 %assemble.1 = f32[64,128,128]{2,1,0:T(8,128)} custom-call(f32[16,128,128]{2,1,0:T(8,128)} %slice.103.kept, bf16[8,128,128]{2,1,0:T(8,128)(2,1)} %collective-permute-done.8.rest_0_, bf16[8,128,128]{2,1,0:T(8,128)(2,1)} %collective-permute-done.9.rest_1_, bf16[8,128,128]{2,1,0:T(8,128)(2,1)} %collective-permute-done.10.rest_2_, ...), custom_call_target="tpu_custom_call" | custom-call | flops 1000000 | bytes 8388608 | tf_op jit(solution)/shard_map/assemble/pallas_call | solution.py:397
  (40 shorter events, 0.2 us)
Async XLA Ops:
  0.6 5.4 %copy-start.8 = (s32[4096]{0:T(1024)S(1)}, s32[4096]{0:T(1024)}, u32[]{:S(2)}) copy-start(s32[4096]{0:T(1024)} %param.12) | copy-start | bytes 49156
  0.6 5.5 %copy-start.6 = (s32[32,512]{1,0:T(8,128)S(1)}, s32[32,512]{1,0:T(8,128)}, u32[]{:S(2)}) copy-start(s32[32,512]{1,0:T(8,128)} %param.13) | copy-start | bytes 196612
  2.9 31.2 %copy-start.7 = (bf16[256,128]{1,0:T(8,128)(2,1)S(1)}, bf16[256,128]{1,0:T(8,128)(2,1)}, u32[]{:S(2)}) copy-start(bf16[256,128]{1,0:T(8,128)(2,1)} %param.8) | copy-start | bytes 196612
  2.9 31.2 %collective-permute-start.3 = (bf16[8,128,128]{2,1,0:T(8,128)(2,1)S(1)}, bf16[8,128,128]{2,1,0:T(8,128)(2,1)S(1)}, u32[]{:S(2)}, u32[]{:S(2)}) collective-permute-start(bf16[8,128,128]{2,1,0:T(8,128)(2,1)S(1)} %bitcast.42), channel_id=1, source_target_pairs={{0,96},{32,0},{64,32},{96,64},{1,97},{33,1},{65,33},{97,65},{2,98}... | collective-permute-start | bytes 786440 | tf_op jit(solution)/shard_map/ppermute | solution.py:273
  16.2 20.7 %all-to-all-start = ((f32[64,8,128]{2,1,0:T(8,128)}), f32[64,8,128]{2,1,0:T(8,128)S(1)}, u32[]{:S(2)}, u32[]{:S(2)}) async-start(f32[64,8,128]{2,1,0:T(8,128)} %pad_maximum_fusion), calls=%async_computation | async-start | bytes 524288 | tf_op jit(solution)/shard_map/all_to_all | solution.py:311
  25.1 34.7 %collective-permute-start.5 = (bf16[8,128,128]{2,1,0:T(8,128)(2,1)}, bf16[8,128,128]{2,1,0:T(8,128)(2,1)}, u32[]{:S(2)}, u32[]{:S(2)}) collective-permute-start(bf16[8,128,128]{2,1,0:T(8,128)(2,1)} %bitcast.13), channel_id=1, source_target_pairs={{0,12},{4,0},{8,4},{12,8},{1,13},{5,1},{9,5},{13,9},{2,14},{6,2},{... | collective-permute-start | bytes 786440 | tf_op jit(solution)/shard_map/ppermute | solution.py:273
  28.0 31.9 %collective-permute-start.2 = (bf16[8,128,128]{2,1,0:T(8,128)(2,1)}, bf16[8,128,128]{2,1,0:T(8,128)(2,1)}, u32[]{:S(2)}, u32[]{:S(2)}) collective-permute-start(bf16[8,128,128]{2,1,0:T(8,128)(2,1)} %bitcast.10), channel_id=1, source_target_pairs={{0,32},{32,64},{64,96},{96,0},{1,33},{33,65},{65,97},{97,1},{2,34}... | collective-permute-start | bytes 786440 | tf_op jit(solution)/shard_map/ppermute | solution.py:273
  29.5 30.4 %collective-permute-start.1 = (bf16[8,128,128]{2,1,0:T(8,128)(2,1)S(1)}, bf16[8,128,128]{2,1,0:T(8,128)(2,1)}, u32[]{:S(2)}, u32[]{:S(2)}) collective-permute-start(bf16[8,128,128]{2,1,0:T(8,128)(2,1)S(1)} %bitcast.41), channel_id=1, source_target_pairs={{0,3},{1,0},{2,1},{3,2},{4,7},{5,4},{6,5},{7,6},{8,11},{9,8},{10,9... | collective-permute-start | bytes 786440 | tf_op jit(solution)/shard_map/ppermute | solution.py:273
  32.2 27.7 %collective-permute-start = (bf16[8,128,128]{2,1,0:T(8,128)(2,1)S(1)}, bf16[8,128,128]{2,1,0:T(8,128)(2,1)}, u32[]{:S(2)}, u32[]{:S(2)}) collective-permute-start(bf16[8,128,128]{2,1,0:T(8,128)(2,1)S(1)} %bitcast.40), channel_id=1, source_target_pairs={{0,1},{1,2},{2,3},{3,0},{4,5},{5,6},{6,7},{7,4},{8,9},{9,10},{10,1... | collective-permute-start | bytes 786440 | tf_op jit(solution)/shard_map/ppermute | solution.py:273
  34.1 4.5 %copy-start.4 = (bf16[8,128,128]{2,1,0:T(8,128)(2,1)}, bf16[8,128,128]{2,1,0:T(8,128)(2,1)S(1)}, u32[]{:S(2)}) copy-start(bf16[8,128,128]{2,1,0:T(8,128)(2,1)S(1)} %collective-permute-done.3.rest_3_) | copy-start | bytes 786436
  34.1 25.8 %collective-permute-start.4 = (bf16[8,128,128]{2,1,0:T(8,128)(2,1)S(1)}, bf16[8,128,128]{2,1,0:T(8,128)(2,1)}, u32[]{:S(2)}, u32[]{:S(2)}) collective-permute-start(bf16[8,128,128]{2,1,0:T(8,128)(2,1)S(1)} %bitcast.39), channel_id=1, source_target_pairs={{0,4},{4,8},{8,12},{12,0},{1,5},{5,9},{9,13},{13,1},{2,6},{6,10},{... | collective-permute-start | bytes 786440 | tf_op jit(solution)/shard_map/ppermute | solution.py:273
  36.8 9.7 %copy-start.3 = (f32[64,8,128]{2,1,0:T(8,128)}, f32[64,8,128]{2,1,0:T(8,128)S(1)}, u32[]{:S(2)}) copy-start(f32[64,8,128]{2,1,0:T(8,128)S(1)} %all-to-all-done.rows_in) | copy-start | bytes 786436
  38.7 36.1 %all-to-all-start.1 = ((bf16[64,128,128]{2,1,0:T(8,128)(2,1)}), bf16[64,128,128]{2,1,0:T(8,128)(2,1)S(1)}, u32[]{:S(2)}, u32[]{:S(2)}) async-start(bf16[64,128,128]{2,1,0:T(8,128)(2,1)} %broadcast_in_dim.7), calls=%async_computation.1 | async-start | bytes 4194304 | tf_op jit(solution)/shard_map/all_to_all | solution.py:266
  62.9 19.4 %collective-permute-start.6 = (bf16[64,128,128]{2,1,0:T(8,128)(2,1)}, bf16[64,128,128]{2,1,0:T(8,128)(2,1)}, u32[]{:S(2)}, u32[]{:S(2)}) collective-permute-start(bf16[64,128,128]{2,1,0:T(8,128)(2,1)} %hold.1.own_in), channel_id=1, source_target_pairs={{0,16},{16,0},{1,17},{17,1},{2,18},{18,2},{3,19},{19,3},{4,20},{20... | collective-permute-start | bytes 6291464 | tf_op jit(solution)/shard_map/ppermute | solution.py:336
  74.8 2.0 copy-start.2
  76.8 35.7 %all-to-all-start.3 = ((bf16[64,128,128]{2,1,0:T(8,128)(2,1)}), bf16[64,128,128]{2,1,0:T(8,128)(2,1)}, u32[]{:S(2)}, u32[]{:S(2)}) async-start(bf16[64,128,128]{2,1,0:T(8,128)(2,1)} %broadcast_in_dim.8), calls=%async_computation.3 | async-start | bytes 4194304 | tf_op jit(solution)/shard_map/all_to_all | solution.py:266
  112.5 52.2 %all-to-all-start.2 = ((bf16[64,128,128]{2,1,0:T(8,128)(2,1)}), bf16[64,128,128]{2,1,0:T(8,128)(2,1)S(1)}, u32[]{:S(2)}, u32[]{:S(2)}) async-start(bf16[64,128,128]{2,1,0:T(8,128)(2,1)} %get-tuple-element.16), calls=%async_computation.2 | async-start | bytes 4194304 | tf_op jit(solution)/shard_map/all_to_all | solution.py:379
  164.5 21.2 %collective-permute-start.7 = (bf16[64,128,128]{2,1,0:T(8,128)(2,1)}, bf16[64,128,128]{2,1,0:T(8,128)(2,1)}, u32[]{:S(2)}, u32[]{:S(2)}) collective-permute-start(bf16[64,128,128]{2,1,0:T(8,128)(2,1)} %get-tuple-element.21), channel_id=1, source_target_pairs={{0,16},{16,0},{1,17},{17,1},{2,18},{18,2},{3,19},{19,3},{4,20},{20... | collective-permute-start | bytes 6291464 | tf_op jit(solution)/shard_map/ppermute | solution.py:382
  164.8 1.3 copy-start
  166.1 55.7 %all-to-all-start.4 = ((bf16[64,128,128]{2,1,0:T(8,128)(2,1)}), bf16[64,128,128]{2,1,0:T(8,128)(2,1)S(1)}, u32[]{:S(2)}, u32[]{:S(2)}) async-start(bf16[64,128,128]{2,1,0:T(8,128)(2,1)} %get-tuple-element.19), calls=%async_computation.4 | async-start | bytes 4194304 | tf_op jit(solution)/shard_map/all_to_all | solution.py:379
  191.6 1.8 copy-start.1
  191.7 26.7 %collective-permute-start.13 = (bf16[8,128,128]{2,1,0:T(8,128)(2,1)S(1)}, bf16[8,128,128]{2,1,0:T(8,128)(2,1)S(1)}, u32[]{:S(2)}, u32[]{:S(2)}) collective-permute-start(bf16[8,128,128]{2,1,0:T(8,128)(2,1)S(1)} %get-tuple-element.26), channel_id=1, source_target_pairs={{12,0},{0,4},{4,8},{8,12},{13,1},{1,5},{5,9},{9,13},{14,2},{2,6},{... | collective-permute-start | bytes 786440 | tf_op jit(solution)/shard_map/ppermute | solution.py:385
  193.7 31.4 %collective-permute-start.12 = (bf16[8,128,128]{2,1,0:T(8,128)(2,1)S(1)}, bf16[8,128,128]{2,1,0:T(8,128)(2,1)}, u32[]{:S(2)}, u32[]{:S(2)}) collective-permute-start(bf16[8,128,128]{2,1,0:T(8,128)(2,1)S(1)} %get-tuple-element.27), channel_id=1, source_target_pairs={{4,0},{8,4},{12,8},{0,12},{5,1},{9,5},{13,9},{1,13},{6,2},{10,6},{... | collective-permute-start | bytes 786440 | tf_op jit(solution)/shard_map/ppermute | solution.py:385
  196.4 28.7 %collective-permute-start.11 = (bf16[8,128,128]{2,1,0:T(8,128)(2,1)S(1)}, bf16[8,128,128]{2,1,0:T(8,128)(2,1)}, u32[]{:S(2)}, u32[]{:S(2)}) collective-permute-start(bf16[8,128,128]{2,1,0:T(8,128)(2,1)S(1)} %get-tuple-element.28), channel_id=1, source_target_pairs={{96,0},{0,32},{32,64},{64,96},{97,1},{1,33},{33,65},{65,97},{98,2}... | collective-permute-start | bytes 786440 | tf_op jit(solution)/shard_map/ppermute | solution.py:385
  197.9 27.1 %collective-permute-start.10 = (bf16[8,128,128]{2,1,0:T(8,128)(2,1)S(1)}, bf16[8,128,128]{2,1,0:T(8,128)(2,1)}, u32[]{:S(2)}, u32[]{:S(2)}) collective-permute-start(bf16[8,128,128]{2,1,0:T(8,128)(2,1)S(1)} %get-tuple-element.29), channel_id=1, source_target_pairs={{32,0},{64,32},{96,64},{0,96},{33,1},{65,33},{97,65},{1,97},{34,2}... | collective-permute-start | bytes 786440 | tf_op jit(solution)/shard_map/ppermute | solution.py:385
  199.6 25.4 %collective-permute-start.9 = (bf16[8,128,128]{2,1,0:T(8,128)(2,1)S(1)}, bf16[8,128,128]{2,1,0:T(8,128)(2,1)}, u32[]{:S(2)}, u32[]{:S(2)}) collective-permute-start(bf16[8,128,128]{2,1,0:T(8,128)(2,1)S(1)} %get-tuple-element.30), channel_id=1, source_target_pairs={{3,0},{0,1},{1,2},{2,3},{7,4},{4,5},{5,6},{6,7},{11,8},{8,9},{9,10... | collective-permute-start | bytes 786440 | tf_op jit(solution)/shard_map/ppermute | solution.py:385
  218.4 0.7 copy-start.5
  219.1 8.6 %collective-permute-start.8 = (bf16[8,128,128]{2,1,0:T(8,128)(2,1)S(1)}, bf16[8,128,128]{2,1,0:T(8,128)(2,1)}, u32[]{:S(2)}, u32[]{:S(2)}) collective-permute-start(bf16[8,128,128]{2,1,0:T(8,128)(2,1)S(1)} %get-tuple-element.31), channel_id=1, source_target_pairs={{1,0},{2,1},{3,2},{0,3},{5,4},{6,5},{7,6},{4,7},{9,8},{10,9},{11,1... | collective-permute-start | bytes 786440 | tf_op jit(solution)/shard_map/ppermute | solution.py:385

commit v4 on v3

--- a/solution.py
+++ b/solution.py
@@ -119,10 +119,10 @@
 
 def chunk_kernel(h, last, items, counts, base, hits, rows_in, q_in, own_in, mate_in, *rest):
     if last:
-        earlier_in, query_out, own_out, mate_out, block_acc, earlier = rest[:6]
+        earlier_in, query_out, own_out, mate_out, earlier, mate_acc = rest[:6]
     else:
-        query_out, block_acc = rest[:2]
-    rows, q, blocks, query_acc, scores, sems = rest[-6:]
+        query_out, block_out = rest[:2]
+    rows, q, blocks, query_acc, block_acc, scores, sems = rest[-7:]
     scale = 2.0 / math.sqrt(q.shape[2])
     factor = scale * math.log2(math.e)
     tiles = q_in.shape[0]
@@ -215,20 +215,31 @@
     dead = jnp.int32(tiles)
     lax.fori_loop(0, counts[h] + 1, step, ((dead, dead),) * UNROLL)
 
+    if last:
+        summed.wait()
+
+        def deliver(b, carry):
+            block_acc[b] = (block_acc[b] + earlier[b]) * scale
+            mate_acc[b] = ((block_acc[b + here] + earlier[b + here]) * scale).astype(jnp.bfloat16)
+            return carry
+
+        lax.fori_loop(0, here, deliver, 0, unroll=2)
+        stores = [
+            pltpu.make_async_copy(mate_acc, mate_out, sems.at[5]),
+            pltpu.make_async_copy(block_acc.at[pl.ds(0, here)], own_out, sems.at[6]),
+        ]
+    else:
+        stores = [pltpu.make_async_copy(block_acc, block_out, sems.at[5])]
+    for store in stores:
+        store.start()
+
     def finish(t, carry):
         query_out[t] = (query_acc[t] * scale).T.astype(jnp.bfloat16)
         return carry
 
     lax.fori_loop(0, tiles, finish, 0, unroll=4)
-    if last:
-        summed.wait()
-
-        def deliver(b, carry):
-            own_out[b] = (block_acc[b] + earlier[b]) * scale
-            mate_out[b] = ((block_acc[b + here] + earlier[b + here]) * scale).astype(jnp.bfloat16)
-            return carry
-
-        lax.fori_loop(0, here, deliver, 0, unroll=2)
+    for store in stores:
+        store.wait()
 
 
 def hold_kernel(counts, kept, *rest):
@@ -346,8 +357,9 @@
             pltpu.VMEM((sources + 1, QTILE, feat_width), jnp.bfloat16),
             pltpu.VMEM((2 * blocks_here, BLOCK, feat_width), jnp.bfloat16),
             pltpu.VMEM((sources + 1, feat_width, QTILE), jnp.float32),
+            pltpu.VMEM(acc_shape.shape, jnp.float32),
             pltpu.VMEM((UNROLL, BLOCK, 2 * QTILE), jnp.float32),
-            pltpu.SemaphoreType.DMA((5,)),
+            pltpu.SemaphoreType.DMA((7,)),
         ]
 
     hbm = pl.BlockSpec(memory_space=pl.ANY)
@@ -356,7 +368,7 @@
         functools.partial(chunk_kernel, 0, False),
         out_shape=(grad_shape, acc_shape),
         in_specs=[smem] * 4 + [hbm] * 4,
-        out_specs=(vmem, vmem),
+        out_specs=(vmem, hbm),
         scratch_shapes=scratch([]),
         compiler_params=limit,
         cost_estimate=cost,
@@ -367,8 +379,10 @@
         functools.partial(chunk_kernel, 1, True),
         out_shape=(grad_shape, own_shape, mate_shape),
         in_specs=[smem] * 4 + [hbm] * 5,
-        out_specs=(vmem, vmem, vmem),
-        scratch_shapes=scratch([pltpu.VMEM(acc_shape.shape, jnp.float32)] * 2),
+        out_specs=(vmem, hbm, hbm),
+        scratch_shapes=scratch(
+            [pltpu.VMEM(acc_shape.shape, jnp.float32), pltpu.VMEM(mate_shape.shape, jnp.bfloat16)]
+        ),
         compiler_params=limit,
         cost_estimate=cost,
         name="chunk_1",

time: 234 us -> 231 us (0.987)
  transfers between devices with their start and end apart: 19 -> 19, of which waited for: 4 -> 4; matrix products, arithmetic and copies ran while one was open for 9% -> 9% of each run, Pallas kernels for 36% -> 35%
where the time goes in v4:
time: 231 us; the launch traced here: 230 us
  Pallas kernels  85 us (37%)
  starting transfers between devices  83.6 us (36%)
  waiting for transfers between devices  34.4 us (15%)
  local copies, waits for them, and re-layouts  13.1 us (6%)
  other arithmetic  12.5 us (5%)
    all_to_all x2, starting transfers between devices, shard_work(): came = lax.all_to_all(part, SAME_CORE, 0, 0, tiled=True)  38.9 us
    pallas_call x1, Pallas kernels, shard_work(): chunk_1(items[1], counts, base, hits, rows, halves[1], held, mate_held, acc)  31.5 us
    pallas_call x1, Pallas kernels, shard_work(): chunk_0(items[0], counts, base, hits, rows, halves[0], held, mate_held)  29.2 us
    ppermute x6, waiting for transfers between devices, shard_work(): lax.ppermute(held_grad[at].astype(jnp.bfloat16), axis, [(j, i) for i, j i...  19.9 us
    all_to_all x2, starting transfers between devices, shard_work(): halves.append(lax.all_to_all(spread, SAME_CORE, 0, 0, tiled=True))  13.5 us
    pallas_call x1, Pallas kernels, shard_work(): *items, counts, base, hits = listing(table)  12.6 us
    all_to_all x2, waiting for transfers between devices, shard_work(): halves.append(lax.all_to_all(spread, SAME_CORE, 0, 0, tiled=True))  11.8 us
    ppermute x6, starting transfers between devices, shard_work(): lax.ppermute(held_grad[at].astype(jnp.bfloat16), axis, [(j, i) for i, j i...  11.7 us
  transfers between devices with their start and end apart: 19, of which 4 were waited for; matrix products, arithmetic and copies ran while one was open for 9% of the time, Pallas kernels for 35%

profile of v4, /device:TPU:0, one launch (start us, length us, event | category | flops | bytes accessed | tf_op | source)
XLA Modules:
  0.0 229.6 jit_solution(5905064732206413471)
XLA Ops:
  0.6 2.3 fusion.5
  2.9 3.1 %collective-permute-start.3 = (bf16[8,128,128]{2,1,0:T(8,128)(2,1)S(1)}, bf16[8,128,128]{2,1,0:T(8,128)(2,1)S(1)}, u32[]{:S(2)}, u32[]{:S(2)}) collective-permute-start(bf16[8,128,128]{2,1,0:T(8,128)(2,1)S(1)} %bitcast.42), channel_id=1, source_target_pairs={{0,96},{32,0},{64,32},{96,64},{1,97},{33,1},{65,33},{97,65},{2,98}... | collective-permute-start | bytes 786440 | tf_op jit(solution)/shard_map/ppermute | solution.py:284
  6.1 0.1 convert_bitcast_fusion
  6.2 0.8 compare_reduce_fusion
  7.0 0.7 compare_reduce_fusion.1
  7.7 0.6 pad_add_fusion.where
  8.3 0.6 shift-left_reduce_fusion
  8.9 4.8 %ask.1 = s32[64,256]{1,0:T(8,128)} custom-call(s32[2]{0:T(128)} %pad_add_fusion.where, s32[64]{0:T(128)} %bitcast.45, s32[64]{0:T(128)} %local.1, s32[64]{0:T(128)} %get-tuple-element.23.hits, s32[64]{0:T(128)} %get-tuple-element.22.lives), custom_call_target="tpu_custom_call" | custom-call | flops 1000000 | bytes 65536 | tf_op jit(solution)/shard_map/ask/pallas_call | solution.py:305
  13.7 0.8 convert_element_type.33
  14.6 0.8 subtract_bitcast_fusion
  15.4 0.8 pad_maximum_fusion
  16.2 9.0 %all-to-all-start = ((f32[64,8,128]{2,1,0:T(8,128)}), f32[64,8,128]{2,1,0:T(8,128)S(1)}, u32[]{:S(2)}, u32[]{:S(2)}) async-start(f32[64,8,128]{2,1,0:T(8,128)} %pad_maximum_fusion), calls=%async_computation | async-start | bytes 524288 | tf_op jit(solution)/shard_map/all_to_all | solution.py:322
  25.1 2.9 %collective-permute-start.5 = (bf16[8,128,128]{2,1,0:T(8,128)(2,1)}, bf16[8,128,128]{2,1,0:T(8,128)(2,1)}, u32[]{:S(2)}, u32[]{:S(2)}) collective-permute-start(bf16[8,128,128]{2,1,0:T(8,128)(2,1)} %bitcast.13), channel_id=1, source_target_pairs={{0,12},{4,0},{8,4},{12,8},{1,13},{5,1},{9,5},{13,9},{2,14},{6,2},{... | collective-permute-start | bytes 786440 | tf_op jit(solution)/shard_map/ppermute | solution.py:284
  28.0 1.5 collective-permute-start.2
  29.5 2.7 %collective-permute-start.1 = (bf16[8,128,128]{2,1,0:T(8,128)(2,1)S(1)}, bf16[8,128,128]{2,1,0:T(8,128)(2,1)}, u32[]{:S(2)}, u32[]{:S(2)}) collective-permute-start(bf16[8,128,128]{2,1,0:T(8,128)(2,1)S(1)} %bitcast.41), channel_id=1, source_target_pairs={{0,3},{1,0},{2,1},{3,2},{4,7},{5,4},{6,5},{7,6},{8,11},{9,8},{10,9... | collective-permute-start | bytes 786440 | tf_op jit(solution)/shard_map/ppermute | solution.py:284
  32.2 1.9 slice.80
  34.1 0.1 collective-permute-start.4
  34.2 2.6 %all-to-all-done.rows_in = f32[64,8,128]{2,1,0:T(8,128)S(1)} async-done(((f32[64,8,128]{2,1,0:T(8,128)}), f32[64,8,128]{2,1,0:T(8,128)S(1)}, u32[]{:S(2)}, u32[]{:S(2)}) %all-to-all-start) | async-done | bytes 262176 | tf_op jit(solution)/shard_map/all_to_all | solution.py:322
  36.8 1.8 broadcast_in_dim.7
  38.7 7.9 %all-to-all-start.1 = ((bf16[64,128,128]{2,1,0:T(8,128)(2,1)}), bf16[64,128,128]{2,1,0:T(8,128)(2,1)S(1)}, u32[]{:S(2)}, u32[]{:S(2)}) async-start(bf16[64,128,128]{2,1,0:T(8,128)(2,1)} %broadcast_in_dim.7), calls=%async_computation.1 | async-start | bytes 4194304 | tf_op jit(solution)/shard_map/all_to_all | solution.py:277
  46.6 0.6 copy.12
  47.3 12.6 %listing.1 = (s32[28720]{0:T(1024)}, s32[28720]{0:T(1024)}, s32[2]{0:T(128)}, s32[1792]{0:T(1024)}, s32[1792]{0:T(1024)}) custom-call(s32[64,256]{1,0:T(8,128)} %bitcast.44), custom_call_target="tpu_custom_call" | custom-call | flops 1000000000 | bytes 1048576 | tf_op jit(solution)/shard_map/listing/pallas_call | solution.py:336
  59.9 3.0 %hold.1.own_in = bf16[64,128,128]{2,1,0:T(8,128)(2,1)} custom-call(s32[2]{0:T(128)} %get-tuple-element.13.counts, bf16[16,128,128]{2,1,0:T(8,128)(2,1)} %bitcast.38, bf16[8,128,128]{2,1,0:T(8,128)(2,1)} %collective-permute-done.rest_0_, bf16[8,128,128]{2,1,0:T(8,128)(2,1)} %collective-permute-done.1.rest_1_, ...), custom_call_target="tpu_custom_call" | custom-call | flops 1000000 | bytes 4194304 | tf_op jit(solution)/shard_map/hold/pallas_call | solution.py:346
  62.9 11.8 %all-to-all-done.1.q_in = bf16[64,128,128]{2,1,0:T(8,128)(2,1)S(1)} async-done(((bf16[64,128,128]{2,1,0:T(8,128)(2,1)}), bf16[64,128,128]{2,1,0:T(8,128)(2,1)S(1)}, u32[]{:S(2)}, u32[]{:S(2)}) %all-to-all-start.1) | async-done | bytes 2097184 | tf_op jit(solution)/shard_map/all_to_all | solution.py:277
  74.8 2.0 broadcast_in_dim.8
  76.8 5.6 %all-to-all-start.3 = ((bf16[64,128,128]{2,1,0:T(8,128)(2,1)}), bf16[64,128,128]{2,1,0:T(8,128)(2,1)}, u32[]{:S(2)}, u32[]{:S(2)}) async-start(bf16[64,128,128]{2,1,0:T(8,128)(2,1)} %broadcast_in_dim.8), calls=%async_computation.3 | async-start | bytes 4194304 | tf_op jit(solution)/shard_map/all_to_all | solution.py:277
  82.4 29.2 %chunk_0.1 = (bf16[64,128,128]{2,1,0:T(8,128)(2,1)}, f32[128,128,128]{2,1,0:T(8,128)}) custom-call(s32[28720]{0:T(1024)} %get-tuple-element.12.items, s32[2]{0:T(128)} %get-tuple-element.13.counts, s32[1792]{0:T(1024)} %get-tuple-element.14.base, s32[1792]{0:T(1024)} %get-tuple-element.15.hits, f32[64,8,128]{2,1,0:T(8,128)} %copy-done.3, ...), custom_call_target="tpu_custom_call" | custom-call | flops 20000000000 | bytes 33554432 | tf_op jit(solution)/shard_map/chunk_0/pallas_call | solution.py:377
  111.6 19.4 %all-to-all-start.2 = ((bf16[64,128,128]{2,1,0:T(8,128)(2,1)}), bf16[64,128,128]{2,1,0:T(8,128)(2,1)S(1)}, u32[]{:S(2)}, u32[]{:S(2)}) async-start(bf16[64,128,128]{2,1,0:T(8,128)(2,1)} %get-tuple-element.16), calls=%async_computation.2 | async-start | bytes 4194304 | tf_op jit(solution)/shard_map/all_to_all | solution.py:393
  131.0 31.5 %chunk_1.1 = (bf16[64,128,128]{2,1,0:T(8,128)(2,1)}, f32[64,128,128]{2,1,0:T(8,128)}, bf16[64,128,128]{2,1,0:T(8,128)(2,1)}) custom-call(s32[28720]{0:T(1024)} %get-tuple-element.17.items, s32[2]{0:T(128)} %get-tuple-element.13.counts, s32[1792]{0:T(1024)} %get-tuple-element.14.base, s32[1792]{0:T(1024)} %get-tuple-element.15.hits, f32[64,8,128]{2,1,0:T(8,128)} %copy-done.3, ...), custom_call_target="tpu_custom_call" | custom-call | flops 20000000000 | bytes 33554432 | tf_op jit(solution)/shard_map/chunk_1/pallas_call | solution.py:390
  162.5 0.3 collective-permute-start.7
  162.8 1.3 copy-done
  164.1 19.5 %all-to-all-start.4 = ((bf16[64,128,128]{2,1,0:T(8,128)(2,1)}), bf16[64,128,128]{2,1,0:T(8,128)(2,1)S(1)}, u32[]{:S(2)}, u32[]{:S(2)}) async-start(bf16[64,128,128]{2,1,0:T(8,128)(2,1)} %get-tuple-element.19), calls=%async_computation.4 | async-start | bytes 4194304 | tf_op jit(solution)/shard_map/all_to_all | solution.py:393
  183.6 6.0 %fusion.3 = (bf16[64,128,128]{2,1,0:T(8,128)(2,1)S(1)}, f32[64,128,128]{2,1,0:T(8,128)}) fusion(f32[64,128,128]{2,1,0:T(8,128)} %get-tuple-element.20, bf16[64,128,128]{2,1,0:T(8,128)(2,1)} %collective-permute-done.7), kind=kLoop, calls=%fused_computation.26 | loop fusion | flops 3145728 | bytes 12582912 | tf_op jit(solution)/shard_map/convert.5
  189.6 0.1 fusion.4
  189.7 1.6 collective-permute-start.13
  191.3 0.3 convert_reduce_fusion.1
  191.6 2.7 %collective-permute-start.12 = (bf16[8,128,128]{2,1,0:T(8,128)(2,1)S(1)}, bf16[8,128,128]{2,1,0:T(8,128)(2,1)}, u32[]{:S(2)}, u32[]{:S(2)}) collective-permute-start(bf16[8,128,128]{2,1,0:T(8,128)(2,1)S(1)} %get-tuple-element.27), channel_id=1, source_target_pairs={{4,0},{8,4},{12,8},{0,12},{5,1},{9,5},{13,9},{1,13},{6,2},{10,6},{... | collective-permute-start | bytes 786440 | tf_op jit(solution)/shard_map/ppermute | solution.py:399
  194.3 1.5 collective-permute-start.11
  195.8 1.7 collective-permute-start.10
  197.6 1.5 collective-permute-start.9
  199.0 17.3 %collective-permute-done.13.rest_5_ = bf16[8,128,128]{2,1,0:T(8,128)(2,1)S(1)} collective-permute-done((bf16[8,128,128]{2,1,0:T(8,128)(2,1)S(1)}, bf16[8,128,128]{2,1,0:T(8,128)(2,1)S(1)}, u32[]{:S(2)}, u32[]{:S(2)}) %collective-permute-start.13) | collective-permute-done | bytes 262176 | tf_op jit(solution)/shard_map/ppermute | solution.py:399
  216.3 0.7 copy-done.5
  217.0 2.6 %collective-permute-start.8 = (bf16[8,128,128]{2,1,0:T(8,128)(2,1)S(1)}, bf16[8,128,128]{2,1,0:T(8,128)(2,1)}, u32[]{:S(2)}, u32[]{:S(2)}) collective-permute-start(bf16[8,128,128]{2,1,0:T(8,128)(2,1)S(1)} %get-tuple-element.31), channel_id=1, source_target_pairs={{1,0},{2,1},{3,2},{0,3},{5,4},{6,5},{7,6},{4,7},{9,8},{10,9},{11,1... | collective-permute-start | bytes 786440 | tf_op jit(solution)/shard_map/ppermute | solution.py:399
  219.7 0.3 convert_reduce_fusion
  220.0 0.7 pad_maximum_fusion.1
  220.7 2.3 %slice.103.kept = f32[16,128,128]{2,1,0:T(8,128)} slice(f32[64,128,128]{2,1,0:T(8,128)} %get-tuple-element.25), slice={[0:16], [0:128], [0:128]} | slice | bytes 2097152 | tf_op jit(solution)/shard_map/slice | solution.py:411
  223.0 2.6 %collective-permute-done.8.rest_0_ = bf16[8,128,128]{2,1,0:T(8,128)(2,1)} collective-permute-done((bf16[8,128,128]{2,1,0:T(8,128)(2,1)S(1)}, bf16[8,128,128]{2,1,0:T(8,128)(2,1)}, u32[]{:S(2)}, u32[]{:S(2)}) %collective-permute-start.8) | collective-permute-done | bytes 262176 | tf_op jit(solution)/shard_map/ppermute | solution.py:399
  225.6 3.9 %assemble.1 = f32[64,128,128]{2,1,0:T(8,128)} custom-call(f32[16,128,128]{2,1,0:T(8,128)} %slice.103.kept, bf16[8,128,128]{2,1,0:T(8,128)(2,1)} %collective-permute-done.8.rest_0_, bf16[8,128,128]{2,1,0:T(8,128)(2,1)} %collective-permute-done.9.rest_1_, bf16[8,128,128]{2,1,0:T(8,128)(2,1)} %collective-permute-done.10.rest_2_, ...), custom_call_target="tpu_custom_call" | custom-call | flops 1000000 | bytes 8388608 | tf_op jit(solution)/shard_map/assemble/pallas_call | solution.py:411
  (40 shorter events, 0.2 us)
Async XLA Ops:
  0.6 5.4 %copy-start.8 = (s32[4096]{0:T(1024)S(1)}, s32[4096]{0:T(1024)}, u32[]{:S(2)}) copy-start(s32[4096]{0:T(1024)} %param.12) | copy-start | bytes 49156
  0.6 5.5 %copy-start.6 = (s32[32,512]{1,0:T(8,128)S(1)}, s32[32,512]{1,0:T(8,128)}, u32[]{:S(2)}) copy-start(s32[32,512]{1,0:T(8,128)} %param.13) | copy-start | bytes 196612
  2.9 31.2 %copy-start.7 = (bf16[256,128]{1,0:T(8,128)(2,1)S(1)}, bf16[256,128]{1,0:T(8,128)(2,1)}, u32[]{:S(2)}) copy-start(bf16[256,128]{1,0:T(8,128)(2,1)} %param.8) | copy-start | bytes 196612
  2.9 31.2 %collective-permute-start.3 = (bf16[8,128,128]{2,1,0:T(8,128)(2,1)S(1)}, bf16[8,128,128]{2,1,0:T(8,128)(2,1)S(1)}, u32[]{:S(2)}, u32[]{:S(2)}) collective-permute-start(bf16[8,128,128]{2,1,0:T(8,128)(2,1)S(1)} %bitcast.42), channel_id=1, source_target_pairs={{0,96},{32,0},{64,32},{96,64},{1,97},{33,1},{65,33},{97,65},{2,98}... | collective-permute-start | bytes 786440 | tf_op jit(solution)/shard_map/ppermute | solution.py:284
  16.2 20.7 %all-to-all-start = ((f32[64,8,128]{2,1,0:T(8,128)}), f32[64,8,128]{2,1,0:T(8,128)S(1)}, u32[]{:S(2)}, u32[]{:S(2)}) async-start(f32[64,8,128]{2,1,0:T(8,128)} %pad_maximum_fusion), calls=%async_computation | async-start | bytes 524288 | tf_op jit(solution)/shard_map/all_to_all | solution.py:322
  25.1 34.7 %collective-permute-start.5 = (bf16[8,128,128]{2,1,0:T(8,128)(2,1)}, bf16[8,128,128]{2,1,0:T(8,128)(2,1)}, u32[]{:S(2)}, u32[]{:S(2)}) collective-permute-start(bf16[8,128,128]{2,1,0:T(8,128)(2,1)} %bitcast.13), channel_id=1, source_target_pairs={{0,12},{4,0},{8,4},{12,8},{1,13},{5,1},{9,5},{13,9},{2,14},{6,2},{... | collective-permute-start | bytes 786440 | tf_op jit(solution)/shard_map/ppermute | solution.py:284
  28.0 31.9 %collective-permute-start.2 = (bf16[8,128,128]{2,1,0:T(8,128)(2,1)}, bf16[8,128,128]{2,1,0:T(8,128)(2,1)}, u32[]{:S(2)}, u32[]{:S(2)}) collective-permute-start(bf16[8,128,128]{2,1,0:T(8,128)(2,1)} %bitcast.10), channel_id=1, source_target_pairs={{0,32},{32,64},{64,96},{96,0},{1,33},{33,65},{65,97},{97,1},{2,34}... | collective-permute-start | bytes 786440 | tf_op jit(solution)/shard_map/ppermute | solution.py:284
  29.5 30.4 %collective-permute-start.1 = (bf16[8,128,128]{2,1,0:T(8,128)(2,1)S(1)}, bf16[8,128,128]{2,1,0:T(8,128)(2,1)}, u32[]{:S(2)}, u32[]{:S(2)}) collective-permute-start(bf16[8,128,128]{2,1,0:T(8,128)(2,1)S(1)} %bitcast.41), channel_id=1, source_target_pairs={{0,3},{1,0},{2,1},{3,2},{4,7},{5,4},{6,5},{7,6},{8,11},{9,8},{10,9... | collective-permute-start | bytes 786440 | tf_op jit(solution)/shard_map/ppermute | solution.py:284
  32.2 27.7 %collective-permute-start = (bf16[8,128,128]{2,1,0:T(8,128)(2,1)S(1)}, bf16[8,128,128]{2,1,0:T(8,128)(2,1)}, u32[]{:S(2)}, u32[]{:S(2)}) collective-permute-start(bf16[8,128,128]{2,1,0:T(8,128)(2,1)S(1)} %bitcast.40), channel_id=1, source_target_pairs={{0,1},{1,2},{2,3},{3,0},{4,5},{5,6},{6,7},{7,4},{8,9},{9,10},{10,1... | collective-permute-start | bytes 786440 | tf_op jit(solution)/shard_map/ppermute | solution.py:284
  34.1 4.5 %copy-start.4 = (bf16[8,128,128]{2,1,0:T(8,128)(2,1)}, bf16[8,128,128]{2,1,0:T(8,128)(2,1)S(1)}, u32[]{:S(2)}) copy-start(bf16[8,128,128]{2,1,0:T(8,128)(2,1)S(1)} %collective-permute-done.3.rest_3_) | copy-start | bytes 786436
  34.1 25.8 %collective-permute-start.4 = (bf16[8,128,128]{2,1,0:T(8,128)(2,1)S(1)}, bf16[8,128,128]{2,1,0:T(8,128)(2,1)}, u32[]{:S(2)}, u32[]{:S(2)}) collective-permute-start(bf16[8,128,128]{2,1,0:T(8,128)(2,1)S(1)} %bitcast.39), channel_id=1, source_target_pairs={{0,4},{4,8},{8,12},{12,0},{1,5},{5,9},{9,13},{13,1},{2,6},{6,10},{... | collective-permute-start | bytes 786440 | tf_op jit(solution)/shard_map/ppermute | solution.py:284
  36.8 9.7 %copy-start.3 = (f32[64,8,128]{2,1,0:T(8,128)}, f32[64,8,128]{2,1,0:T(8,128)S(1)}, u32[]{:S(2)}) copy-start(f32[64,8,128]{2,1,0:T(8,128)S(1)} %all-to-all-done.rows_in) | copy-start | bytes 786436
  38.7 36.1 %all-to-all-start.1 = ((bf16[64,128,128]{2,1,0:T(8,128)(2,1)}), bf16[64,128,128]{2,1,0:T(8,128)(2,1)S(1)}, u32[]{:S(2)}, u32[]{:S(2)}) async-start(bf16[64,128,128]{2,1,0:T(8,128)(2,1)} %broadcast_in_dim.7), calls=%async_computation.1 | async-start | bytes 4194304 | tf_op jit(solution)/shard_map/all_to_all | solution.py:277
  62.9 19.4 %collective-permute-start.6 = (bf16[64,128,128]{2,1,0:T(8,128)(2,1)}, bf16[64,128,128]{2,1,0:T(8,128)(2,1)}, u32[]{:S(2)}, u32[]{:S(2)}) collective-permute-start(bf16[64,128,128]{2,1,0:T(8,128)(2,1)} %hold.1.own_in), channel_id=1, source_target_pairs={{0,16},{16,0},{1,17},{17,1},{2,18},{18,2},{3,19},{19,3},{4,20},{20... | collective-permute-start | bytes 6291464 | tf_op jit(solution)/shard_map/ppermute | solution.py:347
  74.8 2.0 copy-start.2
  76.8 34.8 %all-to-all-start.3 = ((bf16[64,128,128]{2,1,0:T(8,128)(2,1)}), bf16[64,128,128]{2,1,0:T(8,128)(2,1)}, u32[]{:S(2)}, u32[]{:S(2)}) async-start(bf16[64,128,128]{2,1,0:T(8,128)(2,1)} %broadcast_in_dim.8), calls=%async_computation.3 | async-start | bytes 4194304 | tf_op jit(solution)/shard_map/all_to_all | solution.py:277
  111.6 51.2 %all-to-all-start.2 = ((bf16[64,128,128]{2,1,0:T(8,128)(2,1)}), bf16[64,128,128]{2,1,0:T(8,128)(2,1)S(1)}, u32[]{:S(2)}, u32[]{:S(2)}) async-start(bf16[64,128,128]{2,1,0:T(8,128)(2,1)} %get-tuple-element.16), calls=%async_computation.2 | async-start | bytes 4194304 | tf_op jit(solution)/shard_map/all_to_all | solution.py:393
  162.5 21.1 %collective-permute-start.7 = (bf16[64,128,128]{2,1,0:T(8,128)(2,1)}, bf16[64,128,128]{2,1,0:T(8,128)(2,1)}, u32[]{:S(2)}, u32[]{:S(2)}) collective-permute-start(bf16[64,128,128]{2,1,0:T(8,128)(2,1)} %get-tuple-element.21), channel_id=1, source_target_pairs={{0,16},{16,0},{1,17},{17,1},{2,18},{18,2},{3,19},{19,3},{4,20},{20... | collective-permute-start | bytes 6291464 | tf_op jit(solution)/shard_map/ppermute | solution.py:396
  162.8 1.3 copy-start
  164.1 55.6 %all-to-all-start.4 = ((bf16[64,128,128]{2,1,0:T(8,128)(2,1)}), bf16[64,128,128]{2,1,0:T(8,128)(2,1)S(1)}, u32[]{:S(2)}, u32[]{:S(2)}) async-start(bf16[64,128,128]{2,1,0:T(8,128)(2,1)} %get-tuple-element.19), calls=%async_computation.4 | async-start | bytes 4194304 | tf_op jit(solution)/shard_map/all_to_all | solution.py:393
  189.6 1.8 copy-start.1
  189.7 26.7 %collective-permute-start.13 = (bf16[8,128,128]{2,1,0:T(8,128)(2,1)S(1)}, bf16[8,128,128]{2,1,0:T(8,128)(2,1)S(1)}, u32[]{:S(2)}, u32[]{:S(2)}) collective-permute-start(bf16[8,128,128]{2,1,0:T(8,128)(2,1)S(1)} %get-tuple-element.26), channel_id=1, source_target_pairs={{12,0},{0,4},{4,8},{8,12},{13,1},{1,5},{5,9},{9,13},{14,2},{2,6},{... | collective-permute-start | bytes 786440 | tf_op jit(solution)/shard_map/ppermute | solution.py:399
  191.6 31.4 %collective-permute-start.12 = (bf16[8,128,128]{2,1,0:T(8,128)(2,1)S(1)}, bf16[8,128,128]{2,1,0:T(8,128)(2,1)}, u32[]{:S(2)}, u32[]{:S(2)}) collective-permute-start(bf16[8,128,128]{2,1,0:T(8,128)(2,1)S(1)} %get-tuple-element.27), channel_id=1, source_target_pairs={{4,0},{8,4},{12,8},{0,12},{5,1},{9,5},{13,9},{1,13},{6,2},{10,6},{... | collective-permute-start | bytes 786440 | tf_op jit(solution)/shard_map/ppermute | solution.py:399
  194.3 28.7 %collective-permute-start.11 = (bf16[8,128,128]{2,1,0:T(8,128)(2,1)S(1)}, bf16[8,128,128]{2,1,0:T(8,128)(2,1)}, u32[]{:S(2)}, u32[]{:S(2)}) collective-permute-start(bf16[8,128,128]{2,1,0:T(8,128)(2,1)S(1)} %get-tuple-element.28), channel_id=1, source_target_pairs={{96,0},{0,32},{32,64},{64,96},{97,1},{1,33},{33,65},{65,97},{98,2}... | collective-permute-start | bytes 786440 | tf_op jit(solution)/shard_map/ppermute | solution.py:399
  195.8 27.1 %collective-permute-start.10 = (bf16[8,128,128]{2,1,0:T(8,128)(2,1)S(1)}, bf16[8,128,128]{2,1,0:T(8,128)(2,1)}, u32[]{:S(2)}, u32[]{:S(2)}) collective-permute-start(bf16[8,128,128]{2,1,0:T(8,128)(2,1)S(1)} %get-tuple-element.29), channel_id=1, source_target_pairs={{32,0},{64,32},{96,64},{0,96},{33,1},{65,33},{97,65},{1,97},{34,2}... | collective-permute-start | bytes 786440 | tf_op jit(solution)/shard_map/ppermute | solution.py:399
  197.6 25.4 %collective-permute-start.9 = (bf16[8,128,128]{2,1,0:T(8,128)(2,1)S(1)}, bf16[8,128,128]{2,1,0:T(8,128)(2,1)}, u32[]{:S(2)}, u32[]{:S(2)}) collective-permute-start(bf16[8,128,128]{2,1,0:T(8,128)(2,1)S(1)} %get-tuple-element.30), channel_id=1, source_target_pairs={{3,0},{0,1},{1,2},{2,3},{7,4},{4,5},{5,6},{6,7},{11,8},{8,9},{9,10... | collective-permute-start | bytes 786440 | tf_op jit(solution)/shard_map/ppermute | solution.py:399
  216.3 0.7 copy-start.5
  217.0 8.6 %collective-permute-start.8 = (bf16[8,128,128]{2,1,0:T(8,128)(2,1)S(1)}, bf16[8,128,128]{2,1,0:T(8,128)(2,1)}, u32[]{:S(2)}, u32[]{:S(2)}) collective-permute-start(bf16[8,128,128]{2,1,0:T(8,128)(2,1)S(1)} %get-tuple-element.31), channel_id=1, source_target_pairs={{1,0},{2,1},{3,2},{0,3},{5,4},{6,5},{7,6},{4,7},{9,8},{10,9},{11,1... | collective-permute-start | bytes 786440 | tf_op jit(solution)/shard_map/ppermute | solution.py:399

commit v5 on v4

--- a/solution.py
+++ b/solution.py
@@ -23,6 +23,7 @@
 COUNT_AT = PLACES * FIELDS
 DEAD = -1e30
 UNROLL = 12
+PIECE = 2048
 VMEM_LIMIT = 60 * 1024 * 1024
 
 
@@ -117,12 +118,12 @@
         counts[h] = (ends[h] + 2 * UNROLL - 1) // (2 * UNROLL)
 
 
-def chunk_kernel(h, last, items, counts, base, hits, rows_in, q_in, own_in, mate_in, *rest):
+def chunk_kernel(h, last, counts, base, hits, items_in, rows_in, q_in, own_in, mate_in, *rest):
     if last:
         earlier_in, query_out, own_out, mate_out, earlier, mate_acc = rest[:6]
     else:
         query_out, block_out = rest[:2]
-    rows, q, blocks, query_acc, block_acc, scores, sems = rest[-7:]
+    items, rows, q, blocks, query_acc, block_acc, scores, sems = rest[-8:]
     scale = 2.0 / math.sqrt(q.shape[2])
     factor = scale * math.log2(math.e)
     tiles = q_in.shape[0]
@@ -139,6 +140,15 @@
         load.start()
     if last:
         summed.start()
+
+    def load_items(i, carry):
+        at = pl.ds(pl.multiple_of(i * PIECE, PIECE), PIECE)
+        piece = pltpu.make_async_copy(items_in.at[at], items.at[at], sems.at[7])
+        piece.start()
+        piece.wait()
+        return carry
+
+    lax.fori_loop(0, (2 * UNROLL * (counts[h] + 1) + PIECE - 1) // PIECE, load_items, 0)
     zero = jnp.zeros((BLOCK, QTILE), jnp.float32)
     q[tiles] = zero.astype(q.dtype)
     rows[tiles] = jnp.full(rows.shape[1:], -1.0, jnp.float32)
@@ -242,14 +252,11 @@
         store.wait()
 
 
-def hold_kernel(counts, kept, *rest):
+def hold_kernel(kept, *rest):
     *lent, out = rest
-
-    @pl.when(counts[0] >= 0)
-    def _():
-        out[pl.ds(0, KEPT)] = kept[...]
-        for k, part in enumerate(lent):
-            out[pl.ds(KEPT + SLAB * k, SLAB)] = part[...]
+    out[pl.ds(0, KEPT)] = kept[...]
+    for k, part in enumerate(lent):
+        out[pl.ds(KEPT + SLAB * k, SLAB)] = part[...]
 
 
 def assemble_kernel(kept, *rest):
@@ -302,13 +309,9 @@
         cost_estimate=pl.CostEstimate(flops=10**6, bytes_accessed=2**16, transcendentals=0),
         name="ask",
     )
-    table = ask(
-        jnp.stack([first_slot, core]),
-        owners,
-        fetch_local,
-        tile_bits(tile_hit),
-        tile_bits(jnp.logical_or(tile_hit, pos_hit)),
-    )
+    hits = tile_bits(tile_hit)
+    lives = tile_bits(jnp.logical_or(tile_hit, pos_hit))
+    table = ask(jnp.stack([first_slot, core]), owners, fetch_local, hits, lives)
     first_row = narrow_pos * own_rows
     lse_own = lax.dynamic_slice_in_dim(lse_shift, first_row, own_rows, 0)
     loss_own = lax.dynamic_slice_in_dim(loss_weight, first_row, own_rows, 0)
@@ -321,7 +324,7 @@
     packed = jnp.concatenate([per_query, packed], axis=1)
     rows = lax.all_to_all(packed, SAME_CORE, 0, 0, tiled=True)
     table = rows[:, 6:].astype(jnp.int32).reshape(sources, 2 * QTILE)
-    most = sources * PLACES * (tiles // 2) + 4 * UNROLL
+    most = -(-(sources * PLACES * (tiles // 2) + 4 * UNROLL) // PIECE) * PIECE
     list_shape = jax.ShapeDtypeStruct((most,), jnp.int32)
     entry_shape = jax.ShapeDtypeStruct((sources * PLACES,), jnp.int32)
     listing = pl.pallas_call(
@@ -337,13 +340,13 @@
     hold = pl.pallas_call(
         hold_kernel,
         out_shape=jax.ShapeDtypeStruct(stored.shape, stored.dtype),
-        in_specs=[smem] + [vmem] * (1 + len(lent)),
+        in_specs=[vmem] * (1 + len(lent)),
         out_specs=vmem,
         compiler_params=limit,
         cost_estimate=pl.CostEstimate(flops=10**6, bytes_accessed=2**22, transcendentals=0),
         name="hold",
     )
-    held = hold(counts, kept, *lent)
+    held = hold(kept, *lent)
     mate_held = lax.ppermute(held, "c", [(0, 1), (1, 0)])
 
     acc_shape = jax.ShapeDtypeStruct((2 * blocks_here, BLOCK, feat_width), jnp.float32)
@@ -353,13 +356,14 @@
 
     def scratch(extra):
         return extra + [
+            pltpu.SMEM((most,), jnp.int32),
             pltpu.VMEM((sources + 1, 8, QTILE), jnp.float32),
             pltpu.VMEM((sources + 1, QTILE, feat_width), jnp.bfloat16),
             pltpu.VMEM((2 * blocks_here, BLOCK, feat_width), jnp.bfloat16),
             pltpu.VMEM((sources + 1, feat_width, QTILE), jnp.float32),
             pltpu.VMEM(acc_shape.shape, jnp.float32),
             pltpu.VMEM((UNROLL, BLOCK, 2 * QTILE), jnp.float32),
-            pltpu.SemaphoreType.DMA((7,)),
+            pltpu.SemaphoreType.DMA((8,)),
         ]
 
     hbm = pl.BlockSpec(memory_space=pl.ANY)
@@ -367,18 +371,18 @@
     chunk_0 = pl.pallas_call(
         functools.partial(chunk_kernel, 0, False),
         out_shape=(grad_shape, acc_shape),
-        in_specs=[smem] * 4 + [hbm] * 4,
+        in_specs=[smem] * 3 + [hbm] * 5,
         out_specs=(vmem, hbm),
         scratch_shapes=scratch([]),
         compiler_params=limit,
         cost_estimate=cost,
         name="chunk_0",
     )
-    grad_0, acc = chunk_0(items[0], counts, base, hits, rows, halves[0], held, mate_held)
+    grad_0, acc = chunk_0(counts, base, hits, items[0], rows, halves[0], held, mate_held)
     chunk_1 = pl.pallas_call(
         functools.partial(chunk_kernel, 1, True),
         out_shape=(grad_shape, own_shape, mate_shape),
-        in_specs=[smem] * 4 + [hbm] * 5,
+        in_specs=[smem] * 3 + [hbm] * 6,
         out_specs=(vmem, hbm, hbm),
         scratch_shapes=scratch(
             [pltpu.VMEM(acc_shape.shape, jnp.float32), pltpu.VMEM(mate_shape.shape, jnp.bfloat16)]
@@ -387,7 +391,7 @@
         cost_estimate=cost,
         name="chunk_1",
     )
-    grad_1, own_grad, mate_grad = chunk_1(items[1], counts, base, hits, rows, halves[1], held, mate_held, acc)
+    grad_1, own_grad, mate_grad = chunk_1(counts, base, hits, items[1], rows, halves[1], held, mate_held, acc)
     sums = []
     for part in (grad_0, grad_1):
         came = lax.all_to_all(part, SAME_CORE, 0, 0, tiled=True)

time: 231 us -> 249 us (1.078)
  waiting for transfers between devices: 34.4 us -> 47.5 us
  starting transfers between devices: 83.6 us -> 88.6 us
  Pallas kernels: 85 us -> 81.5 us
    ppermute x6, waiting for transfers between devices: 0.02 us -> 22.2 us  [shard_work(): lax.ppermute(stored[at], axis, way)]
    all_to_all x2, waiting for transfers between devices: 11.8 us -> 0.01 us  [shard_work(): halves.append(lax.all_to_all(spread, SAME_CORE, 0, 0, tiled=True))]
    pallas_call x4, Pallas kernels: 68.5 us -> 64.7 us  [the longest x1 29.5 us: shard_work(): chunk_1(counts, base, hits, items[1], rows, halves[1], held, mate_held, acc)]
    all_to_all x2, starting transfers between devices: 38.9 us -> 42.1 us  [shard_work(): came = lax.all_to_all(part, SAME_CORE, 0, 0, tiled=True)]
    all_to_all x1, waiting for transfers between devices: 2.6 us -> 5.33 us  [shard_work(): rows = lax.all_to_all(packed, SAME_CORE, 0, 0, tiled=True)]
    all_to_all x1, starting transfers between devices: 8.96 us -> 11.5 us  [shard_work(): rows = lax.all_to_all(packed, SAME_CORE, 0, 0, tiled=True)]
  transfers between devices with their start and end apart: 19 -> 19, of which waited for: 4 -> 6; matrix products, arithmetic and copies ran while one was open for 9% -> 7% of each run, Pallas kernels for 35% -> 29%
where the time goes in v5:
time: 249 us; the launch traced here: 247 us
  starting transfers between devices  88.6 us (36%)
  Pallas kernels  81.5 us (33%)
  waiting for transfers between devices  47.5 us (19%)
  other arithmetic  14.7 us (6%)
  local copies, waits for them, and re-layouts  13.9 us (6%)
    all_to_all x2, starting transfers between devices, shard_work(): came = lax.all_to_all(part, SAME_CORE, 0, 0, tiled=True)  42.1 us
    pallas_call x1, Pallas kernels, shard_work(): chunk_1(counts, base, hits, items[1], rows, halves[1], held, mate_held, acc)  29.5 us
    pallas_call x1, Pallas kernels, shard_work(): chunk_0(counts, base, hits, items[0], rows, halves[0], held, mate_held)  27.4 us
    ppermute x6, waiting for transfers between devices, shard_work(): lax.ppermute(stored[at], axis, way)  22.2 us
    ppermute x6, waiting for transfers between devices, shard_work(): lax.ppermute(held_grad[at].astype(jnp.bfloat16), axis, [(j, i) for i, j i...  19.9 us
    all_to_all x2, starting transfers between devices, shard_work(): halves.append(lax.all_to_all(spread, SAME_CORE, 0, 0, tiled=True))  13.1 us
    pallas_call x1, Pallas kernels, shard_work(): *items, counts, base, hits = listing(table)  12.9 us
    ppermute x6, starting transfers between devices, shard_work(): lax.ppermute(held_grad[at].astype(jnp.bfloat16), axis, [(j, i) for i, j i...  11.7 us
  transfers between devices with their start and end apart: 19, of which 6 were waited for; matrix products, arithmetic and copies ran while one was open for 7% of the time, Pallas kernels for 29%

profile of v5, /device:TPU:0, one launch (start us, length us, event | category | flops | bytes accessed | tf_op | source)
XLA Modules:
  0.0 247.0 jit_solution(12481674153589936645)
XLA Ops:
  0.6 0.7 add_select_fusion
  1.4 0.8 convert_bitcast_fusion
  2.1 1.5 compare_reduce_fusion
  3.7 0.7 compare_reduce_fusion.1
  4.4 0.7 pad_add_fusion.where
  5.0 0.6 shift-left_reduce_fusion
  5.7 4.8 %ask.1 = s32[64,256]{1,0:T(8,128)} custom-call(s32[2]{0:T(128)} %pad_add_fusion.where, s32[64]{0:T(128)} %bitcast.46, s32[64]{0:T(128)} %local.1, s32[64]{0:T(128)} %get-tuple-element.23.hits, s32[64]{0:T(128)} %get-tuple-element.22.lives), custom_call_target="tpu_custom_call" | custom-call | flops 1000000 | bytes 65536 | tf_op jit(solution)/shard_map/ask/pallas_call | solution.py:314
  10.4 0.8 convert_element_type.33
  11.3 0.8 subtract_bitcast_fusion
  12.2 0.8 pad_maximum_fusion
  12.9 11.5 %all-to-all-start = ((f32[64,8,128]{2,1,0:T(8,128)}), f32[64,8,128]{2,1,0:T(8,128)S(1)}, u32[]{:S(2)}, u32[]{:S(2)}) async-start(f32[64,8,128]{2,1,0:T(8,128)} %pad_maximum_fusion), calls=%async_computation | async-start | bytes 524288 | tf_op jit(solution)/shard_map/all_to_all | solution.py:325
  24.5 2.3 fusion.5
  26.7 3.0 %collective-permute-start.3 = (bf16[8,128,128]{2,1,0:T(8,128)(2,1)}, bf16[8,128,128]{2,1,0:T(8,128)(2,1)S(1)}, u32[]{:S(2)}, u32[]{:S(2)}) collective-permute-start(bf16[8,128,128]{2,1,0:T(8,128)(2,1)} %bitcast.11), channel_id=1, source_target_pairs={{0,96},{32,0},{64,32},{96,64},{1,97},{33,1},{65,33},{97,65},{2,98}... | collective-permute-start | bytes 786440 | tf_op jit(solution)/shard_map/ppermute | solution.py:291
  29.7 5.3 %all-to-all-done.rows_in = f32[64,8,128]{2,1,0:T(8,128)S(1)} async-done(((f32[64,8,128]{2,1,0:T(8,128)}), f32[64,8,128]{2,1,0:T(8,128)S(1)}, u32[]{:S(2)}, u32[]{:S(2)}) %all-to-all-start) | async-done | bytes 262176 | tf_op jit(solution)/shard_map/all_to_all | solution.py:325
  35.1 1.8 broadcast_in_dim.7
  36.9 4.9 %all-to-all-start.1 = ((bf16[64,128,128]{2,1,0:T(8,128)(2,1)}), bf16[64,128,128]{2,1,0:T(8,128)(2,1)S(1)}, u32[]{:S(2)}, u32[]{:S(2)}) async-start(bf16[64,128,128]{2,1,0:T(8,128)(2,1)} %broadcast_in_dim.7), calls=%async_computation.1 | async-start | bytes 4194304 | tf_op jit(solution)/shard_map/all_to_all | solution.py:284
  41.8 2.9 %collective-permute-start.5 = (bf16[8,128,128]{2,1,0:T(8,128)(2,1)}, bf16[8,128,128]{2,1,0:T(8,128)(2,1)S(1)}, u32[]{:S(2)}, u32[]{:S(2)}) collective-permute-start(bf16[8,128,128]{2,1,0:T(8,128)(2,1)} %bitcast.43), channel_id=1, source_target_pairs={{0,12},{4,0},{8,4},{12,8},{1,13},{5,1},{9,5},{13,9},{2,14},{6,2},{... | collective-permute-start | bytes 786440 | tf_op jit(solution)/shard_map/ppermute | solution.py:291
  44.6 1.5 collective-permute-start.2
  46.2 2.7 %collective-permute-start.1 = (bf16[8,128,128]{2,1,0:T(8,128)(2,1)S(1)}, bf16[8,128,128]{2,1,0:T(8,128)(2,1)S(1)}, u32[]{:S(2)}, u32[]{:S(2)}) collective-permute-start(bf16[8,128,128]{2,1,0:T(8,128)(2,1)S(1)} %bitcast.41), channel_id=1, source_target_pairs={{0,3},{1,0},{2,1},{3,2},{4,7},{5,4},{6,5},{7,6},{8,11},{9,8},{10,9... | collective-permute-start | bytes 786440 | tf_op jit(solution)/shard_map/ppermute | solution.py:291
  49.0 1.9 slice.80
  50.9 19.6 %collective-permute-done.5.rest_5_ = bf16[8,128,128]{2,1,0:T(8,128)(2,1)S(1)} collective-permute-done((bf16[8,128,128]{2,1,0:T(8,128)(2,1)}, bf16[8,128,128]{2,1,0:T(8,128)(2,1)S(1)}, u32[]{:S(2)}, u32[]{:S(2)}) %collective-permute-start.5) | collective-permute-done | bytes 262176 | tf_op jit(solution)/shard_map/ppermute | solution.py:291
  70.5 1.4 collective-permute-done.2.rest_2_
  71.9 1.2 collective-permute-done.4.rest_4_
  73.1 0.7 copy-done.9
  73.8 3.0 %hold.1.own_in = bf16[64,128,128]{2,1,0:T(8,128)(2,1)} custom-call(bf16[16,128,128]{2,1,0:T(8,128)(2,1)} %bitcast.38, bf16[8,128,128]{2,1,0:T(8,128)(2,1)} %copy-done.8, bf16[8,128,128]{2,1,0:T(8,128)(2,1)} %copy-done.7, bf16[8,128,128]{2,1,0:T(8,128)(2,1)} %copy-done.6, bf16[8,128,128]{2,1,0:T(8,128)(2,1)} %copy-done.4, bf16[8,128,128]{2,1,0:T(8,128)(2,1)} %copy-done.9, ...), custom_call_target="tpu_custom_call" | custom-call | flops 1000000 | bytes 4194304 | tf_op jit(solution)/shard_map/hold/pallas_call | solution.py:349
  76.8 2.0 broadcast_in_dim.8
  78.8 8.3 %all-to-all-start.3 = ((bf16[64,128,128]{2,1,0:T(8,128)(2,1)}), bf16[64,128,128]{2,1,0:T(8,128)(2,1)}, u32[]{:S(2)}, u32[]{:S(2)}) async-start(bf16[64,128,128]{2,1,0:T(8,128)(2,1)} %broadcast_in_dim.8), calls=%async_computation.3 | async-start | bytes 4194304 | tf_op jit(solution)/shard_map/all_to_all | solution.py:284
  87.2 0.6 copy.12
  87.8 12.9 %listing.1 = (s32[30720]{0:T(1024)}, s32[30720]{0:T(1024)}, s32[2]{0:T(128)}, s32[1792]{0:T(1024)}, s32[1792]{0:T(1024)}) custom-call(s32[64,256]{1,0:T(8,128)} %bitcast.45), custom_call_target="tpu_custom_call" | custom-call | flops 1000000000 | bytes 1048576 | tf_op jit(solution)/shard_map/listing/pallas_call | solution.py:339
  100.7 27.4 %chunk_0.1 = (bf16[64,128,128]{2,1,0:T(8,128)(2,1)}, f32[128,128,128]{2,1,0:T(8,128)}) custom-call(s32[2]{0:T(128)} %get-tuple-element.12.counts, s32[1792]{0:T(1024)} %get-tuple-element.13.base, s32[1792]{0:T(1024)} %get-tuple-element.14.hits, s32[30720]{0:T(1024)} %get-tuple-element.15.items_in, f32[64,8,128]{2,1,0:T(8,128)} %copy-done.3, ...), custom_call_target="tpu_custom_call" | custom-call | flops 20000000000 | bytes 33554432 | tf_op jit(solution)/shard_map/chunk_0/pallas_call | solution.py:381
  128.0 22.6 %all-to-all-start.2 = ((bf16[64,128,128]{2,1,0:T(8,128)(2,1)}), bf16[64,128,128]{2,1,0:T(8,128)(2,1)S(1)}, u32[]{:S(2)}, u32[]{:S(2)}) async-start(bf16[64,128,128]{2,1,0:T(8,128)(2,1)} %get-tuple-element.16), calls=%async_computation.2 | async-start | bytes 4194304 | tf_op jit(solution)/shard_map/all_to_all | solution.py:397
  150.7 29.5 %chunk_1.1 = (bf16[64,128,128]{2,1,0:T(8,128)(2,1)}, f32[64,128,128]{2,1,0:T(8,128)}, bf16[64,128,128]{2,1,0:T(8,128)(2,1)}) custom-call(s32[2]{0:T(128)} %get-tuple-element.12.counts, s32[1792]{0:T(1024)} %get-tuple-element.13.base, s32[1792]{0:T(1024)} %get-tuple-element.14.hits, s32[30720]{0:T(1024)} %get-tuple-element.17.items_in, ...), custom_call_target="tpu_custom_call" | custom-call | flops 20000000000 | bytes 33554432 | tf_op jit(solution)/shard_map/chunk_1/pallas_call | solution.py:394
  180.3 1.3 copy-done
  181.6 19.5 %all-to-all-start.4 = ((bf16[64,128,128]{2,1,0:T(8,128)(2,1)}), bf16[64,128,128]{2,1,0:T(8,128)(2,1)S(1)}, u32[]{:S(2)}, u32[]{:S(2)}) async-start(bf16[64,128,128]{2,1,0:T(8,128)(2,1)} %get-tuple-element.19), calls=%async_computation.4 | async-start | bytes 4194304 | tf_op jit(solution)/shard_map/all_to_all | solution.py:397
  201.1 6.0 %fusion.3 = (bf16[64,128,128]{2,1,0:T(8,128)(2,1)S(1)}, f32[64,128,128]{2,1,0:T(8,128)}) fusion(f32[64,128,128]{2,1,0:T(8,128)} %get-tuple-element.20, bf16[64,128,128]{2,1,0:T(8,128)(2,1)} %collective-permute-done.7), kind=kLoop, calls=%fused_computation.26 | loop fusion | flops 3145728 | bytes 12582912 | tf_op jit(solution)/shard_map/convert.5
  207.1 1.6 collective-permute-start.13
  208.8 0.3 convert_reduce_fusion.1
  209.1 2.7 %collective-permute-start.12 = (bf16[8,128,128]{2,1,0:T(8,128)(2,1)S(1)}, bf16[8,128,128]{2,1,0:T(8,128)(2,1)}, u32[]{:S(2)}, u32[]{:S(2)}) collective-permute-start(bf16[8,128,128]{2,1,0:T(8,128)(2,1)S(1)} %get-tuple-element.27), channel_id=1, source_target_pairs={{4,0},{8,4},{12,8},{0,12},{5,1},{9,5},{13,9},{1,13},{6,2},{10,6},{... | collective-permute-start | bytes 786440 | tf_op jit(solution)/shard_map/ppermute | solution.py:403
  211.8 1.5 collective-permute-start.11
  213.3 1.7 collective-permute-start.10
  215.0 1.5 collective-permute-start.9
  216.5 17.3 %collective-permute-done.13.rest_5_ = bf16[8,128,128]{2,1,0:T(8,128)(2,1)S(1)} collective-permute-done((bf16[8,128,128]{2,1,0:T(8,128)(2,1)S(1)}, bf16[8,128,128]{2,1,0:T(8,128)(2,1)S(1)}, u32[]{:S(2)}, u32[]{:S(2)}) %collective-permute-start.13) | collective-permute-done | bytes 262176 | tf_op jit(solution)/shard_map/ppermute | solution.py:403
  233.8 0.7 copy-done.10
  234.5 2.6 %collective-permute-start.8 = (bf16[8,128,128]{2,1,0:T(8,128)(2,1)S(1)}, bf16[8,128,128]{2,1,0:T(8,128)(2,1)}, u32[]{:S(2)}, u32[]{:S(2)}) collective-permute-start(bf16[8,128,128]{2,1,0:T(8,128)(2,1)S(1)} %get-tuple-element.31), channel_id=1, source_target_pairs={{1,0},{2,1},{3,2},{0,3},{5,4},{6,5},{7,6},{4,7},{9,8},{10,9},{11,1... | collective-permute-start | bytes 786440 | tf_op jit(solution)/shard_map/ppermute | solution.py:403
  237.5 0.7 pad_maximum_fusion.1
  238.1 2.3 slice.103.kept
  240.5 2.6 %collective-permute-done.8.rest_0_ = bf16[8,128,128]{2,1,0:T(8,128)(2,1)} collective-permute-done((bf16[8,128,128]{2,1,0:T(8,128)(2,1)S(1)}, bf16[8,128,128]{2,1,0:T(8,128)(2,1)}, u32[]{:S(2)}, u32[]{:S(2)}) %collective-permute-start.8) | collective-permute-done | bytes 262176 | tf_op jit(solution)/shard_map/ppermute | solution.py:403
  243.1 3.9 %assemble.1 = f32[64,128,128]{2,1,0:T(8,128)} custom-call(f32[16,128,128]{2,1,0:T(8,128)} %slice.103.kept, bf16[8,128,128]{2,1,0:T(8,128)(2,1)} %collective-permute-done.8.rest_0_, bf16[8,128,128]{2,1,0:T(8,128)(2,1)} %collective-permute-done.9.rest_1_, bf16[8,128,128]{2,1,0:T(8,128)(2,1)} %collective-permute-done.10.rest_2_, ...), custom_call_target="tpu_custom_call" | custom-call | flops 1000000 | bytes 8388608 | tf_op jit(solution)/shard_map/assemble/pallas_call | solution.py:415
  (46 shorter events, 0.8 us)
Async XLA Ops:
  12.2 17.6 %copy-start.11 = (bf16[256,128]{1,0:T(8,128)(2,1)S(1)}, bf16[256,128]{1,0:T(8,128)(2,1)}, u32[]{:S(2)}) copy-start(bf16[256,128]{1,0:T(8,128)(2,1)} %param.8) | copy-start | bytes 196612
  12.9 22.1 %all-to-all-start = ((f32[64,8,128]{2,1,0:T(8,128)}), f32[64,8,128]{2,1,0:T(8,128)S(1)}, u32[]{:S(2)}, u32[]{:S(2)}) async-start(f32[64,8,128]{2,1,0:T(8,128)} %pad_maximum_fusion), calls=%async_computation | async-start | bytes 524288 | tf_op jit(solution)/shard_map/all_to_all | solution.py:325
  26.7 22.1 %collective-permute-start.3 = (bf16[8,128,128]{2,1,0:T(8,128)(2,1)}, bf16[8,128,128]{2,1,0:T(8,128)(2,1)S(1)}, u32[]{:S(2)}, u32[]{:S(2)}) collective-permute-start(bf16[8,128,128]{2,1,0:T(8,128)(2,1)} %bitcast.11), channel_id=1, source_target_pairs={{0,96},{32,0},{64,32},{96,64},{1,97},{33,1},{65,33},{97,65},{2,98}... | collective-permute-start | bytes 786440 | tf_op jit(solution)/shard_map/ppermute | solution.py:291
  35.1 52.0 %copy-start.3 = (f32[64,8,128]{2,1,0:T(8,128)}, f32[64,8,128]{2,1,0:T(8,128)S(1)}, u32[]{:S(2)}) copy-start(f32[64,8,128]{2,1,0:T(8,128)S(1)} %all-to-all-done.rows_in) | copy-start | bytes 786436
  36.9 39.9 %all-to-all-start.1 = ((bf16[64,128,128]{2,1,0:T(8,128)(2,1)}), bf16[64,128,128]{2,1,0:T(8,128)(2,1)S(1)}, u32[]{:S(2)}, u32[]{:S(2)}) async-start(bf16[64,128,128]{2,1,0:T(8,128)(2,1)} %broadcast_in_dim.7), calls=%async_computation.1 | async-start | bytes 4194304 | tf_op jit(solution)/shard_map/all_to_all | solution.py:284
  41.8 28.7 %collective-permute-start.5 = (bf16[8,128,128]{2,1,0:T(8,128)(2,1)}, bf16[8,128,128]{2,1,0:T(8,128)(2,1)S(1)}, u32[]{:S(2)}, u32[]{:S(2)}) collective-permute-start(bf16[8,128,128]{2,1,0:T(8,128)(2,1)} %bitcast.43), channel_id=1, source_target_pairs={{0,12},{4,0},{8,4},{12,8},{1,13},{5,1},{9,5},{13,9},{2,14},{6,2},{... | collective-permute-start | bytes 786440 | tf_op jit(solution)/shard_map/ppermute | solution.py:291
  44.6 27.2 %collective-permute-start.2 = (bf16[8,128,128]{2,1,0:T(8,128)(2,1)}, bf16[8,128,128]{2,1,0:T(8,128)(2,1)S(1)}, u32[]{:S(2)}, u32[]{:S(2)}) collective-permute-start(bf16[8,128,128]{2,1,0:T(8,128)(2,1)} %bitcast.42), channel_id=1, source_target_pairs={{0,32},{32,64},{64,96},{96,0},{1,33},{33,65},{65,97},{97,1},{2,34}... | collective-permute-start | bytes 786440 | tf_op jit(solution)/shard_map/ppermute | solution.py:291
  46.2 25.7 %collective-permute-start.1 = (bf16[8,128,128]{2,1,0:T(8,128)(2,1)S(1)}, bf16[8,128,128]{2,1,0:T(8,128)(2,1)S(1)}, u32[]{:S(2)}, u32[]{:S(2)}) collective-permute-start(bf16[8,128,128]{2,1,0:T(8,128)(2,1)S(1)} %bitcast.41), channel_id=1, source_target_pairs={{0,3},{1,0},{2,1},{3,2},{4,7},{5,4},{6,5},{7,6},{8,11},{9,8},{10,9... | collective-permute-start | bytes 786440 | tf_op jit(solution)/shard_map/ppermute | solution.py:291
  48.9 23.0 %collective-permute-start = (bf16[8,128,128]{2,1,0:T(8,128)(2,1)S(1)}, bf16[8,128,128]{2,1,0:T(8,128)(2,1)S(1)}, u32[]{:S(2)}, u32[]{:S(2)}) collective-permute-start(bf16[8,128,128]{2,1,0:T(8,128)(2,1)S(1)} %bitcast.40), channel_id=1, source_target_pairs={{0,1},{1,2},{2,3},{3,0},{4,5},{5,6},{6,7},{7,4},{8,9},{9,10},{10,1... | collective-permute-start | bytes 786440 | tf_op jit(solution)/shard_map/ppermute | solution.py:291
  48.9 24.9 %copy-start.4 = (bf16[8,128,128]{2,1,0:T(8,128)(2,1)}, bf16[8,128,128]{2,1,0:T(8,128)(2,1)S(1)}, u32[]{:S(2)}) copy-start(bf16[8,128,128]{2,1,0:T(8,128)(2,1)S(1)} %collective-permute-done.3.rest_3_) | copy-start | bytes 786436
  48.9 24.2 %collective-permute-start.4 = (bf16[8,128,128]{2,1,0:T(8,128)(2,1)S(1)}, bf16[8,128,128]{2,1,0:T(8,128)(2,1)S(1)}, u32[]{:S(2)}, u32[]{:S(2)}) collective-permute-start(bf16[8,128,128]{2,1,0:T(8,128)(2,1)S(1)} %bitcast.39), channel_id=1, source_target_pairs={{0,4},{4,8},{8,12},{12,0},{1,5},{5,9},{9,13},{13,1},{2,6},{6,10},{... | collective-permute-start | bytes 786440 | tf_op jit(solution)/shard_map/ppermute | solution.py:291
  70.5 3.3 %copy-start.5 = (bf16[8,128,128]{2,1,0:T(8,128)(2,1)}, bf16[8,128,128]{2,1,0:T(8,128)(2,1)S(1)}, u32[]{:S(2)}) copy-start(bf16[8,128,128]{2,1,0:T(8,128)(2,1)S(1)} %collective-permute-done.5.rest_5_) | copy-start | bytes 786436
  71.9 1.9 copy-start.6
  71.9 1.2 copy-start.7
  71.9 1.2 copy-start.8
  73.1 0.7 copy-start.9
  76.8 23.8 %collective-permute-start.6 = (bf16[64,128,128]{2,1,0:T(8,128)(2,1)}, bf16[64,128,128]{2,1,0:T(8,128)(2,1)}, u32[]{:S(2)}, u32[]{:S(2)}) collective-permute-start(bf16[64,128,128]{2,1,0:T(8,128)(2,1)} %hold.1.own_in), channel_id=1, source_target_pairs={{0,16},{16,0},{1,17},{17,1},{2,18},{18,2},{3,19},{19,3},{4,20},{20... | collective-permute-start | bytes 6291464 | tf_op jit(solution)/shard_map/ppermute | solution.py:350
  76.8 2.0 copy-start.2
  78.8 49.2 %all-to-all-start.3 = ((bf16[64,128,128]{2,1,0:T(8,128)(2,1)}), bf16[64,128,128]{2,1,0:T(8,128)(2,1)}, u32[]{:S(2)}, u32[]{:S(2)}) async-start(bf16[64,128,128]{2,1,0:T(8,128)(2,1)} %broadcast_in_dim.8), calls=%async_computation.3 | async-start | bytes 4194304 | tf_op jit(solution)/shard_map/all_to_all | solution.py:284
  128.0 52.2 %all-to-all-start.2 = ((bf16[64,128,128]{2,1,0:T(8,128)(2,1)}), bf16[64,128,128]{2,1,0:T(8,128)(2,1)S(1)}, u32[]{:S(2)}, u32[]{:S(2)}) async-start(bf16[64,128,128]{2,1,0:T(8,128)(2,1)} %get-tuple-element.16), calls=%async_computation.2 | async-start | bytes 4194304 | tf_op jit(solution)/shard_map/all_to_all | solution.py:397
  180.2 20.9 %collective-permute-start.7 = (bf16[64,128,128]{2,1,0:T(8,128)(2,1)}, bf16[64,128,128]{2,1,0:T(8,128)(2,1)}, u32[]{:S(2)}, u32[]{:S(2)}) collective-permute-start(bf16[64,128,128]{2,1,0:T(8,128)(2,1)} %get-tuple-element.21), channel_id=1, source_target_pairs={{0,16},{16,0},{1,17},{17,1},{2,18},{18,2},{3,19},{19,3},{4,20},{20... | collective-permute-start | bytes 6291464 | tf_op jit(solution)/shard_map/ppermute | solution.py:400
  180.3 1.3 copy-start
  181.6 55.6 %all-to-all-start.4 = ((bf16[64,128,128]{2,1,0:T(8,128)(2,1)}), bf16[64,128,128]{2,1,0:T(8,128)(2,1)S(1)}, u32[]{:S(2)}, u32[]{:S(2)}) async-start(bf16[64,128,128]{2,1,0:T(8,128)(2,1)} %get-tuple-element.19), calls=%async_computation.4 | async-start | bytes 4194304 | tf_op jit(solution)/shard_map/all_to_all | solution.py:397
  207.0 1.8 copy-start.1
  207.1 26.7 %collective-permute-start.13 = (bf16[8,128,128]{2,1,0:T(8,128)(2,1)S(1)}, bf16[8,128,128]{2,1,0:T(8,128)(2,1)S(1)}, u32[]{:S(2)}, u32[]{:S(2)}) collective-permute-start(bf16[8,128,128]{2,1,0:T(8,128)(2,1)S(1)} %get-tuple-element.26), channel_id=1, source_target_pairs={{12,0},{0,4},{4,8},{8,12},{13,1},{1,5},{5,9},{9,13},{14,2},{2,6},{... | collective-permute-start | bytes 786440 | tf_op jit(solution)/shard_map/ppermute | solution.py:403
  209.1 31.4 %collective-permute-start.12 = (bf16[8,128,128]{2,1,0:T(8,128)(2,1)S(1)}, bf16[8,128,128]{2,1,0:T(8,128)(2,1)}, u32[]{:S(2)}, u32[]{:S(2)}) collective-permute-start(bf16[8,128,128]{2,1,0:T(8,128)(2,1)S(1)} %get-tuple-element.27), channel_id=1, source_target_pairs={{4,0},{8,4},{12,8},{0,12},{5,1},{9,5},{13,9},{1,13},{6,2},{10,6},{... | collective-permute-start | bytes 786440 | tf_op jit(solution)/shard_map/ppermute | solution.py:403
  211.8 28.7 %collective-permute-start.11 = (bf16[8,128,128]{2,1,0:T(8,128)(2,1)S(1)}, bf16[8,128,128]{2,1,0:T(8,128)(2,1)}, u32[]{:S(2)}, u32[]{:S(2)}) collective-permute-start(bf16[8,128,128]{2,1,0:T(8,128)(2,1)S(1)} %get-tuple-element.28), channel_id=1, source_target_pairs={{96,0},{0,32},{32,64},{64,96},{97,1},{1,33},{33,65},{65,97},{98,2}... | collective-permute-start | bytes 786440 | tf_op jit(solution)/shard_map/ppermute | solution.py:403
  213.3 27.2 %collective-permute-start.10 = (bf16[8,128,128]{2,1,0:T(8,128)(2,1)S(1)}, bf16[8,128,128]{2,1,0:T(8,128)(2,1)}, u32[]{:S(2)}, u32[]{:S(2)}) collective-permute-start(bf16[8,128,128]{2,1,0:T(8,128)(2,1)S(1)} %get-tuple-element.29), channel_id=1, source_target_pairs={{32,0},{64,32},{96,64},{0,96},{33,1},{65,33},{97,65},{1,97},{34,2}... | collective-permute-start | bytes 786440 | tf_op jit(solution)/shard_map/ppermute | solution.py:403
  215.0 25.5 %collective-permute-start.9 = (bf16[8,128,128]{2,1,0:T(8,128)(2,1)S(1)}, bf16[8,128,128]{2,1,0:T(8,128)(2,1)}, u32[]{:S(2)}, u32[]{:S(2)}) collective-permute-start(bf16[8,128,128]{2,1,0:T(8,128)(2,1)S(1)} %get-tuple-element.30), channel_id=1, source_target_pairs={{3,0},{0,1},{1,2},{2,3},{7,4},{4,5},{5,6},{6,7},{11,8},{8,9},{9,10... | collective-permute-start | bytes 786440 | tf_op jit(solution)/shard_map/ppermute | solution.py:403
  233.8 0.7 copy-start.10
  234.5 8.6 %collective-permute-start.8 = (bf16[8,128,128]{2,1,0:T(8,128)(2,1)S(1)}, bf16[8,128,128]{2,1,0:T(8,128)(2,1)}, u32[]{:S(2)}, u32[]{:S(2)}) collective-permute-start(bf16[8,128,128]{2,1,0:T(8,128)(2,1)S(1)} %get-tuple-element.31), channel_id=1, source_target_pairs={{1,0},{2,1},{3,2},{0,3},{5,4},{6,5},{7,6},{4,7},{9,8},{10,9},{11,1... | collective-permute-start | bytes 786440 | tf_op jit(solution)/shard_map/ppermute | solution.py:403

commit v6 on v5

--- a/solution.py
+++ b/solution.py
@@ -68,7 +68,7 @@
     lax.fori_loop(0, owner.shape[0], ask, 0, unroll=4)
 
 
-def list_kernel(table, first_items, second_items, counts, base, hits, live):
+def list_kernel(table, first_out, second_out, counts, base, hits, live, first_items, second_items, sems):
     groups = 4
     sources = table.shape[0]
     in_group = sources // groups
@@ -115,7 +115,18 @@
     for h in range(2):
         for i in range(4 * UNROLL):
             lists[h][ends[h] + i] = dead
-        counts[h] = (ends[h] + 2 * UNROLL - 1) // (2 * UNROLL)
+        count = (ends[h] + 2 * UNROLL - 1) // (2 * UNROLL)
+        counts[h] = count
+        target = (first_out, second_out)[h]
+
+        def store_items(i, carry, h=h, target=target):
+            at = pl.ds(pl.multiple_of(i * PIECE, PIECE), PIECE)
+            piece = pltpu.make_async_copy(lists[h].at[at], target.at[at], sems.at[h])
+            piece.start()
+            piece.wait()
+            return carry
+
+        lax.fori_loop(0, (2 * UNROLL * (count + 1) + PIECE - 1) // PIECE, store_items, 0)
 
 
 def chunk_kernel(h, last, counts, base, hits, items_in, rows_in, q_in, own_in, mate_in, *rest):
@@ -123,7 +134,7 @@
         earlier_in, query_out, own_out, mate_out, earlier, mate_acc = rest[:6]
     else:
         query_out, block_out = rest[:2]
-    items, rows, q, blocks, query_acc, block_acc, scores, sems = rest[-8:]
+    items, rows, q, blocks, query_acc, block_acc, scores, query_grad, sems = rest[-9:]
     scale = 2.0 / math.sqrt(q.shape[2])
     factor = scale * math.log2(math.e)
     tiles = q_in.shape[0]
@@ -244,10 +255,15 @@
         store.start()
 
     def finish(t, carry):
-        query_out[t] = (query_acc[t] * scale).T.astype(jnp.bfloat16)
-        return carry
-
-    lax.fori_loop(0, tiles, finish, 0, unroll=4)
+        query_grad[t] = (query_acc[t] * scale).T.astype(jnp.bfloat16)
+        return carry
+
+    part = tiles // 4
+    for k in range(4):
+        lax.fori_loop(k * part, (k + 1) * part, finish, 0, unroll=4)
+        at = pl.ds(k * part, part)
+        stores.append(pltpu.make_async_copy(query_grad.at[at], query_out.at[at], sems.at[8 + k]))
+        stores[-1].start()
     for store in stores:
         store.wait()
 
@@ -259,11 +275,23 @@
         out[pl.ds(KEPT + SLAB * k, SLAB)] = part[...]
 
 
-def assemble_kernel(kept, *rest):
-    *back, out = rest
-    out[pl.ds(0, KEPT)] = kept[...]
+def assemble_kernel(held, *rest):
+    *back, out, built, sems = rest
+    at = pl.ds(0, KEPT)
+    kept = pltpu.make_async_copy(held.at[at], built.at[at], sems.at[0])
+    kept.start()
+    stores = []
     for k, part in enumerate(back):
-        out[pl.ds(KEPT + SLAB * k, SLAB)] = part[...].astype(jnp.float32)
+        at = pl.ds(KEPT + SLAB * k, SLAB)
+        built[at] = part[...].astype(jnp.float32)
+        stores.append(pltpu.make_async_copy(built.at[at], out.at[at], sems.at[1 + k]))
+        stores[-1].start()
+    kept.wait()
+    at = pl.ds(0, KEPT)
+    stores.append(pltpu.make_async_copy(built.at[at], out.at[at], sems.at[1 + len(back)]))
+    stores[-1].start()
+    for store in stores:
+        store.wait()
 
 
 def shard_work(
@@ -292,6 +320,7 @@
     kept = stored[:KEPT]
     smem = pl.BlockSpec(memory_space=pltpu.SMEM)
     vmem = pl.BlockSpec(memory_space=pltpu.VMEM)
+    hbm = pl.BlockSpec(memory_space=pltpu.HBM)
     limit = pltpu.CompilerParams(vmem_limit_bytes=VMEM_LIMIT)
     owners = fetch_owner[:, 0]
     fetch_count = owners.shape[0]
@@ -331,8 +360,13 @@
         list_kernel,
         out_shape=(list_shape, list_shape, jax.ShapeDtypeStruct((2,), jnp.int32), entry_shape, entry_shape),
         in_specs=[smem],
-        out_specs=(smem,) * 5,
-        scratch_shapes=[pltpu.SMEM(entry_shape.shape, jnp.int32)],
+        out_specs=(hbm, hbm) + (smem,) * 3,
+        scratch_shapes=[
+            pltpu.SMEM(entry_shape.shape, jnp.int32),
+            pltpu.SMEM((most,), jnp.int32),
+            pltpu.SMEM((most,), jnp.int32),
+            pltpu.SemaphoreType.DMA((2,)),
+        ],
         cost_estimate=pl.CostEstimate(flops=10**9, bytes_accessed=2**20, transcendentals=0),
         name="listing",
     )
@@ -363,16 +397,16 @@
             pltpu.VMEM((sources + 1, feat_width, QTILE), jnp.float32),
             pltpu.VMEM(acc_shape.shape, jnp.float32),
             pltpu.VMEM((UNROLL, BLOCK, 2 * QTILE), jnp.float32),
-            pltpu.SemaphoreType.DMA((8,)),
+            pltpu.VMEM(grad_shape.shape, jnp.bfloat16),
+            pltpu.SemaphoreType.DMA((12,)),
         ]
 
-    hbm = pl.BlockSpec(memory_space=pl.ANY)
     cost = pl.CostEstimate(flops=2 * 10**10, bytes_accessed=2**25, transcendentals=10**7)
     chunk_0 = pl.pallas_call(
         functools.partial(chunk_kernel, 0, False),
         out_shape=(grad_shape, acc_shape),
         in_specs=[smem] * 3 + [hbm] * 5,
-        out_specs=(vmem, hbm),
+        out_specs=(hbm, hbm),
         scratch_shapes=scratch([]),
         compiler_params=limit,
         cost_estimate=cost,
@@ -383,7 +417,7 @@
         functools.partial(chunk_kernel, 1, True),
         out_shape=(grad_shape, own_shape, mate_shape),
         in_specs=[smem] * 3 + [hbm] * 6,
-        out_specs=(vmem, hbm, hbm),
+        out_specs=(hbm, hbm, hbm),
         scratch_shapes=scratch(
             [pltpu.VMEM(acc_shape.shape, jnp.float32), pltpu.VMEM(mate_shape.shape, jnp.bfloat16)]
         ),
@@ -406,13 +440,17 @@
     assemble = pl.pallas_call(
         assemble_kernel,
         out_shape=own_shape,
-        in_specs=[vmem] * (1 + len(back)),
-        out_specs=vmem,
+        in_specs=[hbm] + [vmem] * len(back),
+        out_specs=hbm,
+        scratch_shapes=[
+            pltpu.VMEM(own_shape.shape, jnp.float32),
+            pltpu.SemaphoreType.DMA((2 + len(back),)),
+        ],
         compiler_params=limit,
         cost_estimate=pl.CostEstimate(flops=10**6, bytes_accessed=2**23, transcendentals=0),
         name="assemble",
     )
-    index_grad = assemble(held_grad[:KEPT], *back)
+    index_grad = assemble(held_grad, *back)
     return (query_grad, index_grad.reshape(blocks_here * BLOCK, feat_width))
 
 

time: 249 us -> 245 us (0.984)
  Pallas kernels: 81.5 us -> 78 us
    pallas_call x1, Pallas kernels: 12.9 us -> 10.2 us  [shard_work(): *items, counts, base, hits = listing(table)]
  transfers between devices with their start and end apart: 19 -> 19, of which waited for: 6 -> 6; matrix products, arithmetic and copies ran while one was open for 7% -> 7% of each run, Pallas kernels for 29% -> 28%
where the time goes in v6:
time: 245 us; the launch traced here: 243 us
  starting transfers between devices  88 us (36%)
  Pallas kernels  78 us (32%)
  waiting for transfers between devices  49.7 us (20%)
  other arithmetic  14.6 us (6%)
  local copies, waits for them, and re-layouts  11.7 us (5%)
    all_to_all x2, starting transfers between devices, shard_work(): came = lax.all_to_all(part, SAME_CORE, 0, 0, tiled=True)  42.1 us
    pallas_call x1, Pallas kernels, shard_work(): chunk_1(counts, base, hits, items[1], rows, halves[1], held, mate_held, acc)  29 us
    pallas_call x1, Pallas kernels, shard_work(): chunk_0(counts, base, hits, items[0], rows, halves[0], held, mate_held)  26.7 us
    ppermute x6, waiting for transfers between devices, shard_work(): lax.ppermute(stored[at], axis, way)  22.2 us
    ppermute x6, waiting for transfers between devices, shard_work(): lax.ppermute(held_grad[at].astype(jnp.bfloat16), axis, [(j, i) for i, j i...  22.1 us
    all_to_all x2, starting transfers between devices, shard_work(): halves.append(lax.all_to_all(spread, SAME_CORE, 0, 0, tiled=True))  13.1 us
    all_to_all x1, starting transfers between devices, shard_work(): rows = lax.all_to_all(packed, SAME_CORE, 0, 0, tiled=True)  11.5 us
    ppermute x6, starting transfers between devices, shard_work(): lax.ppermute(held_grad[at].astype(jnp.bfloat16), axis, [(j, i) for i, j i...  11.1 us
  transfers between devices with their start and end apart: 19, of which 6 were waited for; matrix products, arithmetic and copies ran while one was open for 7% of the time, Pallas kernels for 28%

profile of v6, /device:TPU:0, one launch (start us, length us, event | category | flops | bytes accessed | tf_op | source)
XLA Modules:
  0.0 243.0 jit_solution(410699752788431508)
XLA Ops:
  0.6 0.7 add_select_fusion
  1.4 0.8 convert_bitcast_fusion
  2.1 1.5 compare_reduce_fusion
  3.7 0.7 compare_reduce_fusion.1
  4.4 0.7 pad_add_fusion.where
  5.1 0.6 shift-left_reduce_fusion
  5.6 4.8 %ask.1 = s32[64,256]{1,0:T(8,128)} custom-call(s32[2]{0:T(128)} %pad_add_fusion.where, s32[64]{0:T(128)} %bitcast.46, s32[64]{0:T(128)} %local.1, s32[64]{0:T(128)} %get-tuple-element.23.hits, s32[64]{0:T(128)} %get-tuple-element.22.lives), custom_call_target="tpu_custom_call" | custom-call | flops 1000000 | bytes 65536 | tf_op jit(solution)/shard_map/ask/pallas_call | solution.py:343
  10.4 0.8 convert_element_type.33
  11.3 0.8 subtract_bitcast_fusion
  12.1 0.8 pad_maximum_fusion
  12.9 11.5 %all-to-all-start = ((f32[64,8,128]{2,1,0:T(8,128)}), f32[64,8,128]{2,1,0:T(8,128)S(1)}, u32[]{:S(2)}, u32[]{:S(2)}) async-start(f32[64,8,128]{2,1,0:T(8,128)} %pad_maximum_fusion), calls=%async_computation | async-start | bytes 524288 | tf_op jit(solution)/shard_map/all_to_all | solution.py:354
  24.4 2.3 fusion.5
  26.7 3.0 %collective-permute-start.3 = (bf16[8,128,128]{2,1,0:T(8,128)(2,1)}, bf16[8,128,128]{2,1,0:T(8,128)(2,1)S(1)}, u32[]{:S(2)}, u32[]{:S(2)}) collective-permute-start(bf16[8,128,128]{2,1,0:T(8,128)(2,1)} %bitcast.11), channel_id=1, source_target_pairs={{0,96},{32,0},{64,32},{96,64},{1,97},{33,1},{65,33},{97,65},{2,98}... | collective-permute-start | bytes 786440 | tf_op jit(solution)/shard_map/ppermute | solution.py:319
  29.7 5.3 %all-to-all-done.rows_in = f32[64,8,128]{2,1,0:T(8,128)S(1)} async-done(((f32[64,8,128]{2,1,0:T(8,128)}), f32[64,8,128]{2,1,0:T(8,128)S(1)}, u32[]{:S(2)}, u32[]{:S(2)}) %all-to-all-start) | async-done | bytes 262176 | tf_op jit(solution)/shard_map/all_to_all | solution.py:354
  35.0 1.8 broadcast_in_dim.7
  36.9 4.9 %all-to-all-start.1 = ((bf16[64,128,128]{2,1,0:T(8,128)(2,1)}), bf16[64,128,128]{2,1,0:T(8,128)(2,1)S(1)}, u32[]{:S(2)}, u32[]{:S(2)}) async-start(bf16[64,128,128]{2,1,0:T(8,128)(2,1)} %broadcast_in_dim.7), calls=%async_computation.1 | async-start | bytes 4194304 | tf_op jit(solution)/shard_map/all_to_all | solution.py:312
  41.7 2.9 %collective-permute-start.5 = (bf16[8,128,128]{2,1,0:T(8,128)(2,1)}, bf16[8,128,128]{2,1,0:T(8,128)(2,1)S(1)}, u32[]{:S(2)}, u32[]{:S(2)}) collective-permute-start(bf16[8,128,128]{2,1,0:T(8,128)(2,1)} %bitcast.43), channel_id=1, source_target_pairs={{0,12},{4,0},{8,4},{12,8},{1,13},{5,1},{9,5},{13,9},{2,14},{6,2},{... | collective-permute-start | bytes 786440 | tf_op jit(solution)/shard_map/ppermute | solution.py:319
  44.6 1.5 collective-permute-start.2
  46.1 2.7 %collective-permute-start.1 = (bf16[8,128,128]{2,1,0:T(8,128)(2,1)S(1)}, bf16[8,128,128]{2,1,0:T(8,128)(2,1)S(1)}, u32[]{:S(2)}, u32[]{:S(2)}) collective-permute-start(bf16[8,128,128]{2,1,0:T(8,128)(2,1)S(1)} %bitcast.41), channel_id=1, source_target_pairs={{0,3},{1,0},{2,1},{3,2},{4,7},{5,4},{6,5},{7,6},{8,11},{9,8},{10,9... | collective-permute-start | bytes 786440 | tf_op jit(solution)/shard_map/ppermute | solution.py:319
  48.9 1.9 slice.77
  50.8 19.6 %collective-permute-done.5.rest_5_ = bf16[8,128,128]{2,1,0:T(8,128)(2,1)S(1)} collective-permute-done((bf16[8,128,128]{2,1,0:T(8,128)(2,1)}, bf16[8,128,128]{2,1,0:T(8,128)(2,1)S(1)}, u32[]{:S(2)}, u32[]{:S(2)}) %collective-permute-start.5) | collective-permute-done | bytes 262176 | tf_op jit(solution)/shard_map/ppermute | solution.py:319
  70.4 1.4 collective-permute-done.2.rest_2_
  71.9 1.2 collective-permute-done.4.rest_4_
  73.0 0.7 copy-done.11
  73.7 3.0 %hold.1.own_in = bf16[64,128,128]{2,1,0:T(8,128)(2,1)} custom-call(bf16[16,128,128]{2,1,0:T(8,128)(2,1)} %bitcast.38, bf16[8,128,128]{2,1,0:T(8,128)(2,1)} %copy-done.10, bf16[8,128,128]{2,1,0:T(8,128)(2,1)} %copy-done.9, bf16[8,128,128]{2,1,0:T(8,128)(2,1)} %copy-done.8, bf16[8,128,128]{2,1,0:T(8,128)(2,1)} %copy-done.4, bf16[8,128,128]{2,1,0:T(8,128)(2,1)} %copy-done.11, ...), custom_call_target="tpu_custom_call" | custom-call | flops 1000000 | bytes 4194304 | tf_op jit(solution)/shard_map/hold/pallas_call | solution.py:383
  76.8 2.0 broadcast_in_dim.8
  78.8 8.3 %all-to-all-start.3 = ((bf16[64,128,128]{2,1,0:T(8,128)(2,1)}), bf16[64,128,128]{2,1,0:T(8,128)(2,1)}, u32[]{:S(2)}, u32[]{:S(2)}) async-start(bf16[64,128,128]{2,1,0:T(8,128)(2,1)} %broadcast_in_dim.8), calls=%async_computation.3 | async-start | bytes 4194304 | tf_op jit(solution)/shard_map/all_to_all | solution.py:312
  87.1 0.6 copy.12
  87.7 10.2 %listing.1 = (s32[30720]{0:T(1024)}, s32[30720]{0:T(1024)}, s32[2]{0:T(128)}, s32[1792]{0:T(1024)}, s32[1792]{0:T(1024)}) custom-call(s32[64,256]{1,0:T(8,128)} %bitcast.45), custom_call_target="tpu_custom_call" | custom-call | flops 1000000000 | bytes 1048576 | tf_op jit(solution)/shard_map/listing/pallas_call | solution.py:373
  97.9 26.7 %chunk_0.1 = (bf16[64,128,128]{2,1,0:T(8,128)(2,1)}, f32[128,128,128]{2,1,0:T(8,128)}) custom-call(s32[2]{0:T(128)} %get-tuple-element.12.counts, s32[1792]{0:T(1024)} %get-tuple-element.13.base, s32[1792]{0:T(1024)} %get-tuple-element.14.hits, s32[30720]{0:T(1024)} %get-tuple-element.15.items_in, f32[64,8,128]{2,1,0:T(8,128)} %copy-done.3, ...), custom_call_target="tpu_custom_call" | custom-call | flops 20000000000 | bytes 33554432 | tf_op jit(solution)/shard_map/chunk_0/pallas_call | solution.py:415
  124.6 22.6 %all-to-all-start.2 = ((bf16[64,128,128]{2,1,0:T(8,128)(2,1)}), bf16[64,128,128]{2,1,0:T(8,128)(2,1)S(1)}, u32[]{:S(2)}, u32[]{:S(2)}) async-start(bf16[64,128,128]{2,1,0:T(8,128)(2,1)} %get-tuple-element.16), calls=%async_computation.2 | async-start | bytes 4194304 | tf_op jit(solution)/shard_map/all_to_all | solution.py:431
  147.3 29.0 %chunk_1.1 = (bf16[64,128,128]{2,1,0:T(8,128)(2,1)}, f32[64,128,128]{2,1,0:T(8,128)}, bf16[64,128,128]{2,1,0:T(8,128)(2,1)}) custom-call(s32[2]{0:T(128)} %get-tuple-element.12.counts, s32[1792]{0:T(1024)} %get-tuple-element.13.base, s32[1792]{0:T(1024)} %get-tuple-element.14.hits, s32[30720]{0:T(1024)} %get-tuple-element.17.items_in, ...), custom_call_target="tpu_custom_call" | custom-call | flops 20000000000 | bytes 33554432 | tf_op jit(solution)/shard_map/chunk_1/pallas_call | solution.py:428
  176.4 1.3 copy-done
  177.8 19.5 %all-to-all-start.4 = ((bf16[64,128,128]{2,1,0:T(8,128)(2,1)}), bf16[64,128,128]{2,1,0:T(8,128)(2,1)S(1)}, u32[]{:S(2)}, u32[]{:S(2)}) async-start(bf16[64,128,128]{2,1,0:T(8,128)(2,1)} %get-tuple-element.19), calls=%async_computation.4 | async-start | bytes 4194304 | tf_op jit(solution)/shard_map/all_to_all | solution.py:431
  197.2 5.9 %fusion.3 = (bf16[64,128,128]{2,1,0:T(8,128)(2,1)S(1)}, f32[64,128,128]{2,1,0:T(8,128)}) fusion(f32[64,128,128]{2,1,0:T(8,128)} %get-tuple-element.20, bf16[64,128,128]{2,1,0:T(8,128)(2,1)} %collective-permute-done.7), kind=kLoop, calls=%fused_computation.26 | loop fusion | flops 3145728 | bytes 12582912 | tf_op jit(solution)/shard_map/convert.5
  203.1 0.9 fusion.4
  204.0 1.6 collective-permute-start.13
  205.6 0.3 convert_reduce_fusion.1
  205.9 2.2 collective-permute-start.12
  208.1 1.5 collective-permute-start.11
  209.6 1.7 collective-permute-start.10
  211.3 1.5 collective-permute-start.9
  212.8 17.2 %collective-permute-done.13.rest_5_ = bf16[8,128,128]{2,1,0:T(8,128)(2,1)S(1)} collective-permute-done((bf16[8,128,128]{2,1,0:T(8,128)(2,1)S(1)}, bf16[8,128,128]{2,1,0:T(8,128)(2,1)S(1)}, u32[]{:S(2)}, u32[]{:S(2)}) %collective-permute-start.13) | collective-permute-done | bytes 262176 | tf_op jit(solution)/shard_map/ppermute | solution.py:437
  230.0 2.7 %collective-permute-start.8 = (bf16[8,128,128]{2,1,0:T(8,128)(2,1)S(1)}, bf16[8,128,128]{2,1,0:T(8,128)(2,1)}, u32[]{:S(2)}, u32[]{:S(2)}) collective-permute-start(bf16[8,128,128]{2,1,0:T(8,128)(2,1)S(1)} %get-tuple-element.31), channel_id=1, source_target_pairs={{1,0},{2,1},{3,2},{0,3},{5,4},{6,5},{7,6},{4,7},{9,8},{10,9},{11,1... | collective-permute-start | bytes 786440 | tf_op jit(solution)/shard_map/ppermute | solution.py:437
  232.6 0.3 convert_reduce_fusion
  232.9 0.7 pad_maximum_fusion.1
  233.6 4.9 %collective-permute-done.8.rest_0_ = bf16[8,128,128]{2,1,0:T(8,128)(2,1)} collective-permute-done((bf16[8,128,128]{2,1,0:T(8,128)(2,1)S(1)}, bf16[8,128,128]{2,1,0:T(8,128)(2,1)}, u32[]{:S(2)}, u32[]{:S(2)}) %collective-permute-start.8) | collective-permute-done | bytes 262176 | tf_op jit(solution)/shard_map/ppermute | solution.py:437
  238.6 4.3 %assemble.1 = f32[64,128,128]{2,1,0:T(8,128)} custom-call(f32[64,128,128]{2,1,0:T(8,128)} %get-tuple-element.25.held, bf16[8,128,128]{2,1,0:T(8,128)(2,1)} %collective-permute-done.8.rest_0_, bf16[8,128,128]{2,1,0:T(8,128)(2,1)} %collective-permute-done.9.rest_1_, bf16[8,128,128]{2,1,0:T(8,128)(2,1)} %collective-permute-done.10.rest_2_, ...), custom_call_target="tpu_custom_call" | custom-call | flops 1000000 | bytes 8388608 | tf_op jit(solution)/shard_map/assemble/pallas_call | solution.py:453
  (47 shorter events, 0.4 us)
Async XLA Ops:
  12.1 17.6 %copy-start.12 = (bf16[256,128]{1,0:T(8,128)(2,1)S(1)}, bf16[256,128]{1,0:T(8,128)(2,1)}, u32[]{:S(2)}) copy-start(bf16[256,128]{1,0:T(8,128)(2,1)} %param.8) | copy-start | bytes 196612
  12.9 22.1 %all-to-all-start = ((f32[64,8,128]{2,1,0:T(8,128)}), f32[64,8,128]{2,1,0:T(8,128)S(1)}, u32[]{:S(2)}, u32[]{:S(2)}) async-start(f32[64,8,128]{2,1,0:T(8,128)} %pad_maximum_fusion), calls=%async_computation | async-start | bytes 524288 | tf_op jit(solution)/shard_map/all_to_all | solution.py:354
  26.7 22.1 %collective-permute-start.3 = (bf16[8,128,128]{2,1,0:T(8,128)(2,1)}, bf16[8,128,128]{2,1,0:T(8,128)(2,1)S(1)}, u32[]{:S(2)}, u32[]{:S(2)}) collective-permute-start(bf16[8,128,128]{2,1,0:T(8,128)(2,1)} %bitcast.11), channel_id=1, source_target_pairs={{0,96},{32,0},{64,32},{96,64},{1,97},{33,1},{65,33},{97,65},{2,98}... | collective-permute-start | bytes 786440 | tf_op jit(solution)/shard_map/ppermute | solution.py:319
  35.0 52.0 %copy-start.3 = (f32[64,8,128]{2,1,0:T(8,128)}, f32[64,8,128]{2,1,0:T(8,128)S(1)}, u32[]{:S(2)}) copy-start(f32[64,8,128]{2,1,0:T(8,128)S(1)} %all-to-all-done.rows_in) | copy-start | bytes 786436
  36.9 39.9 %all-to-all-start.1 = ((bf16[64,128,128]{2,1,0:T(8,128)(2,1)}), bf16[64,128,128]{2,1,0:T(8,128)(2,1)S(1)}, u32[]{:S(2)}, u32[]{:S(2)}) async-start(bf16[64,128,128]{2,1,0:T(8,128)(2,1)} %broadcast_in_dim.7), calls=%async_computation.1 | async-start | bytes 4194304 | tf_op jit(solution)/shard_map/all_to_all | solution.py:312
  41.7 28.7 %collective-permute-start.5 = (bf16[8,128,128]{2,1,0:T(8,128)(2,1)}, bf16[8,128,128]{2,1,0:T(8,128)(2,1)S(1)}, u32[]{:S(2)}, u32[]{:S(2)}) collective-permute-start(bf16[8,128,128]{2,1,0:T(8,128)(2,1)} %bitcast.43), channel_id=1, source_target_pairs={{0,12},{4,0},{8,4},{12,8},{1,13},{5,1},{9,5},{13,9},{2,14},{6,2},{... | collective-permute-start | bytes 786440 | tf_op jit(solution)/shard_map/ppermute | solution.py:319
  44.6 27.2 %collective-permute-start.2 = (bf16[8,128,128]{2,1,0:T(8,128)(2,1)}, bf16[8,128,128]{2,1,0:T(8,128)(2,1)S(1)}, u32[]{:S(2)}, u32[]{:S(2)}) collective-permute-start(bf16[8,128,128]{2,1,0:T(8,128)(2,1)} %bitcast.42), channel_id=1, source_target_pairs={{0,32},{32,64},{64,96},{96,0},{1,33},{33,65},{65,97},{97,1},{2,34}... | collective-permute-start | bytes 786440 | tf_op jit(solution)/shard_map/ppermute | solution.py:319
  46.1 25.7 %collective-permute-start.1 = (bf16[8,128,128]{2,1,0:T(8,128)(2,1)S(1)}, bf16[8,128,128]{2,1,0:T(8,128)(2,1)S(1)}, u32[]{:S(2)}, u32[]{:S(2)}) collective-permute-start(bf16[8,128,128]{2,1,0:T(8,128)(2,1)S(1)} %bitcast.41), channel_id=1, source_target_pairs={{0,3},{1,0},{2,1},{3,2},{4,7},{5,4},{6,5},{7,6},{8,11},{9,8},{10,9... | collective-permute-start | bytes 786440 | tf_op jit(solution)/shard_map/ppermute | solution.py:319
  48.8 23.0 %collective-permute-start = (bf16[8,128,128]{2,1,0:T(8,128)(2,1)S(1)}, bf16[8,128,128]{2,1,0:T(8,128)(2,1)S(1)}, u32[]{:S(2)}, u32[]{:S(2)}) collective-permute-start(bf16[8,128,128]{2,1,0:T(8,128)(2,1)S(1)} %bitcast.40), channel_id=1, source_target_pairs={{0,1},{1,2},{2,3},{3,0},{4,5},{5,6},{6,7},{7,4},{8,9},{9,10},{10,1... | collective-permute-start | bytes 786440 | tf_op jit(solution)/shard_map/ppermute | solution.py:319
  48.8 24.9 %copy-start.4 = (bf16[8,128,128]{2,1,0:T(8,128)(2,1)}, bf16[8,128,128]{2,1,0:T(8,128)(2,1)S(1)}, u32[]{:S(2)}) copy-start(bf16[8,128,128]{2,1,0:T(8,128)(2,1)S(1)} %collective-permute-done.3.rest_3_) | copy-start | bytes 786436
  48.8 24.2 %collective-permute-start.4 = (bf16[8,128,128]{2,1,0:T(8,128)(2,1)S(1)}, bf16[8,128,128]{2,1,0:T(8,128)(2,1)S(1)}, u32[]{:S(2)}, u32[]{:S(2)}) collective-permute-start(bf16[8,128,128]{2,1,0:T(8,128)(2,1)S(1)} %bitcast.39), channel_id=1, source_target_pairs={{0,4},{4,8},{8,12},{12,0},{1,5},{5,9},{9,13},{13,1},{2,6},{6,10},{... | collective-permute-start | bytes 786440 | tf_op jit(solution)/shard_map/ppermute | solution.py:319
  70.4 3.3 %copy-start.7 = (bf16[8,128,128]{2,1,0:T(8,128)(2,1)}, bf16[8,128,128]{2,1,0:T(8,128)(2,1)S(1)}, u32[]{:S(2)}) copy-start(bf16[8,128,128]{2,1,0:T(8,128)(2,1)S(1)} %collective-permute-done.5.rest_5_) | copy-start | bytes 786436
  71.8 1.9 copy-start.8
  71.8 1.2 copy-start.9
  71.8 1.2 copy-start.10
  73.0 0.7 copy-start.11
  76.8 21.2 %collective-permute-start.6 = (bf16[64,128,128]{2,1,0:T(8,128)(2,1)}, bf16[64,128,128]{2,1,0:T(8,128)(2,1)}, u32[]{:S(2)}, u32[]{:S(2)}) collective-permute-start(bf16[64,128,128]{2,1,0:T(8,128)(2,1)} %hold.1.own_in), channel_id=1, source_target_pairs={{0,16},{16,0},{1,17},{17,1},{2,18},{18,2},{3,19},{19,3},{4,20},{20... | collective-permute-start | bytes 6291464 | tf_op jit(solution)/shard_map/ppermute | solution.py:384
  76.8 2.0 copy-start.2
  78.8 45.8 %all-to-all-start.3 = ((bf16[64,128,128]{2,1,0:T(8,128)(2,1)}), bf16[64,128,128]{2,1,0:T(8,128)(2,1)}, u32[]{:S(2)}, u32[]{:S(2)}) async-start(bf16[64,128,128]{2,1,0:T(8,128)(2,1)} %broadcast_in_dim.8), calls=%async_computation.3 | async-start | bytes 4194304 | tf_op jit(solution)/shard_map/all_to_all | solution.py:312
  124.6 51.8 %all-to-all-start.2 = ((bf16[64,128,128]{2,1,0:T(8,128)(2,1)}), bf16[64,128,128]{2,1,0:T(8,128)(2,1)S(1)}, u32[]{:S(2)}, u32[]{:S(2)}) async-start(bf16[64,128,128]{2,1,0:T(8,128)(2,1)} %get-tuple-element.16), calls=%async_computation.2 | async-start | bytes 4194304 | tf_op jit(solution)/shard_map/all_to_all | solution.py:431
  176.3 20.9 %collective-permute-start.7 = (bf16[64,128,128]{2,1,0:T(8,128)(2,1)}, bf16[64,128,128]{2,1,0:T(8,128)(2,1)}, u32[]{:S(2)}, u32[]{:S(2)}) collective-permute-start(bf16[64,128,128]{2,1,0:T(8,128)(2,1)} %get-tuple-element.21), channel_id=1, source_target_pairs={{0,16},{16,0},{1,17},{17,1},{2,18},{18,2},{3,19},{19,3},{4,20},{20... | collective-permute-start | bytes 6291464 | tf_op jit(solution)/shard_map/ppermute | solution.py:434
  176.4 1.4 copy-start
  177.8 54.9 %all-to-all-start.4 = ((bf16[64,128,128]{2,1,0:T(8,128)(2,1)}), bf16[64,128,128]{2,1,0:T(8,128)(2,1)S(1)}, u32[]{:S(2)}, u32[]{:S(2)}) async-start(bf16[64,128,128]{2,1,0:T(8,128)(2,1)} %get-tuple-element.19), calls=%async_computation.4 | async-start | bytes 4194304 | tf_op jit(solution)/shard_map/all_to_all | solution.py:431
  203.1 2.5 %copy-start.1 = (bf16[64,128,128]{2,1,0:T(8,128)(2,1)S(1)}, bf16[64,128,128]{2,1,0:T(8,128)(2,1)}, u32[]{:S(2)}) copy-start(bf16[64,128,128]{2,1,0:T(8,128)(2,1)} %copy-done) | copy-start | bytes 6291460
  204.0 26.0 %collective-permute-start.13 = (bf16[8,128,128]{2,1,0:T(8,128)(2,1)S(1)}, bf16[8,128,128]{2,1,0:T(8,128)(2,1)S(1)}, u32[]{:S(2)}, u32[]{:S(2)}) collective-permute-start(bf16[8,128,128]{2,1,0:T(8,128)(2,1)S(1)} %get-tuple-element.26), channel_id=1, source_target_pairs={{12,0},{0,4},{4,8},{8,12},{13,1},{1,5},{5,9},{9,13},{14,2},{2,6},{... | collective-permute-start | bytes 786440 | tf_op jit(solution)/shard_map/ppermute | solution.py:437
  205.9 27.7 %collective-permute-start.12 = (bf16[8,128,128]{2,1,0:T(8,128)(2,1)}, bf16[8,128,128]{2,1,0:T(8,128)(2,1)S(1)}, u32[]{:S(2)}, u32[]{:S(2)}) collective-permute-start(bf16[8,128,128]{2,1,0:T(8,128)(2,1)} %get-tuple-element.27), channel_id=1, source_target_pairs={{4,0},{8,4},{12,8},{0,12},{5,1},{9,5},{13,9},{1,13},{6,2},{10,6},{... | collective-permute-start | bytes 786440 | tf_op jit(solution)/shard_map/ppermute | solution.py:437
  208.1 25.5 %collective-permute-start.11 = (bf16[8,128,128]{2,1,0:T(8,128)(2,1)}, bf16[8,128,128]{2,1,0:T(8,128)(2,1)}, u32[]{:S(2)}, u32[]{:S(2)}) collective-permute-start(bf16[8,128,128]{2,1,0:T(8,128)(2,1)} %get-tuple-element.28), channel_id=1, source_target_pairs={{96,0},{0,32},{32,64},{64,96},{97,1},{1,33},{33,65},{65,97},{98,2}... | collective-permute-start | bytes 786440 | tf_op jit(solution)/shard_map/ppermute | solution.py:437
  209.6 24.0 %collective-permute-start.10 = (bf16[8,128,128]{2,1,0:T(8,128)(2,1)S(1)}, bf16[8,128,128]{2,1,0:T(8,128)(2,1)}, u32[]{:S(2)}, u32[]{:S(2)}) collective-permute-start(bf16[8,128,128]{2,1,0:T(8,128)(2,1)S(1)} %get-tuple-element.29), channel_id=1, source_target_pairs={{32,0},{64,32},{96,64},{0,96},{33,1},{65,33},{97,65},{1,97},{34,2}... | collective-permute-start | bytes 786440 | tf_op jit(solution)/shard_map/ppermute | solution.py:437
  211.3 22.3 %collective-permute-start.9 = (bf16[8,128,128]{2,1,0:T(8,128)(2,1)S(1)}, bf16[8,128,128]{2,1,0:T(8,128)(2,1)}, u32[]{:S(2)}, u32[]{:S(2)}) collective-permute-start(bf16[8,128,128]{2,1,0:T(8,128)(2,1)S(1)} %get-tuple-element.30), channel_id=1, source_target_pairs={{3,0},{0,1},{1,2},{2,3},{7,4},{4,5},{5,6},{6,7},{11,8},{8,9},{9,10... | collective-permute-start | bytes 786440 | tf_op jit(solution)/shard_map/ppermute | solution.py:437
  230.0 8.6 %copy-start.5 = (bf16[8,128,128]{2,1,0:T(8,128)(2,1)}, bf16[8,128,128]{2,1,0:T(8,128)(2,1)S(1)}, u32[]{:S(2)}) copy-start(bf16[8,128,128]{2,1,0:T(8,128)(2,1)S(1)} %collective-permute-done.13.rest_5_) | copy-start | bytes 786436
  230.0 8.6 %collective-permute-start.8 = (bf16[8,128,128]{2,1,0:T(8,128)(2,1)S(1)}, bf16[8,128,128]{2,1,0:T(8,128)(2,1)}, u32[]{:S(2)}, u32[]{:S(2)}) collective-permute-start(bf16[8,128,128]{2,1,0:T(8,128)(2,1)S(1)} %get-tuple-element.31), channel_id=1, source_target_pairs={{1,0},{2,1},{3,2},{0,3},{5,4},{6,5},{7,6},{4,7},{9,8},{10,9},{11,1... | collective-permute-start | bytes 786440 | tf_op jit(solution)/shard_map/ppermute | solution.py:437
  233.6 4.9 %copy-start.6 = (bf16[8,128,128]{2,1,0:T(8,128)(2,1)}, bf16[8,128,128]{2,1,0:T(8,128)(2,1)S(1)}, u32[]{:S(2)}) copy-start(bf16[8,128,128]{2,1,0:T(8,128)(2,1)S(1)} %collective-permute-done.12.rest_4_) | copy-start | bytes 786436

commit v7 on v6

--- a/solution.py
+++ b/solution.py
@@ -275,23 +275,11 @@
         out[pl.ds(KEPT + SLAB * k, SLAB)] = part[...]
 
 
-def assemble_kernel(held, *rest):
-    *back, out, built, sems = rest
-    at = pl.ds(0, KEPT)
-    kept = pltpu.make_async_copy(held.at[at], built.at[at], sems.at[0])
-    kept.start()
-    stores = []
+def assemble_kernel(kept, *rest):
+    *back, out = rest
+    out[pl.ds(0, KEPT)] = kept[...]
     for k, part in enumerate(back):
-        at = pl.ds(KEPT + SLAB * k, SLAB)
-        built[at] = part[...].astype(jnp.float32)
-        stores.append(pltpu.make_async_copy(built.at[at], out.at[at], sems.at[1 + k]))
-        stores[-1].start()
-    kept.wait()
-    at = pl.ds(0, KEPT)
-    stores.append(pltpu.make_async_copy(built.at[at], out.at[at], sems.at[1 + len(back)]))
-    stores[-1].start()
-    for store in stores:
-        store.wait()
+        out[pl.ds(KEPT + SLAB * k, SLAB)] = part[...].astype(jnp.float32)
 
 
 def shard_work(
@@ -440,17 +428,13 @@
     assemble = pl.pallas_call(
         assemble_kernel,
         out_shape=own_shape,
-        in_specs=[hbm] + [vmem] * len(back),
-        out_specs=hbm,
-        scratch_shapes=[
-            pltpu.VMEM(own_shape.shape, jnp.float32),
-            pltpu.SemaphoreType.DMA((2 + len(back),)),
-        ],
+        in_specs=[vmem] * (1 + len(back)),
+        out_specs=vmem,
         compiler_params=limit,
         cost_estimate=pl.CostEstimate(flops=10**6, bytes_accessed=2**23, transcendentals=0),
         name="assemble",
     )
-    index_grad = assemble(held_grad, *back)
+    index_grad = assemble(held_grad[:KEPT], *back)
     return (query_grad, index_grad.reshape(blocks_here * BLOCK, feat_width))
 
 

time: 245 us -> 245 us (level)
  transfers between devices with their start and end apart: 19 -> 19, of which waited for: 6 -> 6; matrix products, arithmetic and copies ran while one was open for 7% -> 8% of each run, Pallas kernels for 28% -> 28%
where the time goes in v7:
time: 245 us; the launch traced here: 243 us
  starting transfers between devices  88.6 us (36%)
  Pallas kernels  77.6 us (32%)
  waiting for transfers between devices  47.5 us (19%)
  other arithmetic  14.7 us (6%)
  local copies, waits for them, and re-layouts  13.9 us (6%)
    all_to_all x2, starting transfers between devices, shard_work(): came = lax.all_to_all(part, SAME_CORE, 0, 0, tiled=True)  42.1 us
    pallas_call x1, Pallas kernels, shard_work(): chunk_1(counts, base, hits, items[1], rows, halves[1], held, mate_held, acc)  29 us
    pallas_call x1, Pallas kernels, shard_work(): chunk_0(counts, base, hits, items[0], rows, halves[0], held, mate_held)  26.7 us
    ppermute x6, waiting for transfers between devices, shard_work(): lax.ppermute(stored[at], axis, way)  22.2 us
    ppermute x6, waiting for transfers between devices, shard_work(): lax.ppermute(held_grad[at].astype(jnp.bfloat16), axis, [(j, i) for i, j i...  19.9 us
    all_to_all x2, starting transfers between devices, shard_work(): halves.append(lax.all_to_all(spread, SAME_CORE, 0, 0, tiled=True))  13.1 us
    ppermute x6, starting transfers between devices, shard_work(): lax.ppermute(held_grad[at].astype(jnp.bfloat16), axis, [(j, i) for i, j i...  11.7 us
    all_to_all x1, starting transfers between devices, shard_work(): rows = lax.all_to_all(packed, SAME_CORE, 0, 0, tiled=True)  11.5 us
  transfers between devices with their start and end apart: 19, of which 6 were waited for; matrix products, arithmetic and copies ran while one was open for 8% of the time, Pallas kernels for 28%

profile of v7, /device:TPU:0, one launch (start us, length us, event | category | flops | bytes accessed | tf_op | source)
XLA Modules:
  0.0 243.2 jit_solution(11420890031641461717)
XLA Ops:
  0.6 0.7 add_select_fusion
  1.4 0.8 convert_bitcast_fusion
  2.1 1.5 compare_reduce_fusion
  3.7 0.7 compare_reduce_fusion.1
  4.4 0.7 pad_add_fusion.where
  5.0 0.6 shift-left_reduce_fusion
  5.7 4.8 %ask.1 = s32[64,256]{1,0:T(8,128)} custom-call(s32[2]{0:T(128)} %pad_add_fusion.where, s32[64]{0:T(128)} %bitcast.46, s32[64]{0:T(128)} %local.1, s32[64]{0:T(128)} %get-tuple-element.23.hits, s32[64]{0:T(128)} %get-tuple-element.22.lives), custom_call_target="tpu_custom_call" | custom-call | flops 1000000 | bytes 65536 | tf_op jit(solution)/shard_map/ask/pallas_call | solution.py:331
  10.4 0.8 convert_element_type.33
  11.3 0.8 subtract_bitcast_fusion
  12.2 0.8 pad_maximum_fusion
  12.9 11.5 %all-to-all-start = ((f32[64,8,128]{2,1,0:T(8,128)}), f32[64,8,128]{2,1,0:T(8,128)S(1)}, u32[]{:S(2)}, u32[]{:S(2)}) async-start(f32[64,8,128]{2,1,0:T(8,128)} %pad_maximum_fusion), calls=%async_computation | async-start | bytes 524288 | tf_op jit(solution)/shard_map/all_to_all | solution.py:342
  24.5 2.3 fusion.5
  26.7 3.0 %collective-permute-start.3 = (bf16[8,128,128]{2,1,0:T(8,128)(2,1)}, bf16[8,128,128]{2,1,0:T(8,128)(2,1)S(1)}, u32[]{:S(2)}, u32[]{:S(2)}) collective-permute-start(bf16[8,128,128]{2,1,0:T(8,128)(2,1)} %bitcast.11), channel_id=1, source_target_pairs={{0,96},{32,0},{64,32},{96,64},{1,97},{33,1},{65,33},{97,65},{2,98}... | collective-permute-start | bytes 786440 | tf_op jit(solution)/shard_map/ppermute | solution.py:307
  29.7 5.3 %all-to-all-done.rows_in = f32[64,8,128]{2,1,0:T(8,128)S(1)} async-done(((f32[64,8,128]{2,1,0:T(8,128)}), f32[64,8,128]{2,1,0:T(8,128)S(1)}, u32[]{:S(2)}, u32[]{:S(2)}) %all-to-all-start) | async-done | bytes 262176 | tf_op jit(solution)/shard_map/all_to_all | solution.py:342
  35.1 1.8 broadcast_in_dim.7
  36.9 4.9 %all-to-all-start.1 = ((bf16[64,128,128]{2,1,0:T(8,128)(2,1)}), bf16[64,128,128]{2,1,0:T(8,128)(2,1)S(1)}, u32[]{:S(2)}, u32[]{:S(2)}) async-start(bf16[64,128,128]{2,1,0:T(8,128)(2,1)} %broadcast_in_dim.7), calls=%async_computation.1 | async-start | bytes 4194304 | tf_op jit(solution)/shard_map/all_to_all | solution.py:300
  41.8 2.9 %collective-permute-start.5 = (bf16[8,128,128]{2,1,0:T(8,128)(2,1)}, bf16[8,128,128]{2,1,0:T(8,128)(2,1)S(1)}, u32[]{:S(2)}, u32[]{:S(2)}) collective-permute-start(bf16[8,128,128]{2,1,0:T(8,128)(2,1)} %bitcast.43), channel_id=1, source_target_pairs={{0,12},{4,0},{8,4},{12,8},{1,13},{5,1},{9,5},{13,9},{2,14},{6,2},{... | collective-permute-start | bytes 786440 | tf_op jit(solution)/shard_map/ppermute | solution.py:307
  44.6 1.5 collective-permute-start.2
  46.2 2.7 %collective-permute-start.1 = (bf16[8,128,128]{2,1,0:T(8,128)(2,1)S(1)}, bf16[8,128,128]{2,1,0:T(8,128)(2,1)S(1)}, u32[]{:S(2)}, u32[]{:S(2)}) collective-permute-start(bf16[8,128,128]{2,1,0:T(8,128)(2,1)S(1)} %bitcast.41), channel_id=1, source_target_pairs={{0,3},{1,0},{2,1},{3,2},{4,7},{5,4},{6,5},{7,6},{8,11},{9,8},{10,9... | collective-permute-start | bytes 786440 | tf_op jit(solution)/shard_map/ppermute | solution.py:307
  49.0 1.9 slice.80
  50.9 19.6 %collective-permute-done.5.rest_5_ = bf16[8,128,128]{2,1,0:T(8,128)(2,1)S(1)} collective-permute-done((bf16[8,128,128]{2,1,0:T(8,128)(2,1)}, bf16[8,128,128]{2,1,0:T(8,128)(2,1)S(1)}, u32[]{:S(2)}, u32[]{:S(2)}) %collective-permute-start.5) | collective-permute-done | bytes 262176 | tf_op jit(solution)/shard_map/ppermute | solution.py:307
  70.5 1.4 collective-permute-done.2.rest_2_
  71.9 1.2 collective-permute-done.4.rest_4_
  73.1 0.7 copy-done.9
  73.8 3.0 %hold.1.own_in = bf16[64,128,128]{2,1,0:T(8,128)(2,1)} custom-call(bf16[16,128,128]{2,1,0:T(8,128)(2,1)} %bitcast.38, bf16[8,128,128]{2,1,0:T(8,128)(2,1)} %copy-done.8, bf16[8,128,128]{2,1,0:T(8,128)(2,1)} %copy-done.7, bf16[8,128,128]{2,1,0:T(8,128)(2,1)} %copy-done.6, bf16[8,128,128]{2,1,0:T(8,128)(2,1)} %copy-done.4, bf16[8,128,128]{2,1,0:T(8,128)(2,1)} %copy-done.9, ...), custom_call_target="tpu_custom_call" | custom-call | flops 1000000 | bytes 4194304 | tf_op jit(solution)/shard_map/hold/pallas_call | solution.py:371
  76.8 2.0 broadcast_in_dim.8
  78.8 8.3 %all-to-all-start.3 = ((bf16[64,128,128]{2,1,0:T(8,128)(2,1)}), bf16[64,128,128]{2,1,0:T(8,128)(2,1)}, u32[]{:S(2)}, u32[]{:S(2)}) async-start(bf16[64,128,128]{2,1,0:T(8,128)(2,1)} %broadcast_in_dim.8), calls=%async_computation.3 | async-start | bytes 4194304 | tf_op jit(solution)/shard_map/all_to_all | solution.py:300
  87.2 0.6 copy.12
  87.8 10.2 %listing.1 = (s32[30720]{0:T(1024)}, s32[30720]{0:T(1024)}, s32[2]{0:T(128)}, s32[1792]{0:T(1024)}, s32[1792]{0:T(1024)}) custom-call(s32[64,256]{1,0:T(8,128)} %bitcast.45), custom_call_target="tpu_custom_call" | custom-call | flops 1000000000 | bytes 1048576 | tf_op jit(solution)/shard_map/listing/pallas_call | solution.py:361
  98.0 26.7 %chunk_0.1 = (bf16[64,128,128]{2,1,0:T(8,128)(2,1)}, f32[128,128,128]{2,1,0:T(8,128)}) custom-call(s32[2]{0:T(128)} %get-tuple-element.12.counts, s32[1792]{0:T(1024)} %get-tuple-element.13.base, s32[1792]{0:T(1024)} %get-tuple-element.14.hits, s32[30720]{0:T(1024)} %get-tuple-element.15.items_in, f32[64,8,128]{2,1,0:T(8,128)} %copy-done.3, ...), custom_call_target="tpu_custom_call" | custom-call | flops 20000000000 | bytes 33554432 | tf_op jit(solution)/shard_map/chunk_0/pallas_call | solution.py:403
  124.7 22.6 %all-to-all-start.2 = ((bf16[64,128,128]{2,1,0:T(8,128)(2,1)}), bf16[64,128,128]{2,1,0:T(8,128)(2,1)S(1)}, u32[]{:S(2)}, u32[]{:S(2)}) async-start(bf16[64,128,128]{2,1,0:T(8,128)(2,1)} %get-tuple-element.16), calls=%async_computation.2 | async-start | bytes 4194304 | tf_op jit(solution)/shard_map/all_to_all | solution.py:419
  147.3 29.0 %chunk_1.1 = (bf16[64,128,128]{2,1,0:T(8,128)(2,1)}, f32[64,128,128]{2,1,0:T(8,128)}, bf16[64,128,128]{2,1,0:T(8,128)(2,1)}) custom-call(s32[2]{0:T(128)} %get-tuple-element.12.counts, s32[1792]{0:T(1024)} %get-tuple-element.13.base, s32[1792]{0:T(1024)} %get-tuple-element.14.hits, s32[30720]{0:T(1024)} %get-tuple-element.17.items_in, ...), custom_call_target="tpu_custom_call" | custom-call | flops 20000000000 | bytes 33554432 | tf_op jit(solution)/shard_map/chunk_1/pallas_call | solution.py:416
  176.5 1.3 copy-done
  177.8 19.5 %all-to-all-start.4 = ((bf16[64,128,128]{2,1,0:T(8,128)(2,1)}), bf16[64,128,128]{2,1,0:T(8,128)(2,1)S(1)}, u32[]{:S(2)}, u32[]{:S(2)}) async-start(bf16[64,128,128]{2,1,0:T(8,128)(2,1)} %get-tuple-element.19), calls=%async_computation.4 | async-start | bytes 4194304 | tf_op jit(solution)/shard_map/all_to_all | solution.py:419
  197.3 6.0 %fusion.3 = (bf16[64,128,128]{2,1,0:T(8,128)(2,1)S(1)}, f32[64,128,128]{2,1,0:T(8,128)}) fusion(f32[64,128,128]{2,1,0:T(8,128)} %get-tuple-element.20, bf16[64,128,128]{2,1,0:T(8,128)(2,1)} %collective-permute-done.7), kind=kLoop, calls=%fused_computation.26 | loop fusion | flops 3145728 | bytes 12582912 | tf_op jit(solution)/shard_map/convert.5
  203.3 1.6 collective-permute-start.13
  205.0 0.3 convert_reduce_fusion.1
  205.3 2.7 %collective-permute-start.12 = (bf16[8,128,128]{2,1,0:T(8,128)(2,1)S(1)}, bf16[8,128,128]{2,1,0:T(8,128)(2,1)}, u32[]{:S(2)}, u32[]{:S(2)}) collective-permute-start(bf16[8,128,128]{2,1,0:T(8,128)(2,1)S(1)} %get-tuple-element.27), channel_id=1, source_target_pairs={{4,0},{8,4},{12,8},{0,12},{5,1},{9,5},{13,9},{1,13},{6,2},{10,6},{... | collective-permute-start | bytes 786440 | tf_op jit(solution)/shard_map/ppermute | solution.py:425
  208.0 1.5 collective-permute-start.11
  209.5 1.7 collective-permute-start.10
  211.2 1.5 collective-permute-start.9
  212.7 17.3 %collective-permute-done.13.rest_5_ = bf16[8,128,128]{2,1,0:T(8,128)(2,1)S(1)} collective-permute-done((bf16[8,128,128]{2,1,0:T(8,128)(2,1)S(1)}, bf16[8,128,128]{2,1,0:T(8,128)(2,1)S(1)}, u32[]{:S(2)}, u32[]{:S(2)}) %collective-permute-start.13) | collective-permute-done | bytes 262176 | tf_op jit(solution)/shard_map/ppermute | solution.py:425
  230.0 0.7 copy-done.10
  230.7 2.6 %collective-permute-start.8 = (bf16[8,128,128]{2,1,0:T(8,128)(2,1)S(1)}, bf16[8,128,128]{2,1,0:T(8,128)(2,1)}, u32[]{:S(2)}, u32[]{:S(2)}) collective-permute-start(bf16[8,128,128]{2,1,0:T(8,128)(2,1)S(1)} %get-tuple-element.31), channel_id=1, source_target_pairs={{1,0},{2,1},{3,2},{0,3},{5,4},{6,5},{7,6},{4,7},{9,8},{10,9},{11,1... | collective-permute-start | bytes 786440 | tf_op jit(solution)/shard_map/ppermute | solution.py:425
  233.7 0.7 pad_maximum_fusion.1
  234.3 2.3 slice.103.kept
  236.7 2.6 %collective-permute-done.8.rest_0_ = bf16[8,128,128]{2,1,0:T(8,128)(2,1)} collective-permute-done((bf16[8,128,128]{2,1,0:T(8,128)(2,1)S(1)}, bf16[8,128,128]{2,1,0:T(8,128)(2,1)}, u32[]{:S(2)}, u32[]{:S(2)}) %collective-permute-start.8) | collective-permute-done | bytes 262176 | tf_op jit(solution)/shard_map/ppermute | solution.py:425
  239.3 3.9 %assemble.1 = f32[64,128,128]{2,1,0:T(8,128)} custom-call(f32[16,128,128]{2,1,0:T(8,128)} %slice.103.kept, bf16[8,128,128]{2,1,0:T(8,128)(2,1)} %collective-permute-done.8.rest_0_, bf16[8,128,128]{2,1,0:T(8,128)(2,1)} %collective-permute-done.9.rest_1_, bf16[8,128,128]{2,1,0:T(8,128)(2,1)} %collective-permute-done.10.rest_2_, ...), custom_call_target="tpu_custom_call" | custom-call | flops 1000000 | bytes 8388608 | tf_op jit(solution)/shard_map/assemble/pallas_call | solution.py:437
  (46 shorter events, 0.8 us)
Async XLA Ops:
  12.2 17.6 %copy-start.11 = (bf16[256,128]{1,0:T(8,128)(2,1)S(1)}, bf16[256,128]{1,0:T(8,128)(2,1)}, u32[]{:S(2)}) copy-start(bf16[256,128]{1,0:T(8,128)(2,1)} %param.8) | copy-start | bytes 196612
  12.9 22.1 %all-to-all-start = ((f32[64,8,128]{2,1,0:T(8,128)}), f32[64,8,128]{2,1,0:T(8,128)S(1)}, u32[]{:S(2)}, u32[]{:S(2)}) async-start(f32[64,8,128]{2,1,0:T(8,128)} %pad_maximum_fusion), calls=%async_computation | async-start | bytes 524288 | tf_op jit(solution)/shard_map/all_to_all | solution.py:342
  26.7 22.1 %collective-permute-start.3 = (bf16[8,128,128]{2,1,0:T(8,128)(2,1)}, bf16[8,128,128]{2,1,0:T(8,128)(2,1)S(1)}, u32[]{:S(2)}, u32[]{:S(2)}) collective-permute-start(bf16[8,128,128]{2,1,0:T(8,128)(2,1)} %bitcast.11), channel_id=1, source_target_pairs={{0,96},{32,0},{64,32},{96,64},{1,97},{33,1},{65,33},{97,65},{2,98}... | collective-permute-start | bytes 786440 | tf_op jit(solution)/shard_map/ppermute | solution.py:307
  35.1 52.0 %copy-start.3 = (f32[64,8,128]{2,1,0:T(8,128)}, f32[64,8,128]{2,1,0:T(8,128)S(1)}, u32[]{:S(2)}) copy-start(f32[64,8,128]{2,1,0:T(8,128)S(1)} %all-to-all-done.rows_in) | copy-start | bytes 786436
  36.9 39.9 %all-to-all-start.1 = ((bf16[64,128,128]{2,1,0:T(8,128)(2,1)}), bf16[64,128,128]{2,1,0:T(8,128)(2,1)S(1)}, u32[]{:S(2)}, u32[]{:S(2)}) async-start(bf16[64,128,128]{2,1,0:T(8,128)(2,1)} %broadcast_in_dim.7), calls=%async_computation.1 | async-start | bytes 4194304 | tf_op jit(solution)/shard_map/all_to_all | solution.py:300
  41.8 28.7 %collective-permute-start.5 = (bf16[8,128,128]{2,1,0:T(8,128)(2,1)}, bf16[8,128,128]{2,1,0:T(8,128)(2,1)S(1)}, u32[]{:S(2)}, u32[]{:S(2)}) collective-permute-start(bf16[8,128,128]{2,1,0:T(8,128)(2,1)} %bitcast.43), channel_id=1, source_target_pairs={{0,12},{4,0},{8,4},{12,8},{1,13},{5,1},{9,5},{13,9},{2,14},{6,2},{... | collective-permute-start | bytes 786440 | tf_op jit(solution)/shard_map/ppermute | solution.py:307
  44.6 27.2 %collective-permute-start.2 = (bf16[8,128,128]{2,1,0:T(8,128)(2,1)}, bf16[8,128,128]{2,1,0:T(8,128)(2,1)S(1)}, u32[]{:S(2)}, u32[]{:S(2)}) collective-permute-start(bf16[8,128,128]{2,1,0:T(8,128)(2,1)} %bitcast.42), channel_id=1, source_target_pairs={{0,32},{32,64},{64,96},{96,0},{1,33},{33,65},{65,97},{97,1},{2,34}... | collective-permute-start | bytes 786440 | tf_op jit(solution)/shard_map/ppermute | solution.py:307
  46.2 25.7 %collective-permute-start.1 = (bf16[8,128,128]{2,1,0:T(8,128)(2,1)S(1)}, bf16[8,128,128]{2,1,0:T(8,128)(2,1)S(1)}, u32[]{:S(2)}, u32[]{:S(2)}) collective-permute-start(bf16[8,128,128]{2,1,0:T(8,128)(2,1)S(1)} %bitcast.41), channel_id=1, source_target_pairs={{0,3},{1,0},{2,1},{3,2},{4,7},{5,4},{6,5},{7,6},{8,11},{9,8},{10,9... | collective-permute-start | bytes 786440 | tf_op jit(solution)/shard_map/ppermute | solution.py:307
  48.9 23.0 %collective-permute-start = (bf16[8,128,128]{2,1,0:T(8,128)(2,1)S(1)}, bf16[8,128,128]{2,1,0:T(8,128)(2,1)S(1)}, u32[]{:S(2)}, u32[]{:S(2)}) collective-permute-start(bf16[8,128,128]{2,1,0:T(8,128)(2,1)S(1)} %bitcast.40), channel_id=1, source_target_pairs={{0,1},{1,2},{2,3},{3,0},{4,5},{5,6},{6,7},{7,4},{8,9},{9,10},{10,1... | collective-permute-start | bytes 786440 | tf_op jit(solution)/shard_map/ppermute | solution.py:307
  48.9 24.9 %copy-start.4 = (bf16[8,128,128]{2,1,0:T(8,128)(2,1)}, bf16[8,128,128]{2,1,0:T(8,128)(2,1)S(1)}, u32[]{:S(2)}) copy-start(bf16[8,128,128]{2,1,0:T(8,128)(2,1)S(1)} %collective-permute-done.3.rest_3_) | copy-start | bytes 786436
  48.9 24.2 %collective-permute-start.4 = (bf16[8,128,128]{2,1,0:T(8,128)(2,1)S(1)}, bf16[8,128,128]{2,1,0:T(8,128)(2,1)S(1)}, u32[]{:S(2)}, u32[]{:S(2)}) collective-permute-start(bf16[8,128,128]{2,1,0:T(8,128)(2,1)S(1)} %bitcast.39), channel_id=1, source_target_pairs={{0,4},{4,8},{8,12},{12,0},{1,5},{5,9},{9,13},{13,1},{2,6},{6,10},{... | collective-permute-start | bytes 786440 | tf_op jit(solution)/shard_map/ppermute | solution.py:307
  70.5 3.3 %copy-start.5 = (bf16[8,128,128]{2,1,0:T(8,128)(2,1)}, bf16[8,128,128]{2,1,0:T(8,128)(2,1)S(1)}, u32[]{:S(2)}) copy-start(bf16[8,128,128]{2,1,0:T(8,128)(2,1)S(1)} %collective-permute-done.5.rest_5_) | copy-start | bytes 786436
  71.9 1.9 copy-start.6
  71.9 1.2 copy-start.7
  71.9 1.2 copy-start.8
  73.1 0.7 copy-start.9
  76.8 21.2 %collective-permute-start.6 = (bf16[64,128,128]{2,1,0:T(8,128)(2,1)}, bf16[64,128,128]{2,1,0:T(8,128)(2,1)}, u32[]{:S(2)}, u32[]{:S(2)}) collective-permute-start(bf16[64,128,128]{2,1,0:T(8,128)(2,1)} %hold.1.own_in), channel_id=1, source_target_pairs={{0,16},{16,0},{1,17},{17,1},{2,18},{18,2},{3,19},{19,3},{4,20},{20... | collective-permute-start | bytes 6291464 | tf_op jit(solution)/shard_map/ppermute | solution.py:372
  76.8 2.0 copy-start.2
  78.8 45.8 %all-to-all-start.3 = ((bf16[64,128,128]{2,1,0:T(8,128)(2,1)}), bf16[64,128,128]{2,1,0:T(8,128)(2,1)}, u32[]{:S(2)}, u32[]{:S(2)}) async-start(bf16[64,128,128]{2,1,0:T(8,128)(2,1)} %broadcast_in_dim.8), calls=%async_computation.3 | async-start | bytes 4194304 | tf_op jit(solution)/shard_map/all_to_all | solution.py:300
  124.7 51.8 %all-to-all-start.2 = ((bf16[64,128,128]{2,1,0:T(8,128)(2,1)}), bf16[64,128,128]{2,1,0:T(8,128)(2,1)S(1)}, u32[]{:S(2)}, u32[]{:S(2)}) async-start(bf16[64,128,128]{2,1,0:T(8,128)(2,1)} %get-tuple-element.16), calls=%async_computation.2 | async-start | bytes 4194304 | tf_op jit(solution)/shard_map/all_to_all | solution.py:419
  176.3 20.9 %collective-permute-start.7 = (bf16[64,128,128]{2,1,0:T(8,128)(2,1)}, bf16[64,128,128]{2,1,0:T(8,128)(2,1)}, u32[]{:S(2)}, u32[]{:S(2)}) collective-permute-start(bf16[64,128,128]{2,1,0:T(8,128)(2,1)} %get-tuple-element.21), channel_id=1, source_target_pairs={{0,16},{16,0},{1,17},{17,1},{2,18},{18,2},{3,19},{19,3},{4,20},{20... | collective-permute-start | bytes 6291464 | tf_op jit(solution)/shard_map/ppermute | solution.py:422
  176.4 1.3 copy-start
  177.8 55.6 %all-to-all-start.4 = ((bf16[64,128,128]{2,1,0:T(8,128)(2,1)}), bf16[64,128,128]{2,1,0:T(8,128)(2,1)S(1)}, u32[]{:S(2)}, u32[]{:S(2)}) async-start(bf16[64,128,128]{2,1,0:T(8,128)(2,1)} %get-tuple-element.19), calls=%async_computation.4 | async-start | bytes 4194304 | tf_op jit(solution)/shard_map/all_to_all | solution.py:419
  203.2 1.8 copy-start.1
  203.3 26.7 %collective-permute-start.13 = (bf16[8,128,128]{2,1,0:T(8,128)(2,1)S(1)}, bf16[8,128,128]{2,1,0:T(8,128)(2,1)S(1)}, u32[]{:S(2)}, u32[]{:S(2)}) collective-permute-start(bf16[8,128,128]{2,1,0:T(8,128)(2,1)S(1)} %get-tuple-element.26), channel_id=1, source_target_pairs={{12,0},{0,4},{4,8},{8,12},{13,1},{1,5},{5,9},{9,13},{14,2},{2,6},{... | collective-permute-start | bytes 786440 | tf_op jit(solution)/shard_map/ppermute | solution.py:425
  205.3 31.4 %collective-permute-start.12 = (bf16[8,128,128]{2,1,0:T(8,128)(2,1)S(1)}, bf16[8,128,128]{2,1,0:T(8,128)(2,1)}, u32[]{:S(2)}, u32[]{:S(2)}) collective-permute-start(bf16[8,128,128]{2,1,0:T(8,128)(2,1)S(1)} %get-tuple-element.27), channel_id=1, source_target_pairs={{4,0},{8,4},{12,8},{0,12},{5,1},{9,5},{13,9},{1,13},{6,2},{10,6},{... | collective-permute-start | bytes 786440 | tf_op jit(solution)/shard_map/ppermute | solution.py:425
  208.0 28.7 %collective-permute-start.11 = (bf16[8,128,128]{2,1,0:T(8,128)(2,1)S(1)}, bf16[8,128,128]{2,1,0:T(8,128)(2,1)}, u32[]{:S(2)}, u32[]{:S(2)}) collective-permute-start(bf16[8,128,128]{2,1,0:T(8,128)(2,1)S(1)} %get-tuple-element.28), channel_id=1, source_target_pairs={{96,0},{0,32},{32,64},{64,96},{97,1},{1,33},{33,65},{65,97},{98,2}... | collective-permute-start | bytes 786440 | tf_op jit(solution)/shard_map/ppermute | solution.py:425
  209.5 27.2 %collective-permute-start.10 = (bf16[8,128,128]{2,1,0:T(8,128)(2,1)S(1)}, bf16[8,128,128]{2,1,0:T(8,128)(2,1)}, u32[]{:S(2)}, u32[]{:S(2)}) collective-permute-start(bf16[8,128,128]{2,1,0:T(8,128)(2,1)S(1)} %get-tuple-element.29), channel_id=1, source_target_pairs={{32,0},{64,32},{96,64},{0,96},{33,1},{65,33},{97,65},{1,97},{34,2}... | collective-permute-start | bytes 786440 | tf_op jit(solution)/shard_map/ppermute | solution.py:425
  211.2 25.5 %collective-permute-start.9 = (bf16[8,128,128]{2,1,0:T(8,128)(2,1)S(1)}, bf16[8,128,128]{2,1,0:T(8,128)(2,1)}, u32[]{:S(2)}, u32[]{:S(2)}) collective-permute-start(bf16[8,128,128]{2,1,0:T(8,128)(2,1)S(1)} %get-tuple-element.30), channel_id=1, source_target_pairs={{3,0},{0,1},{1,2},{2,3},{7,4},{4,5},{5,6},{6,7},{11,8},{8,9},{9,10... | collective-permute-start | bytes 786440 | tf_op jit(solution)/shard_map/ppermute | solution.py:425
  230.0 0.7 copy-start.10
  230.7 8.6 %collective-permute-start.8 = (bf16[8,128,128]{2,1,0:T(8,128)(2,1)S(1)}, bf16[8,128,128]{2,1,0:T(8,128)(2,1)}, u32[]{:S(2)}, u32[]{:S(2)}) collective-permute-start(bf16[8,128,128]{2,1,0:T(8,128)(2,1)S(1)} %get-tuple-element.31), channel_id=1, source_target_pairs={{1,0},{2,1},{3,2},{0,3},{5,4},{6,5},{7,6},{4,7},{9,8},{10,9},{11,1... | collective-permute-start | bytes 786440 | tf_op jit(solution)/shard_map/ppermute | solution.py:425
